TPU v7x, 512 devices: a whole 4x8x8 slice. The times are simulated.
512 devices in a mesh: tm: 16 (over z, core), lat: 32 (over x, y).
Axes of the slice: x: 4, y: 8, z: 8, core: 2. Of those that a mesh axis runs over, the one named last changes fastest.
Arguments:
- trajectory: float32 [16, 84, 128, 128], P('tm', None, 'lat'), may hold values from -6 to 6
- step_levels: int32 [17], replicated, may hold values from 0 to 63, as said below
- in_weight: bfloat16 [256, 84], replicated, may hold values from -0.625 to 0.625
- in_bias: float32 [256], replicated, may hold values from -4 to 4
- conv_weight: bfloat16 [2, 256, 2304], replicated, may hold values from -0.125 to 0.125
- cond_weight: bfloat16 [256, 1024], replicated, may hold values from -0.375 to 0.375
- out_weight: bfloat16 [84, 256], replicated, may hold values from -0.375 to 0.375
Outputs:
- advanced: float32 [16, 84, 128, 128], P('tm', None, 'lat')
Inputs may be any that keep to these rules, and one draw needn't show every extreme that they name: `step_levels`: strictly increasing; the first entry is 0 and the last is 63.
All inputs are finite; a program needn't handle non-finite values.
Results may differ from a plain program's by a relative error of at most 0.0055.
Values may be sent and summed in bfloat16 or wider, within the bound.
No kernel may reach another device: no remote copies, remote signals or barrier semaphores. Data moves between devices by JAX's collectives and lax.ppermute only.
A program may use at most 64 MiB of HBM per device.

v0:
```python
import jax
import jax.numpy as jnp
from jax import lax
from jax.sharding import PartitionSpec as P

LEVELS = 64
ITERS = 2


sigma_top = 1.0
sigma_low = 0.02
rho_power = 7.0


def extended(block, sides, width):
    for axis, dim in sides:
        count = lax.axis_size(axis)
        forward = [(i, i + 1) for i in range(count - 1)]
        backward = [(target, source) for source, target in forward]
        low = lax.ppermute(
            lax.slice_in_dim(block, block.shape[dim] - width, None, axis=dim), axis, forward
        )
        high = lax.ppermute(lax.slice_in_dim(block, 0, width, axis=dim), axis, backward)
        block = jnp.concatenate([low, block, high], axis=dim)
    return block


def carried_in(value, axis, join, neutral):
    count, mine = (lax.axis_size(axis), lax.axis_index(axis))
    pieces = lax.all_gather(value, axis)
    subtotal = jnp.full_like(value, 0) + jnp.asarray(neutral, value.dtype)

    def hop(position, subtotal):
        longer = join(subtotal, pieces[position])
        return jnp.where(position < mine, longer, subtotal)

    return lax.fori_loop(0, count - 1, hop, subtotal)


def from_root(array, axis, root):
    mine = lax.axis_index(axis) == root
    return lax.psum(jnp.where(mine, array, jnp.zeros_like(array)), axis)


def level_sigma(levels):
    fraction = levels.astype(jnp.float32) / (LEVELS - 1)
    root_value = sigma_top ** (1.0 / rho_power) + fraction * (
        sigma_low ** (1.0 / rho_power) - sigma_top ** (1.0 / rho_power)
    )
    return root_value**rho_power


def conditions_of(sigma_now, cond_weight):
    freq_count = cond_weight.shape[0] // 2
    frequency = 100.0 ** (jnp.arange(freq_count).astype(jnp.float32) / freq_count)
    phases = jnp.log(sigma_now) / 4.0 * frequency
    embedding = jnp.concatenate([jnp.cos(phases), jnp.sin(phases)]).astype(jnp.bfloat16)[None, :]
    conditions = jnp.dot(embedding, cond_weight, preferred_element_type=jnp.float32)[0]
    return jnp.split(conditions, 4)


def convolve(padded, weight):
    row_count = padded.shape[1] - 2
    shifted = []
    for offset_row in range(3):
        for offset_col in (-1, 0, 1):
            shifted.append(
                jnp.roll(padded[:, offset_row : offset_row + row_count, :], -offset_col, axis=2)
            )
    columns_all = jnp.concatenate(shifted, axis=0)
    flattened = columns_all.reshape(columns_all.shape[0], -1)
    response = jnp.dot(weight, flattened, preferred_element_type=jnp.float32)
    return response.reshape(weight.shape[0], row_count, padded.shape[2])


def project(scaled, in_weight, in_bias):
    channels, row_count, columns = scaled.shape
    hidden = (
        jnp.dot(in_weight, scaled.reshape(channels, -1), preferred_element_type=jnp.float32)
        + in_bias[:, None]
    )
    return hidden.reshape(-1, row_count, columns)


def field_drift(
    current, sigma_now, sigma_next, in_weight, in_bias, conv_weight, cond_weight, out_weight
):
    scale_one, shift_one, scale_two, shift_two = conditions_of(sigma_now, cond_weight)
    variance = sigma_now * sigma_now + 0.25
    scaled = (current / jnp.sqrt(variance)).astype(jnp.bfloat16)
    channels, row_count, columns = current.shape
    hidden_zero = project(scaled, in_weight, in_bias).astype(jnp.bfloat16)
    padded = extended(hidden_zero, (("lat", 1),), 1)
    response = convolve(padded, conv_weight[0])
    hidden_one = jax.nn.silu(
        response * (1.0 + scale_one[:, None, None]) + shift_one[:, None, None]
    ).astype(jnp.bfloat16)
    padded_one = extended(hidden_one, (("lat", 1),), 1)
    response = convolve(padded_one, conv_weight[1])
    hidden_two = hidden_one.astype(jnp.float32) + jax.nn.silu(
        response * (1.0 + scale_two[:, None, None]) + shift_two[:, None, None]
    )
    hidden_two = hidden_two.astype(jnp.bfloat16)
    network = jnp.dot(
        out_weight, hidden_two.reshape(hidden_two.shape[0], -1), preferred_element_type=jnp.float32
    )
    network = network.reshape(channels, row_count, columns)
    denoised = 0.25 / variance * current + 0.5 * sigma_now / jnp.sqrt(variance) * network
    return (current - denoised) * ((sigma_next - sigma_now) / sigma_now)


def add_pair(earlier_sum, later_sum):
    return earlier_sum + later_sum


def earlier_drifts(carried):
    return carried_in(carried, "tm", add_pair, jnp.zeros_like(carried))


def on_device(trajectory, step_levels, in_weight, in_bias, conv_weight, cond_weight, out_weight):
    time_slot = lax.axis_index("tm")
    current = trajectory[0]
    bounds = lax.dynamic_slice_in_dim(step_levels, time_slot, 2)
    sigmas = level_sigma(bounds)
    sigma_now = sigmas[0]
    sigma_next = sigmas[1]
    anchor = from_root(current, "tm", 0)
    result = current
    for sweep in range(ITERS):
        drift_term = field_drift(
            current, sigma_now, sigma_next, in_weight, in_bias, conv_weight, cond_weight, out_weight
        )
        earlier = earlier_drifts(drift_term)
        if sweep + 1 < ITERS:
            current = earlier + anchor
        else:
            result = earlier + anchor + drift_term
    return result[None]


def solution(mesh):
    in_specs = (P("tm", None, "lat", None), P(), P(), P(), P(), P(), P())
    out_specs = P("tm", None, "lat", None)
    return jax.shard_map(
        on_device, mesh=mesh, in_specs=in_specs, out_specs=out_specs, check_vma=False
    )
```

profile of v0, /device:TPU:7, one launch (start us, length us, event | category | flops | bytes accessed | tf_op | source)
XLA Modules:
  0.0 297.5 jit_solution(8111973741452247749)
XLA Ops:
  9.3 1.6 select_bitcast_fusion
  12.1 3.2 %collective-permute-start = (bf16[256,1,128]{0,2,1:T(8,128)(2,1)S(1)}, bf16[256,1,128]{0,2,1:T(8,128)(2,1)S(1)}, u32[]{:S(2)}, u32[]{:S(2)}) collective-permute-start(bf16[256,1,128]{0,2,1:T(8,128)(2,1)S(1)} %get-tuple-element.258), channel_id=1, source_target_pairs={{0,1},{1,2},{2,3},{3,4},{4,5},{5,6},{6,7},{7,8},{8,9},{9,10},{10,1... | collective-permute-start | bytes 196616 | tf_op jit(solution)/shard_map/ppermute | solution.py:20
  15.3 4.2 %collective-permute-start.1 = (bf16[256,1,128]{0,2,1:T(8,128)(2,1)S(1)}, bf16[256,1,128]{0,2,1:T(8,128)(2,1)S(1)}, u32[]{:S(2)}, u32[]{:S(2)}) collective-permute-start(bf16[256,1,128]{0,2,1:T(8,128)(2,1)S(1)} %get-tuple-element.257), channel_id=1, source_target_pairs={{1,0},{2,1},{3,2},{4,3},{5,4},{6,5},{7,6},{8,7},{9,8},{10,9},{11,1... | collective-permute-start | bytes 196616 | tf_op jit(solution)/shard_map/ppermute | solution.py:23
  23.9 1.4 copy-done.8
  26.3 1.9 collective-permute-start.2
  28.2 5.5 %collective-permute-start.3 = (bf16[256,1,128]{0,2,1:T(8,128)(2,1)S(1)}, bf16[256,1,128]{0,2,1:T(8,128)(2,1)S(1)}, u32[]{:S(2)}, u32[]{:S(2)}) collective-permute-start(bf16[256,1,128]{0,2,1:T(8,128)(2,1)S(1)} %get-tuple-element.249), channel_id=1, source_target_pairs={{1,0},{2,1},{3,2},{4,3},{5,4},{6,5},{7,6},{8,7},{9,8},{10,9},{11,1... | collective-permute-start | bytes 196616 | tf_op jit(solution)/shard_map/ppermute | solution.py:23
  33.7 1.3 collective-permute-done.3
  35.8 1.4 copy-done.5
  37.2 3.2 %fusion.13 = f32[84,512]{1,0:T(8,128)S(1)} fusion(bf16[84,256]{1,0:T(8,128)(2,1)S(1)} %copy-done.10, bf16[2304,512]{0,1:T(8,128)(2,1)} %bitcast.145, bf16[2,256,2304]{2,1,0:T(8,128)(2,1)} %param.15, f32[512,256]{1,0:T(8,128)S(1)} %fusion.10, f32[256]{0:T(256)S(1)} %get-tuple-element.264, f32[256]{0:T(256)S(1)} %get-tuple-element.263, ...), kind=kOutput, calls=%fused_computation.21 | convolution fusion | flops 628140032 | bytes 4282372 | tf_op jit(solution)/shard_map/dot_general | solution.py:104
  42.0 48.7 %all-gather.4.cloned.1.call-done = f32[16,84,4,128]{3,2,1,0:T(4,128)} async-done(((f32[1,84,4,128]{3,2,1,0:T(4,128)}), f32[16,84,4,128]{3,2,1,0:T(4,128)}) %all-gather.4.cloned.1.call-update) | async-done | bytes 2752528 | tf_op jit(solution)/shard_map/all_gather | solution.py:30
  90.7 17.4 %while.28 = (s32[]{:T(128)}, f32[84,4,128]{2,1,0:T(4,128)S(1)}, s32[]{:T(128)}, f32[16,84,4,128]{3,2,1,0:T(4,128)}, s32[]{:T(128)}, /*index=5*/s32[]{:T(128)}) while((s32[]{:T(128)}, f32[84,4,128]{2,1,0:T(4,128)S(1)}, s32[]{:T(128)}, f32[16,84,4,128]{3,2,1,0:T(4,128)}, s32[]{:T(128)}, /*index=5*/s32[]{:T(128)}) %tuple.98), condition=%wide.region_1.2_spmd.clone, body=%wide.region_0.1_spmd.clone.sunk | while | flops 129028 | bytes 516189 | solution.py:37
  91.9 1.1 add_select_fusion.4
  93.0 1.1 add_select_fusion.4
  94.2 1.1 add_select_fusion.4
  95.4 1.1 add_select_fusion.4
  96.5 1.1 add_select_fusion.4
  97.7 1.1 add_select_fusion.4
  98.8 1.1 add_select_fusion.4
  100.0 1.1 add_select_fusion.4
  101.1 1.1 add_select_fusion.4
  102.3 1.1 add_select_fusion.4
  103.5 1.1 add_select_fusion.4
  104.6 1.1 add_select_fusion.4
  105.8 1.1 add_select_fusion.4
  106.9 1.1 add_select_fusion.4
  108.1 92.5 %all-reduce.2.cloned.1.call-done = f32[84,4,128]{2,1,0:T(4,128)} async-done(((f32[84,4,128]{2,1,0:T(4,128)}), f32[84,4,128]{2,1,0:T(4,128)}) %all-reduce.2.cloned.1.call-update) | async-done | bytes 172048 | tf_op jit(solution)/shard_map/psum | solution.py:42
  202.0 3.1 %collective-permute-start.4 = (bf16[256,1,128]{0,2,1:T(8,128)(2,1)S(1)}, bf16[256,1,128]{0,2,1:T(8,128)(2,1)S(1)}, u32[]{:S(2)}, u32[]{:S(2)}) collective-permute-start(bf16[256,1,128]{0,2,1:T(8,128)(2,1)S(1)} %get-tuple-element.242), channel_id=1, source_target_pairs={{0,1},{1,2},{2,3},{3,4},{4,5},{5,6},{6,7},{7,8},{8,9},{9,10},{10,1... | collective-permute-start | bytes 196616 | tf_op jit(solution)/shard_map/ppermute | solution.py:20
  205.1 4.3 %collective-permute-start.5 = (bf16[256,1,128]{0,2,1:T(8,128)(2,1)S(1)}, bf16[256,1,128]{0,2,1:T(8,128)(2,1)S(1)}, u32[]{:S(2)}, u32[]{:S(2)}) collective-permute-start(bf16[256,1,128]{0,2,1:T(8,128)(2,1)S(1)} %get-tuple-element.241), channel_id=1, source_target_pairs={{1,0},{2,1},{3,2},{4,3},{5,4},{6,5},{7,6},{8,7},{9,8},{10,9},{11,1... | collective-permute-start | bytes 196616 | tf_op jit(solution)/shard_map/ppermute | solution.py:23
  211.3 1.4 copy-done.9
  213.7 2.9 collective-permute-start.6
  216.6 5.2 %collective-permute-start.7 = (bf16[256,1,128]{0,2,1:T(8,128)(2,1)S(1)}, bf16[256,1,128]{0,2,1:T(8,128)(2,1)S(1)}, u32[]{:S(2)}, u32[]{:S(2)}) collective-permute-start(bf16[256,1,128]{0,2,1:T(8,128)(2,1)S(1)} %get-tuple-element.233), channel_id=1, source_target_pairs={{1,0},{2,1},{3,2},{4,3},{5,4},{6,5},{7,6},{8,7},{9,8},{10,9},{11,1... | collective-permute-start | bytes 196616 | tf_op jit(solution)/shard_map/ppermute | solution.py:23
  221.8 1.3 collective-permute-done.7
  223.9 1.4 copy-done.6
  225.3 3.1 %fusion.12 = f32[84,512]{1,0:T(8,128)S(1)} fusion(bf16[84,256]{1,0:T(8,128)(2,1)S(1)} %copy-done.10, bf16[2304,512]{0,1:T(8,128)(2,1)} %bitcast.147, bf16[2,256,2304]{2,1,0:T(8,128)(2,1)} %param.15, f32[512,256]{1,0:T(8,128)S(1)} %fusion.8, f32[256]{0:T(256)S(1)} %get-tuple-element.264, f32[256]{0:T(256)S(1)} %get-tuple-element.263, ...), kind=kOutput, calls=%fused_computation.19 | convolution fusion | flops 628140032 | bytes 4282372 | tf_op jit(solution)/shard_map/dot_general | solution.py:104
  229.3 43.6 %all-gather.6.cloned.1.call-done = f32[1344,4,128]{2,1,0:T(4,128)} async-done(((f32[84,4,128]{2,1,0:T(4,128)}), f32[1344,4,128]{2,1,0:T(4,128)}) %all-gather.6.cloned.1.call-update) | async-done | bytes 2752528 | tf_op jit(solution)/shard_map/all_gather | solution.py:30
  272.9 17.3 %while.29 = (s32[]{:T(128)}, f32[84,4,128]{2,1,0:T(4,128)S(1)}, s32[]{:T(128)}, f32[16,84,4,128]{3,2,1,0:T(4,128)}, s32[]{:T(128)}, /*index=5*/s32[]{:T(128)}) while((s32[]{:T(128)}, f32[84,4,128]{2,1,0:T(4,128)S(1)}, s32[]{:T(128)}, f32[16,84,4,128]{3,2,1,0:T(4,128)}, s32[]{:T(128)}, /*index=5*/s32[]{:T(128)}) %tuple.110), condition=%wide.region_4.5_spmd.clone, body=%wide.region_3.4_spmd.clone.sunk | while | flops 129028 | bytes 516189 | solution.py:37
  274.0 1.1 add_select_fusion.5
  275.2 1.1 add_select_fusion.5
  276.4 1.1 add_select_fusion.5
  277.5 1.1 add_select_fusion.5
  278.7 1.1 add_select_fusion.5
  279.8 1.1 add_select_fusion.5
  281.0 1.1 add_select_fusion.5
  282.1 1.1 add_select_fusion.5
  283.3 1.1 add_select_fusion.5
  284.5 1.1 add_select_fusion.5
  285.6 1.1 add_select_fusion.5
  286.8 1.1 add_select_fusion.5
  (107 shorter events, 17.5 us)
Async XLA Ops:
  6.5 13.8 %copy-start = (bf16[256,1024]{1,0:T(8,128)(2,1)S(1)}, bf16[256,1024]{1,0:T(8,128)(2,1)}, u32[]{:S(2)}) copy-start(bf16[256,1024]{1,0:T(8,128)(2,1)} %param.16) | copy-start | bytes 1572868
  6.5 84.2 %all-gather.4.cloned.1.call-start = ((), (), s32[]{:S(2)}) async-start(), calls=%async_computation | async-start | bytes 2924544 | tf_op jit(solution)/shard_map/all_gather | solution.py:30
  12.1 11.2 %collective-permute-start = (bf16[256,1,128]{0,2,1:T(8,128)(2,1)S(1)}, bf16[256,1,128]{0,2,1:T(8,128)(2,1)S(1)}, u32[]{:S(2)}, u32[]{:S(2)}) collective-permute-start(bf16[256,1,128]{0,2,1:T(8,128)(2,1)S(1)} %get-tuple-element.258), channel_id=1, source_target_pairs={{0,1},{1,2},{2,3},{3,4},{4,5},{5,6},{6,7},{7,8},{8,9},{9,10},{10,1... | collective-permute-start | bytes 196616 | tf_op jit(solution)/shard_map/ppermute | solution.py:20
  15.3 8.0 %collective-permute-start.1 = (bf16[256,1,128]{0,2,1:T(8,128)(2,1)S(1)}, bf16[256,1,128]{0,2,1:T(8,128)(2,1)S(1)}, u32[]{:S(2)}, u32[]{:S(2)}) collective-permute-start(bf16[256,1,128]{0,2,1:T(8,128)(2,1)S(1)} %get-tuple-element.257), channel_id=1, source_target_pairs={{1,0},{2,1},{3,2},{4,3},{5,4},{6,5},{7,6},{8,7},{9,8},{10,9},{11,1... | collective-permute-start | bytes 196616 | tf_op jit(solution)/shard_map/ppermute | solution.py:23
  23.6 1.7 copy-start.8
  26.3 7.4 %collective-permute-start.2 = (bf16[256,1,128]{0,2,1:T(8,128)(2,1)S(1)}, bf16[256,1,128]{0,2,1:T(8,128)(2,1)S(1)}, u32[]{:S(2)}, u32[]{:S(2)}) collective-permute-start(bf16[256,1,128]{0,2,1:T(8,128)(2,1)S(1)} %get-tuple-element.250), channel_id=1, source_target_pairs={{0,1},{1,2},{2,3},{3,4},{4,5},{5,6},{6,7},{7,8},{8,9},{9,10},{10,1... | collective-permute-start | bytes 196616 | tf_op jit(solution)/shard_map/ppermute | solution.py:20
  28.2 6.8 %collective-permute-start.3 = (bf16[256,1,128]{0,2,1:T(8,128)(2,1)S(1)}, bf16[256,1,128]{0,2,1:T(8,128)(2,1)S(1)}, u32[]{:S(2)}, u32[]{:S(2)}) collective-permute-start(bf16[256,1,128]{0,2,1:T(8,128)(2,1)S(1)} %get-tuple-element.249), channel_id=1, source_target_pairs={{1,0},{2,1},{3,2},{4,3},{5,4},{6,5},{7,6},{8,7},{9,8},{10,9},{11,1... | collective-permute-start | bytes 196616 | tf_op jit(solution)/shard_map/ppermute | solution.py:23
  35.3 1.9 copy-start.10
  35.8 1.4 copy-start.5
  37.2 3.3 %copy-start.2 = (f32[1,84,4,128]{3,2,1,0:T(4,128)S(1)}, f32[1,84,4,128]{3,2,1,0:T(4,128)}, u32[]{:S(2)}) copy-start(f32[1,84,4,128]{3,2,1,0:T(4,128)} %param.11) | copy-start | bytes 516100
  40.5 161.2 %copy-start.4 = (bf16[256,84]{0,1:T(8,128)(2,1)S(1)}, bf16[256,84]{0,1:T(8,128)(2,1)}, u32[]{:S(2)}) copy-start(bf16[256,84]{0,1:T(8,128)(2,1)} %param.13) | copy-start | bytes 129028
  40.5 161.2 %copy-start.7 = (f32[256]{0:T(256)S(1)}, f32[256]{0:T(256)}, u32[]{:S(2)}) copy-start(f32[256]{0:T(256)} %param.14) | copy-start | bytes 3076
  41.2 159.4 %all-reduce.2.cloned.1.call-start = ((), (), s32[]{:S(2)}) async-start(), calls=%async_computation.1 | async-start | bytes 344064 | tf_op jit(solution)/shard_map/psum | solution.py:42
  42.0 230.9 %all-gather.6.cloned.1.call-start = ((), (), s32[]{:S(2)}) async-start(), calls=%async_computation.2 | async-start | bytes 2924544 | tf_op jit(solution)/shard_map/all_gather | solution.py:30
  202.0 7.8 %collective-permute-start.4 = (bf16[256,1,128]{0,2,1:T(8,128)(2,1)S(1)}, bf16[256,1,128]{0,2,1:T(8,128)(2,1)S(1)}, u32[]{:S(2)}, u32[]{:S(2)}) collective-permute-start(bf16[256,1,128]{0,2,1:T(8,128)(2,1)S(1)} %get-tuple-element.242), channel_id=1, source_target_pairs={{0,1},{1,2},{2,3},{3,4},{4,5},{5,6},{6,7},{7,8},{8,9},{9,10},{10,1... | collective-permute-start | bytes 196616 | tf_op jit(solution)/shard_map/ppermute | solution.py:20
  205.1 5.6 %collective-permute-start.5 = (bf16[256,1,128]{0,2,1:T(8,128)(2,1)S(1)}, bf16[256,1,128]{0,2,1:T(8,128)(2,1)S(1)}, u32[]{:S(2)}, u32[]{:S(2)}) collective-permute-start(bf16[256,1,128]{0,2,1:T(8,128)(2,1)S(1)} %get-tuple-element.241), channel_id=1, source_target_pairs={{1,0},{2,1},{3,2},{4,3},{5,4},{6,5},{7,6},{8,7},{9,8},{10,9},{11,1... | collective-permute-start | bytes 196616 | tf_op jit(solution)/shard_map/ppermute | solution.py:23
  211.0 1.7 copy-start.9
  213.7 8.1 %collective-permute-start.6 = (bf16[256,1,128]{0,2,1:T(8,128)(2,1)S(1)}, bf16[256,1,128]{0,2,1:T(8,128)(2,1)S(1)}, u32[]{:S(2)}, u32[]{:S(2)}) collective-permute-start(bf16[256,1,128]{0,2,1:T(8,128)(2,1)S(1)} %get-tuple-element.234), channel_id=1, source_target_pairs={{0,1},{1,2},{2,3},{3,4},{4,5},{5,6},{6,7},{7,8},{8,9},{9,10},{10,1... | collective-permute-start | bytes 196616 | tf_op jit(solution)/shard_map/ppermute | solution.py:20
  216.6 6.5 %collective-permute-start.7 = (bf16[256,1,128]{0,2,1:T(8,128)(2,1)S(1)}, bf16[256,1,128]{0,2,1:T(8,128)(2,1)S(1)}, u32[]{:S(2)}, u32[]{:S(2)}) collective-permute-start(bf16[256,1,128]{0,2,1:T(8,128)(2,1)S(1)} %get-tuple-element.233), channel_id=1, source_target_pairs={{1,0},{2,1},{3,2},{4,3},{5,4},{6,5},{7,6},{8,7},{9,8},{10,9},{11,1... | collective-permute-start | bytes 196616 | tf_op jit(solution)/shard_map/ppermute | solution.py:23
  223.9 1.4 copy-start.6
  228.4 61.8 %copy-start.3 = (f32[84,4,128]{2,1,0:T(4,128)S(1)}, f32[84,4,128]{2,1,0:T(4,128)}, u32[]{:S(2)}) copy-start(f32[84,4,128]{2,1,0:T(4,128)} %all-reduce.2.cloned.1.call-done) | copy-start | bytes 516100
  229.2 61.0 %copy-start.1 = (f32[42,8,128]{2,1,0:T(8,128)S(1)}, f32[42,8,128]{2,1,0:T(8,128)}, u32[]{:S(2)}) copy-start(f32[42,8,128]{2,1,0:T(8,128)} %subtract_multiply_fusion) | copy-start | bytes 516100
Sparse Core Ops, SparseCore 0:
  41.3 49.3 all-gather.3
  93.1 107.5 all-reduce.1
  229.4 43.4 all-gather.5
where the time goes:
time: 300 us; the launch traced here: 298 us
  waiting for transfers between devices  189 us (63%)
  other arithmetic  42.8 us (14%)
  starting transfers between devices  30.4 us (10%)
  between operations  18.7 us (6%)
  matrix products  9.37 us (3%)
  local copies, waits for them, and re-layouts  6.55 us (2%)
    psum x1, waiting for transfers between devices, from_root(): return lax.psum(jnp.where(mine, array, jnp.zeros_like(array)), axis)  92.5 us
    all_gather x2, waiting for transfers between devices, carried_in(): pieces = lax.all_gather(value, axis)  92.3 us
    select_n x30, other arithmetic, hop(): return jnp.where(position < mine, longer, subtotal)  34.4 us
    ppermute x4, starting transfers between devices, extended(): lax.ppermute(lax.slice_in_dim(block, 0, width, axis=dim), axis, backward)  19.1 us
    ppermute x4, starting transfers between devices, extended(): lax.ppermute(lax.slice_in_dim(block, block.shape[dim] - width, None, axis...  11.2 us
    dot_general x2, matrix products, field_drift(): jnp.dot(out_weight, hidden_two.reshape(hidden_two.shape[0], -1), preferre...  6.3 us
  transfers between devices with their start and end apart: 11, of which 7 were waited for; matrix products, arithmetic and copies ran while one was open for 6% of the time, Pallas kernels for 0%

commit v1 on v0

v1 whole, which is shorter than its diff:
```python
import functools

import jax
import jax.numpy as jnp
from jax import lax
from jax.experimental import pallas as pl
from jax.experimental.pallas import tpu as pltpu
from jax.sharding import PartitionSpec as P

LEVELS = 64
C = 84
HID = 256
SLOTS = 16
ROWS = 4
COLS = 8
PIECE = 48

SIGMA_TOP = 1.0
SIGMA_LOW = 0.02
RHO = 7.0
ROOT_TOP = SIGMA_TOP ** (1.0 / RHO)
ROOT_LOW = SIGMA_LOW ** (1.0 / RHO)

F32 = jnp.float32
BF16 = jnp.bfloat16
VMEM = pltpu.VMEM
NT = (((1,), (1,)), ((), ()))
TN = (((0,), (0,)), ((), ()))


def iota(shape, dim):
    return lax.broadcasted_iota(jnp.int32, shape, dim)


def one_hot(mask):
    return jnp.where(mask, 1.0, 0.0).astype(BF16)


def sigma_of(level):
    root = ROOT_TOP + level.astype(F32) / (LEVELS - 1) * (ROOT_LOW - ROOT_TOP)
    square = root * root
    return square * square * square * root


def lane_of(channel, row):
    head = channel + jnp.where(row >= 2, 64, 0)
    tail = 128 + 32 * row + (channel - 64)
    return jnp.where(channel < 64, head, tail)


def pack_kernel(levels_ref, x_ref, o_ref):
    slot = lax.axis_index("tm")
    level = levels_ref[slot]
    sigma = sigma_of(jnp.full((1, 128), level, jnp.int32))
    scale = jnp.sqrt(sigma * sigma + 0.25)
    scaled = pltpu.roll(x_ref[...] / scale, 4, 1).astype(BF16)
    shape = (C * ROWS, 3 * 128)
    index, lane = iota(shape, 0), iota(shape, 1)
    channel, row = index >> 2, index & 3
    target = lane_of(channel, row)
    target = jnp.where(target < 128, target + 128 * (row & 1), target + 128)
    packed = lax.dot_general(scaled, one_hot(lane == target), TN, preferred_element_type=F32)
    for window in range(SLOTS):
        start = COLS * window
        if window < SLOTS - 1:
            part = packed[start : start + 2 * COLS]
        else:
            part = jnp.concatenate([packed[start:], packed[:COLS]], axis=0)
        part = part.astype(BF16)
        for group in range(3):
            o_ref[window, 16 * group : 16 * group + 16, :] = part[:, 128 * group : 128 * group + 128]


def pack(levels, x):
    return pl.pallas_call(
        pack_kernel,
        out_shape=jax.ShapeDtypeStruct((SLOTS, PIECE, 128), BF16),
        in_specs=[pl.BlockSpec(memory_space=pltpu.SMEM), pl.BlockSpec(memory_space=VMEM)],
        out_specs=pl.BlockSpec(memory_space=VMEM),
        name="pack",
    )(levels, x)


def tables_kernel(now_ref, next_ref, in_w_ref, cond_ref, out_w_ref, film_ref, coef_ref, in_pack_ref, pick_ref, in_t_ref, out_t_ref):
    now, following = sigma_of(now_ref[...]), sigma_of(next_ref[...])
    variance = now * now + 0.25
    root = jnp.sqrt(variance)
    ratio = (following - now) / now
    coef_ref[0] = 1.0 / root
    coef_ref[1] = root
    coef_ref[2] = (1.0 - 0.25 / variance) * ratio
    coef_ref[3] = 0.5 * now / root * ratio
    j = iota((SLOTS, 128), 1).astype(F32)
    frequency = jnp.exp(j * (jnp.log(F32(100.0)) / 128.0))
    phases = jnp.log(now) / 4.0 * frequency
    embedding = jnp.concatenate([jnp.cos(phases), jnp.sin(phases)], axis=1).astype(BF16)
    conditions = jnp.dot(embedding, cond_ref[...], preferred_element_type=F32)
    film_ref[0] = 0.5 * (1.0 + conditions[:, 0:256])
    film_ref[1] = 0.5 * conditions[:, 256:512]
    film_ref[2] = 0.5 * (1.0 + conditions[:, 512:768])
    film_ref[3] = 0.5 * conditions[:, 768:1024]
    channel, lane = iota((128, 256), 0), iota((128, 256), 1)
    in_w = in_w_ref[...]
    for row in range(ROWS):
        pick = one_hot((lane == lane_of(channel, row)) & (channel < C))
        pick_ref[row] = pick
        in_pack_ref[row] = jnp.dot(in_w, pick[:C], preferred_element_type=F32).astype(BF16)
    eye = one_hot((iota((C, 128), 0) == iota((C, 128), 1)))
    in_t_ref[...] = jnp.dot(in_w, eye, preferred_element_type=F32).astype(BF16)
    out_t_ref[...] = lax.dot_general(eye, out_w_ref[...], TN, preferred_element_type=F32).astype(BF16)


def tables(now, following, in_weight, cond_weight, out_weight):
    return pl.pallas_call(
        tables_kernel,
        out_shape=[
            jax.ShapeDtypeStruct((4, SLOTS, HID), F32),
            jax.ShapeDtypeStruct((4, SLOTS, 128), F32),
            jax.ShapeDtypeStruct((ROWS, HID, 256), BF16),
            jax.ShapeDtypeStruct((ROWS, 128, 256), BF16),
            jax.ShapeDtypeStruct((HID, 128), BF16),
            jax.ShapeDtypeStruct((128, HID), BF16),
        ],
        in_specs=[pl.BlockSpec(memory_space=VMEM)] * 5,
        out_specs=[pl.BlockSpec(memory_space=VMEM)] * 6,
        name="tables",
    )(now, following, in_weight, cond_weight, out_weight)


def split(value):
    high = value.astype(BF16)
    return high, (value - high.astype(F32)).astype(BF16)


def taps(ref, row, pitch, start, count):
    parts = []
    for a in (-1, 0, 1):
        for b in (-1, 0, 1):
            parts.append(ref[pl.ds((row + a) * pitch + start + 16 * b, count), :])
    return jnp.concatenate(parts, axis=1)


def film(response, scale, shift):
    cells = response.shape[0] // SLOTS
    half = response.reshape(cells, SLOTS, HID) * scale[None] + shift[None]
    return (half * jnp.tanh(half) + half).reshape(cells * SLOTS, HID)


def main_kernel(low_ref, own_ref, high_ref, film_ref, coef_ref, in_pack_ref, pick_ref, in_t_ref, out_t_ref, bias_ref, conv_ref, o_ref, h0, h1, g0, g1, x1, s2):
    place = lax.axis_index("lat")
    count = lax.axis_size("lat")
    inside_low = jnp.where(place > 0, 1.0, 0.0).astype(F32)
    inside_high = jnp.where(place < count - 1, 1.0, 0.0).astype(F32)
    blocks = (low_ref, own_ref, high_ref)
    gates = (inside_low, F32(1.0), inside_high)
    bias = bias_ref[...]

    shape = (256, 256)
    to, frm = iota(shape, 0), iota(shape, 1)
    swap = one_hot(((to >> 4) == (frm & 15)) & ((to & 15) == (frm >> 4)))

    packed = []
    for ref in blocks:
        groups = []
        for group in range(3):
            part = ref[:, 16 * group : 16 * group + 16, :].reshape(256, 128)
            groups.append(jnp.dot(swap, part, preferred_element_type=F32).astype(BF16))
        packed.append(groups)
    for row in range(ROWS):
        for at in range(3):
            lhs = jnp.concatenate([packed[at][row & 1], packed[at][2]], axis=1)
            hidden = lax.dot_general(lhs, in_pack_ref[row], NT, preferred_element_type=F32) + bias * gates[at]
            i = 4 * at + row
            h0[256 * i : 256 * i + 256, :] = hidden.astype(BF16)
            if 2 <= i < 10:
                value = lax.dot_general(lhs[32:224], pick_ref[row], NT, preferred_element_type=F32)
                value = value.reshape(12, SLOTS, 128) * coef_ref[1][None]
                x1[192 * (i - 2) : 192 * (i - 2) + 192, :] = value.reshape(192, 128)

    def gate_of(row):
        outside = ((place == 0) & (row < 0)) | ((place == count - 1) & (row >= ROWS))
        return jnp.where(outside, 0.0, 1.0).astype(F32)

    def conv_one(i, _):
        gate = gate_of(i - 4)
        response = lax.dot_general(taps(h0, i, 256, 16, 224), conv_ref[0], NT, preferred_element_type=F32)
        hidden = film(response, film_ref[0] * gate, film_ref[1] * gate)
        h1[pl.ds((i - 1) * 224, 224), :] = hidden.astype(BF16)
        return 0

    lax.fori_loop(1, 11, conv_one, 0, unroll=2)

    to, frm = iota((192, 384), 0), iota((192, 384), 1)
    frm = jnp.where(frm >= 192, frm - 192, frm)
    before = one_hot(((to >> 4) == (frm >> 4)) & ((frm & 15) < (to & 15)))

    def conv_two(i, _):
        gate = gate_of(i - 3)
        response = lax.dot_general(taps(h1, i, 224, 16, 192), conv_ref[1], NT, preferred_element_type=F32)
        hidden = h1[pl.ds(i * 224 + 16, 192), :].astype(F32) + film(response, film_ref[2], film_ref[3])
        network = lax.dot_general(hidden.astype(BF16), out_t_ref[...], NT, preferred_element_type=F32)
        x = x1[pl.ds((i - 1) * 192, 192), :].reshape(12, SLOTS, 128)
        drift = coef_ref[2][None] * x - coef_ref[3][None] * network.reshape(12, SLOTS, 128)
        high, low = split(drift.reshape(192, 128))
        earlier = jnp.dot(before, jnp.concatenate([high, low], axis=0), preferred_element_type=F32)
        state = earlier.reshape(12, SLOTS, 128) + x[:, 0:1, :]
        s2[pl.ds((i - 1) * 192, 192), :] = state.reshape(192, 128)
        scaled = (state * (coef_ref[0] * gate)[None]).reshape(192, 128).astype(BF16)
        hidden = lax.dot_general(scaled, in_t_ref[...], NT, preferred_element_type=F32) + bias * gate
        g0[pl.ds((i - 1) * 192, 192), :] = hidden.astype(BF16)
        return 0

    lax.fori_loop(1, 9, conv_two, 0, unroll=2)

    def conv_three(i, _):
        gate = gate_of(i - 2)
        response = lax.dot_general(taps(g0, i, 192, 16, 160), conv_ref[0], NT, preferred_element_type=F32)
        hidden = film(response, film_ref[0] * gate, film_ref[1] * gate)
        g1[pl.ds((i - 1) * 160, 160), :] = hidden.astype(BF16)
        return 0

    lax.fori_loop(1, 7, conv_three, 0, unroll=2)

    to, frm = iota((128, 512), 0), iota((128, 512), 1)
    part, source = frm >> 7, frm & 127
    same = (to & 7) == (source >> 4)
    upto = (part < 2) & ((source & 15) <= (to >> 3))
    start = (part >= 2) & ((source & 15) == 0)
    gather = one_hot(same & (upto | start))

    for row in range(ROWS):
        response = lax.dot_general(taps(g1, row + 1, 160, 16, 128), conv_ref[1], NT, preferred_element_type=F32)
        hidden = g1[160 * (row + 1) + 16 : 160 * (row + 1) + 144, :].astype(F32) + film(response, film_ref[2], film_ref[3])
        network = lax.dot_general(hidden.astype(BF16), out_t_ref[...], NT, preferred_element_type=F32)
        state = s2[192 * (row + 2) + 32 : 192 * (row + 2) + 160, :].reshape(COLS, SLOTS, 128)
        drift = coef_ref[2][None] * state - coef_ref[3][None] * network.reshape(COLS, SLOTS, 128)
        high, low = split(drift.reshape(128, 128))
        anchor_high, anchor_low = split(state.reshape(128, 128))
        advanced = jnp.dot(gather, jnp.concatenate([high, low, anchor_high, anchor_low], axis=0), preferred_element_type=F32)
        o_ref[:, COLS * row : COLS * row + COLS, :] = advanced.reshape(SLOTS, COLS, 128).astype(BF16)


def main(low, own, high, film_table, coef, in_pack, pick, in_t, out_t, bias, conv_weight):
    return pl.pallas_call(
        main_kernel,
        out_shape=jax.ShapeDtypeStruct((SLOTS, ROWS * COLS, 128), BF16),
        in_specs=[pl.BlockSpec(memory_space=VMEM)] * 11,
        out_specs=pl.BlockSpec(memory_space=VMEM),
        scratch_shapes=[
            VMEM((12 * 256, HID), BF16),
            VMEM((10 * 224, HID), BF16),
            VMEM((8 * 192, HID), BF16),
            VMEM((6 * 160, HID), BF16),
            VMEM((8 * 192, 128), F32),
            VMEM((8 * 192, 128), F32),
        ],
        name="patch",
    )(low, own, high, film_table, coef, in_pack, pick, in_t, out_t, bias, conv_weight)


def unpack_kernel(p_ref, o_ref):
    for row in range(ROWS):
        part = jnp.concatenate(
            [p_ref[w, :, :].astype(F32)[COLS * row : COLS * row + COLS, :] for w in range(SLOTS)], axis=0
        )
        o_ref[pl.ds(row, C, stride=ROWS), :] = part.T[:C]


def unpack(pieces):
    return pl.pallas_call(
        unpack_kernel,
        out_shape=jax.ShapeDtypeStruct((C * ROWS, 128), F32),
        in_specs=[pl.BlockSpec(memory_space=VMEM)],
        out_specs=pl.BlockSpec(memory_space=VMEM),
        name="unpack",
    )(pieces)


def on_device(trajectory, step_levels, in_weight, in_bias, conv_weight, cond_weight, out_weight):
    count = lax.axis_size("lat")
    forward = [(i, i + 1) for i in range(count - 1)]
    backward = [(b, a) for a, b in forward]
    pieces = pack(step_levels, trajectory.reshape(C * ROWS, 128))
    own = lax.all_to_all(pieces, "tm", 0, 0)
    low = lax.ppermute(own, "lat", forward)
    high = lax.ppermute(own, "lat", backward)
    now = jnp.broadcast_to(step_levels[:-1, None], (SLOTS, 128))
    following = jnp.broadcast_to(step_levels[1:, None], (SLOTS, 128))
    prepared = tables(now, following, in_weight, cond_weight, out_weight)
    done = main(low, own, high, *prepared, in_bias[None, :], conv_weight)
    back = lax.all_to_all(done, "tm", 0, 0)
    return unpack(back).reshape(1, C, ROWS, 128)


def solution(mesh):
    in_specs = (P("tm", None, "lat", None), P(), P(), P(), P(), P(), P())
    out_specs = P("tm", None, "lat", None)
    return jax.shard_map(on_device, mesh=mesh, in_specs=in_specs, out_specs=out_specs, check_vma=False)
```

time: 300 us -> 80.7 us (0.27)
  waiting for transfers between devices: 189 us -> 12.7 us
  other arithmetic: 42.8 us -> 0 us
  Pallas kernels: 0 us -> 30.9 us
  between operations: 18.7 us -> 0.03 us
  blocking collectives: 0 us -> 14.1 us
  starting transfers between devices: 30.4 us -> 18.3 us
  matrix products: 9.37 us -> 0 us
    psum x1 -> x0, waiting for transfers between devices: 92.5 us -> none  [from_root(): return lax.psum(jnp.where(mine, array, jnp.zeros_like(array)), axis)]
    all_gather x2 -> x0, waiting for transfers between devices: 92.3 us -> none  [carried_in(): pieces = lax.all_gather(value, axis)]
    select_n x31 -> x0, other arithmetic: 36.1 us -> none  [the longest x30 34.4 us: hop(): return jnp.where(position < mine, longer, subtotal)]
    pallas_call x0 -> x4, Pallas kernels: none -> 30.9 us  [the longest x1 24.9 us: main(): pl.pallas_call(main_kernel, out_shape=jax.ShapeDtypeStruct((SLOTS, ROWS *...]
    ppermute x8 -> x2, starting transfers between devices: 30.3 us -> 7.28 us  [the longest x1 5.36 us: on_device(): high = lax.ppermute(own, 'lat', backward)]
    all_to_all x0 -> x1, blocking collectives: none -> 14.1 us  [on_device(): back = lax.all_to_all(done, 'tm', 0, 0)]
    all_to_all x0 -> x1, starting transfers between devices: none -> 11 us  [on_device(): own = lax.all_to_all(pieces, 'tm', 0, 0)]
    dot_general x7 -> x0, matrix products: 9.37 us -> none  [the longest x2 6.3 us: field_drift(): jnp.dot(out_weight, hidden_two.reshape(hidden_two.shape[0], -1), preferre...]
  transfers between devices with their start and end apart: 11 -> 3, of which waited for: 7 -> 2; matrix products, arithmetic and copies ran while one was open for 6% -> 5% of each run, Pallas kernels for 0% -> 3%
where the time goes in v1:
time: 80.7 us; the launch traced here: 80.3 us
  Pallas kernels  30.9 us (38%)
  starting transfers between devices  18.3 us (23%)
  blocking collectives  14.1 us (17%)
  waiting for transfers between devices  12.7 us (16%)
  local copies, waits for them, and re-layouts  4.34 us (5%)
    pallas_call x1, Pallas kernels, main(): pl.pallas_call(main_kernel, out_shape=jax.ShapeDtypeStruct((SLOTS, ROWS *...  24.9 us
    all_to_all x1, blocking collectives, on_device(): back = lax.all_to_all(done, 'tm', 0, 0)  14.1 us
    all_to_all x1, starting transfers between devices, on_device(): own = lax.all_to_all(pieces, 'tm', 0, 0)  11 us
    all_to_all x1, waiting for transfers between devices, on_device(): own = lax.all_to_all(pieces, 'tm', 0, 0)  8.68 us
    ppermute x1, starting transfers between devices, on_device(): high = lax.ppermute(own, 'lat', backward)  5.36 us
    ppermute x1, waiting for transfers between devices, on_device(): low = lax.ppermute(own, 'lat', forward)  3.99 us
    pallas_call x1, Pallas kernels, tables(): pl.pallas_call(tables_kernel, out_shape=[jax.ShapeDtypeStruct((4, SLOTS,...  2.35 us
    unnamed x7, local copies, waits for them, and re-layouts  2.21 us
  transfers between devices with their start and end apart: 3, of which 2 were waited for; matrix products, arithmetic and copies ran while one was open for 5% of the time, Pallas kernels for 3%

profile of v1, /device:TPU:7, one launch (start us, length us, event | category | flops | bytes accessed | tf_op | source)
XLA Modules:
  0.0 80.3 jit_solution(2561422584732441280)
XLA Ops:
  0.0 2.0 %pack.1 = bf16[16,48,128]{2,1,0:T(8,128)(2,1)} custom-call(s32[17]{0:T(128)} %levels_ref.1, f32[336,128]{1,0:T(8,128)} %bitcast.3), custom_call_target="tpu_custom_call" | custom-call | tf_op jit(solution)/shard_map/pack/pallas_call | solution.py:75
  2.0 11.0 %all-to-all-start = ((bf16[16,48,128]{2,1,0:T(8,128)(2,1)}), bf16[16,48,128]{2,1,0:T(8,128)(2,1)S(1)}, u32[]{:S(2)}, u32[]{:S(2)}) async-start(bf16[16,48,128]{2,1,0:T(8,128)(2,1)} %pack.1), calls=%async_computation | async-start | bytes 393216 | tf_op jit(solution)/shard_map/all_to_all | solution.py:284
  13.0 1.5 %copy.8.in_w_ref = bf16[256,84]{1,0:T(8,128)(2,1)} copy(bf16[256,84]{0,1:T(8,128)(2,1)} %param.9) | data formatting | bytes 86016 | tf_op args[2]
  14.5 8.7 %all-to-all-done.own_ref = bf16[16,48,128]{2,1,0:T(8,128)(2,1)S(1)} async-done(((bf16[16,48,128]{2,1,0:T(8,128)(2,1)}), bf16[16,48,128]{2,1,0:T(8,128)(2,1)S(1)}, u32[]{:S(2)}, u32[]{:S(2)}) %all-to-all-start) | async-done | bytes 196640 | tf_op jit(solution)/shard_map/all_to_all | solution.py:284
  23.2 0.0 copy-start
  23.2 5.4 %collective-permute-start.1 = (bf16[16,48,128]{2,1,0:T(8,128)(2,1)S(1)}, bf16[16,48,128]{2,1,0:T(8,128)(2,1)S(1)}, u32[]{:S(2)}, u32[]{:S(2)}) collective-permute-start(bf16[16,48,128]{2,1,0:T(8,128)(2,1)S(1)} %all-to-all-done.own_ref), channel_id=1, source_target_pairs={{1,0},{2,1},{3,2},{4,3},{5,4},{6,5},{7,6},{8,7},{9,8},{10,9},{11,1... | collective-permute-start | bytes 589832 | tf_op jit(solution)/shard_map/ppermute | solution.py:286
  28.5 1.9 %collective-permute-start = (bf16[16,48,128]{2,1,0:T(8,128)(2,1)S(1)}, bf16[16,48,128]{2,1,0:T(8,128)(2,1)S(1)}, u32[]{:S(2)}, u32[]{:S(2)}) collective-permute-start(bf16[16,48,128]{2,1,0:T(8,128)(2,1)S(1)} %all-to-all-done.own_ref), channel_id=1, source_target_pairs={{0,1},{1,2},{2,3},{3,4},{4,5},{5,6},{6,7},{7,8},{8,9},{9,10},{10,1... | collective-permute-start | bytes 589832 | tf_op jit(solution)/shard_map/ppermute | solution.py:285
  30.5 0.8 %fusion = (s32[16]{0:T(128)S(1)}, s32[16]{0:T(128)S(1)}) fusion(s32[17]{0:T(128)} %levels_ref.1), kind=kLoop, calls=%fused_computation | loop fusion | bytes 256 | tf_op jit(solution)/shard_map/slice | solution.py:288
  31.3 0.7 broadcast_in_dim.7.next_ref
  31.9 0.7 broadcast_in_dim.6.now_ref
  32.6 2.3 %tables.1 = (f32[4,16,256]{2,1,0:T(8,128)}, f32[4,16,128]{2,1,0:T(8,128)}, bf16[4,256,256]{2,1,0:T(8,128)(2,1)}, bf16[4,128,256]{2,1,0:T(8,128)(2,1)}, bf16[256,...) custom-call(s32[16,128]{1,0:T(8,128)} %broadcast_in_dim.6.now_ref, s32[16,128]{1,0:T(8,128)} %broadcast_in_dim.7.next_ref, ...), custom_call_target="tpu_custom_call" | custom-call | tf_op jit(solution)/shard_map/tables/pallas_call | solution.py:114
  35.0 0.0 collective-permute-done.1.high_ref
  35.0 0.0 copy-start.1
  35.0 4.0 %collective-permute-done.low_ref = bf16[16,48,128]{2,1,0:T(8,128)(2,1)S(1)} collective-permute-done((bf16[16,48,128]{2,1,0:T(8,128)(2,1)S(1)}, bf16[16,48,128]{2,1,0:T(8,128)(2,1)S(1)}, u32[]{:S(2)}, u32[]{:S(2)}) %collective-permute-start) | collective-permute-done | bytes 196640 | tf_op jit(solution)/shard_map/ppermute | solution.py:285
  39.0 0.0 copy-start.2
  39.0 0.0 copy-done
  39.0 0.0 copy-done.1
  39.0 0.7 copy-done.2
  39.6 24.9 %patch.1 = bf16[16,32,128]{2,1,0:T(8,128)(2,1)} custom-call(bf16[16,48,128]{2,1,0:T(8,128)(2,1)} %copy-done.2, bf16[16,48,128]{2,1,0:T(8,128)(2,1)} %copy-done, bf16[16,48,128]{2,1,0:T(8,128)(2,1)} %copy-done.1, f32[4,16,256]{2,1,0:T(8,128)} %get-tuple-element.11.film_ref, f32[4,16,128]{2,1,0:T(8,128)} %get-tuple-element.12.coef_ref, ...), custom_call_target="tpu_custom_call" | custom-call | tf_op jit(solution)/shard_map/patch/pallas_call | solution.py:244
  64.5 14.1 %all_to_all.10.p_ref = bf16[16,32,128]{2,1,0:T(8,128)(2,1)} all-to-all(bf16[16,32,128]{2,1,0:T(8,128)(2,1)} %patch.1), channel_id=1, replica_groups=mesh['tm'=16,'lat'=32] {'tm'}, dimensions={0} | all-to-all | bytes 262144 | tf_op jit(solution)/shard_map/all_to_all | solution.py:291
  78.6 1.7 %unpack.1 = f32[336,128]{1,0:T(8,128)} custom-call(bf16[16,32,128]{2,1,0:T(8,128)(2,1)} %all_to_all.10.p_ref), custom_call_target="tpu_custom_call" | custom-call | tf_op jit(solution)/shard_map/unpack/pallas_call | solution.py:270
Async XLA Ops:
  2.0 21.2 %all-to-all-start = ((bf16[16,48,128]{2,1,0:T(8,128)(2,1)}), bf16[16,48,128]{2,1,0:T(8,128)(2,1)S(1)}, u32[]{:S(2)}, u32[]{:S(2)}) async-start(bf16[16,48,128]{2,1,0:T(8,128)(2,1)} %pack.1), calls=%async_computation | async-start | bytes 393216 | tf_op jit(solution)/shard_map/all_to_all | solution.py:284
  23.2 15.8 %copy-start = (bf16[16,48,128]{2,1,0:T(8,128)(2,1)}, bf16[16,48,128]{2,1,0:T(8,128)(2,1)S(1)}, u32[]{:S(2)}) copy-start(bf16[16,48,128]{2,1,0:T(8,128)(2,1)S(1)} %all-to-all-done.own_ref) | copy-start | bytes 589828
  23.2 11.8 %collective-permute-start.1 = (bf16[16,48,128]{2,1,0:T(8,128)(2,1)S(1)}, bf16[16,48,128]{2,1,0:T(8,128)(2,1)S(1)}, u32[]{:S(2)}, u32[]{:S(2)}) collective-permute-start(bf16[16,48,128]{2,1,0:T(8,128)(2,1)S(1)} %all-to-all-done.own_ref), channel_id=1, source_target_pairs={{1,0},{2,1},{3,2},{4,3},{5,4},{6,5},{7,6},{8,7},{9,8},{10,9},{11,1... | collective-permute-start | bytes 589832 | tf_op jit(solution)/shard_map/ppermute | solution.py:286
  28.5 10.4 %collective-permute-start = (bf16[16,48,128]{2,1,0:T(8,128)(2,1)S(1)}, bf16[16,48,128]{2,1,0:T(8,128)(2,1)S(1)}, u32[]{:S(2)}, u32[]{:S(2)}) collective-permute-start(bf16[16,48,128]{2,1,0:T(8,128)(2,1)S(1)} %all-to-all-done.own_ref), channel_id=1, source_target_pairs={{0,1},{1,2},{2,3},{3,4},{4,5},{5,6},{6,7},{7,8},{8,9},{9,10},{10,1... | collective-permute-start | bytes 589832 | tf_op jit(solution)/shard_map/ppermute | solution.py:285
  35.0 4.0 %copy-start.1 = (bf16[16,48,128]{2,1,0:T(8,128)(2,1)}, bf16[16,48,128]{2,1,0:T(8,128)(2,1)S(1)}, u32[]{:S(2)}) copy-start(bf16[16,48,128]{2,1,0:T(8,128)(2,1)S(1)} %collective-permute-done.1.high_ref) | copy-start | bytes 589828
  39.0 0.7 copy-start.2

commit v2 on v1

v2 whole, which is shorter than its diff:
```python
import functools

import jax
import jax.numpy as jnp
from jax import lax
from jax.experimental import pallas as pl
from jax.experimental.pallas import tpu as pltpu
from jax.sharding import PartitionSpec as P

LEVELS = 64
C = 84
HID = 256
SLOTS = 16
ROWS = 4
COLS = 8
PIECE = 48
BACK = 24

SIGMA_TOP = 1.0
SIGMA_LOW = 0.02
RHO = 7.0
ROOT_TOP = SIGMA_TOP ** (1.0 / RHO)
ROOT_LOW = SIGMA_LOW ** (1.0 / RHO)

F32 = jnp.float32
BF16 = jnp.bfloat16
VMEM = pltpu.VMEM
NT = (((1,), (1,)), ((), ()))
TN = (((0,), (0,)), ((), ()))


def iota(shape, dim):
    return lax.broadcasted_iota(jnp.int32, shape, dim)


def one_hot(mask):
    return jnp.where(mask, 1.0, 0.0).astype(BF16)


def sigma_of(level):
    root = ROOT_TOP + level.astype(F32) / (LEVELS - 1) * (ROOT_LOW - ROOT_TOP)
    square = root * root
    return square * square * square * root


def lane_of(channel, row):
    head = channel + jnp.where(row >= 2, 64, 0)
    tail = 128 + 32 * row + (channel - 64)
    return jnp.where(channel < 64, head, tail)


def pack_kernel(levels_hbm, x_hbm, o_ref, levels_ref, x_ref, sems):
    get_levels = pltpu.make_async_copy(levels_hbm, levels_ref, sems.at[0])
    get_x = pltpu.make_async_copy(x_hbm, x_ref, sems.at[1])
    get_levels.start()
    get_x.start()
    slot = lax.axis_index("tm")
    shape = (C * ROWS, 3 * 128)
    index, lane = iota(shape, 0), iota(shape, 1)
    channel, row = index >> 2, index & 3
    target = lane_of(channel, row)
    target = jnp.where(target < 128, target + 128 * (row & 1), target + 128)
    places = one_hot(lane == target)
    get_levels.wait()
    sigma = sigma_of(jnp.full((1, 128), levels_ref[slot], jnp.int32))
    scale = jnp.sqrt(sigma * sigma + 0.25)
    get_x.wait()
    scaled = pltpu.roll(x_ref[...] / scale, 4, 1).astype(BF16)
    packed = lax.dot_general(scaled, places, TN, preferred_element_type=F32)
    for window in range(SLOTS):
        start = COLS * window
        if window < SLOTS - 1:
            part = packed[start : start + 2 * COLS]
        else:
            part = jnp.concatenate([packed[start:], packed[:COLS]], axis=0)
        part = part.astype(BF16)
        for group in range(3):
            o_ref[window, 16 * group : 16 * group + 16, :] = part[:, 128 * group : 128 * group + 128]


def pack(levels, x):
    return pl.pallas_call(
        pack_kernel,
        out_shape=jax.ShapeDtypeStruct((SLOTS, PIECE, 128), BF16),
        in_specs=[pl.BlockSpec(memory_space=pltpu.HBM)] * 2,
        out_specs=pl.BlockSpec(memory_space=VMEM),
        scratch_shapes=[
            pltpu.SMEM((SLOTS + 1,), jnp.int32),
            VMEM((C * ROWS, 128), F32),
            pltpu.SemaphoreType.DMA((2,)),
        ],
        name="pack",
        compiler_params=pltpu.CompilerParams(vmem_limit_bytes=12 << 20),
    )(levels, x)


def tables_kernel(levels_hbm, in_w_hbm, bias_hbm, cond_hbm, out_w_hbm, conv_hbm, film_ref, coef_ref, in_pack_ref, in_t_ref, out_t_ref, bias_ref, conv_ref, swap_ref, before_ref, gather_ref, levels_ref, in_w_ref, cond_ref, out_w_ref, sems):
    sources = (levels_hbm, in_w_hbm, cond_hbm, out_w_hbm, bias_hbm, conv_hbm)
    targets = (levels_ref, in_w_ref, cond_ref, out_w_ref, bias_ref, conv_ref)
    copies = [pltpu.make_async_copy(a, b, sems.at[i]) for i, (a, b) in enumerate(zip(sources, targets))]
    for copy in copies:
        copy.start()
    to, frm = iota((256, 256), 0), iota((256, 256), 1)
    swap_ref[...] = one_hot(((to >> 4) == (frm & 15)) & ((to & 15) == (frm >> 4)))
    to, frm = iota((128, 256), 0), iota((128, 256), 1) & 127
    before_ref[...] = one_hot(((to >> 4) == (frm >> 4)) & ((frm & 15) < (to & 15)))
    gather_ref[...] = one_hot(((to & 7) == (frm >> 4)) & ((frm & 15) <= (to >> 3)))
    copies[0].wait()
    place = iota((SLOTS, 128), 0)
    now = jnp.zeros((SLOTS, 128), jnp.int32)
    following = now
    for k in range(SLOTS):
        now = jnp.where(place == k, levels_ref[k], now)
        following = jnp.where(place == k, levels_ref[k + 1], following)
    now, following = sigma_of(now), sigma_of(following)
    variance = now * now + 0.25
    root = jnp.sqrt(variance)
    ratio = (following - now) / now
    coef_ref[0] = 1.0 / root
    coef_ref[1] = root
    coef_ref[2] = (1.0 - 0.25 / variance) * ratio
    coef_ref[3] = 0.5 * now / root * ratio
    j = iota((SLOTS, 128), 1).astype(F32)
    frequency = jnp.exp(j * (jnp.log(F32(100.0)) / 128.0))
    phases = jnp.log(now) / 4.0 * frequency
    embedding = jnp.concatenate([jnp.cos(phases), jnp.sin(phases)], axis=1).astype(BF16)
    copies[1].wait()
    copies[2].wait()
    copies[3].wait()
    conditions = jnp.dot(embedding, cond_ref[...], preferred_element_type=F32)
    film_ref[0] = 0.5 * (1.0 + conditions[:, 0:256])
    film_ref[1] = 0.5 * conditions[:, 256:512]
    film_ref[2] = 0.5 * (1.0 + conditions[:, 512:768])
    film_ref[3] = 0.5 * conditions[:, 768:1024]
    channel, lane = iota((C, 256), 0), iota((C, 256), 1)
    for row in range(ROWS):
        pick = one_hot(lane == lane_of(channel, row))
        in_pack_ref[row] = lax.dot_general(pick, in_w_ref[...], TN, preferred_element_type=F32).astype(BF16)
    eye = one_hot(iota((C, 128), 0) == iota((C, 128), 1))
    in_t_ref[...] = lax.dot_general(eye, in_w_ref[...], TN, preferred_element_type=F32).astype(BF16)
    out_t_ref[...] = lax.dot_general(out_w_ref[...], eye, TN, preferred_element_type=F32).astype(BF16)
    copies[4].wait()
    copies[5].wait()


def tables(levels, in_weight_t, in_bias, cond_weight, out_weight, conv_weight):
    return pl.pallas_call(
        tables_kernel,
        out_shape=[
            jax.ShapeDtypeStruct((4, SLOTS, HID), F32),
            jax.ShapeDtypeStruct((4, SLOTS, 128), F32),
            jax.ShapeDtypeStruct((ROWS, 256, HID), BF16),
            jax.ShapeDtypeStruct((128, HID), BF16),
            jax.ShapeDtypeStruct((HID, 128), BF16),
            jax.ShapeDtypeStruct((1, HID), F32),
            jax.ShapeDtypeStruct((2, HID, 9 * HID), BF16),
            jax.ShapeDtypeStruct((256, 256), BF16),
            jax.ShapeDtypeStruct((128, 256), BF16),
            jax.ShapeDtypeStruct((128, 256), BF16),
        ],
        in_specs=[pl.BlockSpec(memory_space=pltpu.HBM)] * 6,
        out_specs=[pl.BlockSpec(memory_space=VMEM)] * 10,
        scratch_shapes=[
            pltpu.SMEM((SLOTS + 1,), jnp.int32),
            VMEM((C, HID), BF16),
            VMEM((256, 1024), BF16),
            VMEM((C, HID), BF16),
            pltpu.SemaphoreType.DMA((6,)),
        ],
        name="tables",
        compiler_params=pltpu.CompilerParams(vmem_limit_bytes=12 << 20),
    )(levels, in_weight_t, in_bias, cond_weight, out_weight, conv_weight)


def split(value):
    high = value.astype(BF16)
    return high, (value - high.astype(F32)).astype(BF16)


def convolve(ref, top, rows, cells, weight):
    parts = []
    for a in range(3):
        for b in range(3):
            view = ref[top + a : top + a + rows, 16 * b : 16 * b + cells, :]
            parts.append(view.reshape(rows * cells, HID))
    return lax.dot_general(jnp.concatenate(parts, axis=1), weight, NT, preferred_element_type=F32)


def film(response, scale, shift):
    cells = response.shape[0] // SLOTS
    half = response.reshape(cells, SLOTS, HID) * scale[None] + shift[None]
    return (half * jnp.tanh(half) + half).reshape(cells * SLOTS, HID)


def halves(value):
    high, low = split(value)
    return jnp.concatenate([high, low], axis=0)


def main_kernel(low_ref, own_ref, high_ref, film_ref, coef_ref, in_pack_ref, in_t_ref, out_t_ref, bias_ref, conv_ref, swap_ref, before_ref, gather_ref, o_ref, h0, h1, g0, g1, x1, s2):
    place = lax.axis_index("lat")
    count = lax.axis_size("lat")
    inside_low = jnp.where(place > 0, 1.0, 0.0).astype(F32)
    inside_high = jnp.where(place < count - 1, 1.0, 0.0).astype(F32)
    gates = (inside_low, F32(1.0), inside_high)
    bias = bias_ref[...]
    lane = iota((1, 128), 1)
    first = iota((1, SLOTS, 128), 1) == 0

    def gate_of(row):
        return inside_low if row < 0 else inside_high if row >= ROWS else F32(1.0)

    blocks = [
        [ref[:, 16 * group : 16 * group + 16, :].reshape(256, 128) for group in range(3)]
        for ref in (low_ref, own_ref, high_ref)
    ]
    swap = swap_ref[...]

    def swapped(left, right):
        both = jnp.dot(swap, jnp.concatenate([left, right], axis=1), preferred_element_type=F32)
        return both[:, :128], both[:, 128:]

    heads = [swapped(block[0], block[1]) for block in blocks]
    tails = [*swapped(blocks[0][2], blocks[1][2])]
    tails.append(jnp.dot(swap, blocks[2][2], preferred_element_type=F32))

    for row in range(ROWS):
        lhs = jnp.concatenate(
            [jnp.concatenate([heads[at][row & 1], tails[at]], axis=1).astype(BF16) for at in range(3)], axis=0
        )
        hidden = jnp.dot(lhs, in_pack_ref[row], preferred_element_type=F32)
        for at in range(3):
            i = 4 * at + row
            h0[i] = (hidden[256 * at : 256 * at + 256] + bias * gates[at]).astype(BF16)
            if 2 <= i < 10:
                head, tail = heads[at][row & 1][32:224], tails[at][32:224]
                if row >= 2:
                    head = pltpu.roll(head, 64, 1)
                if row != 2:
                    tail = pltpu.roll(tail, (64 - 32 * row) % 128, 1)
                value = jnp.where(lane < 64, head, jnp.where(lane < C, tail, 0.0))
                x1[i - 2] = (value.reshape(12, SLOTS, 128) * coef_ref[1][None]).reshape(192, 128)

    for top in (0, 5):
        response = convolve(h0, top, 5, 224, conv_ref[0])
        for at in range(5):
            gate = gate_of(top + at - 3)
            hidden = film(response[224 * at : 224 * at + 224], film_ref[0] * gate, film_ref[1] * gate)
            h1[top + at] = hidden.astype(BF16)

    for top in (0, 4):
        response = convolve(h1, top, 4, 192, conv_ref[1])
        hidden = h1[top + 1 : top + 5, 16:208, :].reshape(768, HID).astype(F32)
        hidden = hidden + film(response, film_ref[2], film_ref[3])
        network = jnp.dot(hidden.astype(BF16), out_t_ref[...], preferred_element_type=F32)
        x = x1[top : top + 4].reshape(48, SLOTS, 128)
        anchor = jnp.where(first, x, 0.0)
        drift = coef_ref[2][None] * x - coef_ref[3][None] * network.reshape(48, SLOTS, 128) + anchor
        drift = drift.reshape(768, 128)
        earlier = []
        for pair in range(3):
            rhs = [halves(drift[256 * pair + 128 * k : 256 * pair + 128 * k + 128]) for k in range(2)]
            both = jnp.dot(before_ref[...], jnp.concatenate(rhs, axis=1), preferred_element_type=F32)
            earlier += [both[:, :128], both[:, 128:]]
        state = jnp.concatenate(earlier, axis=0).reshape(48, SLOTS, 128) + anchor
        scaled = []
        for at in range(4):
            i = top + at
            here = state[12 * at : 12 * at + 12]
            if 2 <= i < 6:
                s2[i - 2] = here[2:10].reshape(128, 128)
            scaled.append((here * (coef_ref[0] * gate_of(i - 2))[None]).reshape(192, 128).astype(BF16))
        hidden = jnp.dot(jnp.concatenate(scaled, axis=0), in_t_ref[...], preferred_element_type=F32)
        for at in range(4):
            g0[top + at] = (hidden[192 * at : 192 * at + 192] + bias * gate_of(top + at - 2)).astype(BF16)

    for top in (0, 3):
        response = convolve(g0, top, 3, 160, conv_ref[0])
        for at in range(3):
            gate = gate_of(top + at - 1)
            hidden = film(response[160 * at : 160 * at + 160], film_ref[0] * gate, film_ref[1] * gate)
            g1[top + at] = hidden.astype(BF16)

    response = convolve(g1, 0, 4, 128, conv_ref[1])
    hidden = g1[1:5, 16:144, :].reshape(512, HID).astype(F32)
    hidden = hidden + film(response, film_ref[2], film_ref[3])
    network = jnp.dot(hidden.astype(BF16), out_t_ref[...], preferred_element_type=F32)
    state = s2[...].reshape(32, SLOTS, 128)
    anchor = jnp.where(first, state, 0.0)
    drift = coef_ref[2][None] * state - coef_ref[3][None] * network.reshape(32, SLOTS, 128) + anchor
    drift = drift.reshape(512, 128)
    done = []
    for pair in range(2):
        rhs = [halves(drift[256 * pair + 128 * k : 256 * pair + 128 * k + 128]) for k in range(2)]
        both = jnp.dot(gather_ref[...], jnp.concatenate(rhs, axis=1), preferred_element_type=F32)
        done += [both[:, :128], both[:, 128:]]
    tail = pltpu.roll(done[0], 64, 1)
    for row in range(1, ROWS):
        here = done[row] if row == 2 else pltpu.roll(done[row], (32 * row - 64) % 128, 1)
        tail = jnp.where(lane < 32 * row, tail, here)
    for half in range(2):
        head = jnp.where(lane < 64, done[half], pltpu.roll(done[half + 2], 64, 1))
        o_ref[:, COLS * half : COLS * half + COLS, :] = head.reshape(SLOTS, COLS, 128).astype(BF16)
    o_ref[:, 2 * COLS :, :] = tail.reshape(SLOTS, COLS, 128).astype(BF16)


def main(low, own, high, prepared):
    return pl.pallas_call(
        main_kernel,
        out_shape=jax.ShapeDtypeStruct((SLOTS, BACK, 128), BF16),
        in_specs=[pl.BlockSpec(memory_space=VMEM)] * 13,
        out_specs=pl.BlockSpec(memory_space=VMEM),
        scratch_shapes=[
            VMEM((12, 256, HID), BF16),
            VMEM((10, 224, HID), BF16),
            VMEM((8, 192, HID), BF16),
            VMEM((6, 160, HID), BF16),
            VMEM((8, 192, 128), F32),
            VMEM((ROWS, 128, 128), F32),
        ],
        name="patch",
        compiler_params=pltpu.CompilerParams(vmem_limit_bytes=32 << 20),
    )(low, own, high, *prepared)


def unpack_kernel(p_ref, o_ref):
    pieces = p_ref[...].astype(F32)

    def turned(group):
        return pieces[:, COLS * group : COLS * group + COLS, :].reshape(128, 128).T

    heads, tail = [turned(0), turned(1)], turned(2)
    for row in range(ROWS):
        start = 64 if row >= 2 else 0
        o_ref[pl.ds(row, 64, stride=ROWS), :] = heads[row & 1][start : start + 64]
        o_ref[pl.ds(64 * ROWS + row, C - 64, stride=ROWS), :] = tail[32 * row : 32 * row + C - 64]


def unpack(pieces):
    return pl.pallas_call(
        unpack_kernel,
        out_shape=jax.ShapeDtypeStruct((C * ROWS, 128), F32),
        in_specs=[pl.BlockSpec(memory_space=VMEM)],
        out_specs=pl.BlockSpec(memory_space=VMEM),
        name="unpack",
        compiler_params=pltpu.CompilerParams(vmem_limit_bytes=8 << 20),
    )(pieces)


def on_device(trajectory, step_levels, in_weight, in_bias, conv_weight, cond_weight, out_weight):
    count = lax.axis_size("lat")
    forward = [(i, i + 1) for i in range(count - 1)]
    backward = [(b, a) for a, b in forward]
    pieces = pack(step_levels, trajectory.reshape(C * ROWS, 128))
    own = lax.all_to_all(pieces, "tm", 0, 0)
    prepared = tables(step_levels, in_weight.T, in_bias[None, :], cond_weight, out_weight, conv_weight)
    own, prepared = lax.optimization_barrier((own, prepared))
    low = lax.ppermute(own, "lat", forward)
    high = lax.ppermute(own, "lat", backward)
    done = main(low, own, high, prepared)
    back = lax.all_to_all(done, "tm", 0, 0)
    return unpack(back).reshape(1, C, ROWS, 128)


def solution(mesh):
    in_specs = (P("tm", None, "lat", None), P(), P(), P(), P(), P(), P())
    out_specs = P("tm", None, "lat", None)
    return jax.shard_map(on_device, mesh=mesh, in_specs=in_specs, out_specs=out_specs, check_vma=False)
```

time: 80.7 us -> 65.8 us (0.82)
  Pallas kernels: 30.9 us -> 13.9 us
  local copies, waits for them, and re-layouts: 4.34 us -> 8.55 us
  waiting for transfers between devices: 12.7 us -> 11.4 us
  blocking collectives: 14.1 us -> 13.1 us
    pallas_call x1, Pallas kernels: 24.9 us -> 10.4 us  [main(): pl.pallas_call(main_kernel, out_shape=jax.ShapeDtypeStruct((SLOTS, BACK,...]
    unnamed x7 -> x20, local copies, waits for them, and re-layouts: 2.21 us -> 8.55 us
    all_to_all x1, waiting for transfers between devices: 8.68 us -> 2.9 us  [on_device(): own = lax.all_to_all(pieces, 'tm', 0, 0)]
    ppermute x1, waiting for transfers between devices: 0.01 us -> 2.53 us  [on_device(): high = lax.ppermute(own, 'lat', backward)]
    ppermute x1, waiting for transfers between devices: 3.99 us -> 5.95 us  [on_device(): low = lax.ppermute(own, 'lat', forward)]
    broadcast_in_dim x2 -> x0, local copies, waits for them, and re-layouts: 1.33 us -> none  [the longest x1 0.66 us: on_device(): now = jnp.broadcast_to(step_levels[:-1, None], (SLOTS, 128))]
    pallas_call x1, Pallas kernels: 2.35 us -> 1.06 us  [tables(): pl.pallas_call(tables_kernel, out_shape=[jax.ShapeDtypeStruct((4, SLOTS,...]
    all_to_all x1, blocking collectives: 14.1 us -> 13.1 us  [on_device(): back = lax.all_to_all(done, 'tm', 0, 0)]
  transfers between devices with their start and end apart: 3 -> 3, of which waited for: 2 -> 3; matrix products, arithmetic and copies ran while one was open for 5% -> 0% of each run, Pallas kernels for 3% -> 2%
where the time goes in v2:
time: 65.8 us; the launch traced here: 65.2 us
  starting transfers between devices  18.3 us (28%)
  Pallas kernels  13.9 us (21%)
  blocking collectives  13.1 us (20%)
  waiting for transfers between devices  11.4 us (17%)
  local copies, waits for them, and re-layouts  8.55 us (13%)
    all_to_all x1, blocking collectives, on_device(): back = lax.all_to_all(done, 'tm', 0, 0)  13.1 us
    all_to_all x1, starting transfers between devices, on_device(): own = lax.all_to_all(pieces, 'tm', 0, 0)  11 us
    pallas_call x1, Pallas kernels, main(): pl.pallas_call(main_kernel, out_shape=jax.ShapeDtypeStruct((SLOTS, BACK,...  10.4 us
    unnamed x20, local copies, waits for them, and re-layouts  8.55 us
    ppermute x1, waiting for transfers between devices, on_device(): low = lax.ppermute(own, 'lat', forward)  5.95 us
    ppermute x1, starting transfers between devices, on_device(): high = lax.ppermute(own, 'lat', backward)  5.35 us
    all_to_all x1, waiting for transfers between devices, on_device(): own = lax.all_to_all(pieces, 'tm', 0, 0)  2.9 us
    ppermute x1, waiting for transfers between devices, on_device(): high = lax.ppermute(own, 'lat', backward)  2.53 us
  transfers between devices with their start and end apart: 3, of which 3 were waited for; matrix products, arithmetic and copies ran while one was open for 0% of the time, Pallas kernels for 2%

profile of v2, /device:TPU:7, one launch (start us, length us, event | category | flops | bytes accessed | tf_op | source)
XLA Modules:
  0.0 65.2 jit_solution(10853115036993994598)
XLA Ops:
  0.0 0.0 copy-start.2
  0.0 0.9 %copy-done.2 = f32[1,84,4,128]{3,2,1,0:T(4,128)S(1)} copy-done((f32[1,84,4,128]{3,2,1,0:T(4,128)S(1)}, f32[1,84,4,128]{3,2,1,0:T(4,128)}, u32[]{:S(2)}) %copy-start.2) | copy-done | bytes 172056
  0.9 0.0 copy-start.7
  0.9 0.7 %copy-done.7 = s32[17]{0:T(128)S(1)} copy-done((s32[17]{0:T(128)S(1)}, s32[17]{0:T(128)}, u32[]{:S(2)}) %copy-start.7) | copy-done | bytes 92
  1.6 1.6 %pack.1 = bf16[16,48,128]{2,1,0:T(8,128)(2,1)} custom-call(s32[17]{0:T(128)S(1)} %copy-done.7, f32[336,128]{1,0:T(8,128)S(1)} %bitcast.4), custom_call_target="tpu_custom_call" | custom-call | tf_op jit(solution)/shard_map/pack/pallas_call | solution.py:82
  3.2 11.0 %all-to-all-start = ((bf16[16,48,128]{2,1,0:T(8,128)(2,1)}), bf16[16,48,128]{2,1,0:T(8,128)(2,1)S(1)}, u32[]{:S(2)}, u32[]{:S(2)}) async-start(bf16[16,48,128]{2,1,0:T(8,128)(2,1)} %pack.1), calls=%async_computation | async-start | bytes 393216 | tf_op jit(solution)/shard_map/all_to_all | solution.py:355
  14.2 0.0 copy-start
  14.2 1.7 %copy-done = bf16[2,256,2304]{2,1,0:T(8,128)(2,1)S(1)} copy-done((bf16[2,256,2304]{2,1,0:T(8,128)(2,1)S(1)}, bf16[2,256,2304]{2,1,0:T(8,128)(2,1)}, u32[]{:S(2)}) %copy-start) | copy-done | bytes 2359320
  15.9 0.0 copy-start.1
  15.9 1.0 %copy-done.1 = bf16[256,1024]{1,0:T(8,128)(2,1)S(1)} copy-done((bf16[256,1024]{1,0:T(8,128)(2,1)S(1)}, bf16[256,1024]{1,0:T(8,128)(2,1)}, u32[]{:S(2)}) %copy-start.1) | copy-done | bytes 524312
  16.9 0.0 copy-start.3
  16.9 0.8 %copy-done.3 = bf16[256,84]{0,1:T(8,128)(2,1)S(1)} copy-done((bf16[256,84]{0,1:T(8,128)(2,1)S(1)}, bf16[256,84]{0,1:T(8,128)(2,1)}, u32[]{:S(2)}) %copy-start.3) | copy-done | bytes 43032
  17.7 0.0 copy-start.4
  17.7 0.8 %copy-done.4 = bf16[84,256]{1,0:T(8,128)(2,1)S(1)} copy-done((bf16[84,256]{1,0:T(8,128)(2,1)S(1)}, bf16[84,256]{1,0:T(8,128)(2,1)}, u32[]{:S(2)}) %copy-start.4) | copy-done | bytes 43032
  18.5 0.0 copy-start.8
  18.5 0.7 %copy-done.8 = s32[17]{0:T(128)S(1)} copy-done((s32[17]{0:T(128)S(1)}, s32[17]{0:T(128)}, u32[]{:S(2)}) %copy-start.8) | copy-done | bytes 92
  19.1 0.0 copy-start.9
  19.1 0.7 %copy-done.9 = f32[256]{0:T(256)S(1)} copy-done((f32[256]{0:T(256)S(1)}, f32[256]{0:T(256)}, u32[]{:S(2)}) %copy-start.9) | copy-done | bytes 1048
  19.8 1.1 %tables.1 = (f32[4,16,256]{2,1,0:T(8,128)S(1)}, f32[4,16,128]{2,1,0:T(8,128)S(1)}, bf16[4,256,256]{2,1,0:T(8,128)(2,1)S(1)}, bf16[128,256]{1,0:T(8,128)(2,1)S(1)...) custom-call(s32[17]{0:T(128)S(1)} %copy-done.8, ...), custom_call_target="tpu_custom_call" | custom-call | tf_op jit(solution)/shard_map/tables/pallas_call | solution.py:147
  20.9 0.0 copy-start.5
  20.9 0.6 copy-done.5
  21.5 2.9 %all-to-all-done.own_ref = bf16[16,48,128]{2,1,0:T(8,128)(2,1)S(1)} async-done(((bf16[16,48,128]{2,1,0:T(8,128)(2,1)}), bf16[16,48,128]{2,1,0:T(8,128)(2,1)S(1)}, u32[]{:S(2)}, u32[]{:S(2)}) %all-to-all-start) | async-done | bytes 196640 | tf_op jit(solution)/shard_map/all_to_all | solution.py:355
  24.4 5.3 %collective-permute-start.1 = (bf16[16,48,128]{2,1,0:T(8,128)(2,1)S(1)}, bf16[16,48,128]{2,1,0:T(8,128)(2,1)S(1)}, u32[]{:S(2)}, u32[]{:S(2)}) collective-permute-start(bf16[16,48,128]{2,1,0:T(8,128)(2,1)S(1)} %all-to-all-done.own_ref), channel_id=1, source_target_pairs={{1,0},{2,1},{3,2},{4,3},{5,4},{6,5},{7,6},{8,7},{9,8},{10,9},{11,1... | collective-permute-start | bytes 589832 | tf_op jit(solution)/shard_map/ppermute | solution.py:359
  29.8 1.9 %collective-permute-start = (bf16[16,48,128]{2,1,0:T(8,128)(2,1)S(1)}, bf16[16,48,128]{2,1,0:T(8,128)(2,1)S(1)}, u32[]{:S(2)}, u32[]{:S(2)}) collective-permute-start(bf16[16,48,128]{2,1,0:T(8,128)(2,1)S(1)} %all-to-all-done.own_ref), channel_id=1, source_target_pairs={{0,1},{1,2},{2,3},{3,4},{4,5},{5,6},{6,7},{7,8},{8,9},{9,10},{10,1... | collective-permute-start | bytes 589832 | tf_op jit(solution)/shard_map/ppermute | solution.py:358
  31.7 2.5 %collective-permute-done.1.high_ref = bf16[16,48,128]{2,1,0:T(8,128)(2,1)S(1)} collective-permute-done((bf16[16,48,128]{2,1,0:T(8,128)(2,1)S(1)}, bf16[16,48,128]{2,1,0:T(8,128)(2,1)S(1)}, u32[]{:S(2)}, u32[]{:S(2)}) %collective-permute-start.1) | collective-permute-done | bytes 196640 | tf_op jit(solution)/shard_map/ppermute | solution.py:359
  34.2 5.9 %collective-permute-done.low_ref = bf16[16,48,128]{2,1,0:T(8,128)(2,1)S(1)} collective-permute-done((bf16[16,48,128]{2,1,0:T(8,128)(2,1)S(1)}, bf16[16,48,128]{2,1,0:T(8,128)(2,1)S(1)}, u32[]{:S(2)}, u32[]{:S(2)}) %collective-permute-start) | collective-permute-done | bytes 196640 | tf_op jit(solution)/shard_map/ppermute | solution.py:358
  40.2 0.0 copy-start.6
  40.2 0.8 %copy-done.6 = f32[4,16,128]{2,1,0:T(8,128)S(1)} copy-done((f32[4,16,128]{2,1,0:T(8,128)S(1)}, f32[4,16,128]{2,1,0:T(8,128)}, u32[]{:S(2)}) %copy-start.6) | copy-done | bytes 32792
  40.9 10.4 %patch.1 = bf16[16,24,128]{2,1,0:T(8,128)(2,1)S(1)} custom-call(bf16[16,48,128]{2,1,0:T(8,128)(2,1)S(1)} %collective-permute-done.low_ref, bf16[16,48,128]{2,1,0:T(8,128)(2,1)S(1)} %all-to-all-done.own_ref, bf16[16,48,128]{2,1,0:T(8,128)(2,1)S(1)} %collective-permute-done.1.high_ref, f32[4,16,256]{2,1,0:T(8,128)S(1)} %get-tuple-element.37.film_ref, ...), custom_call_target="tpu_custom_call" | custom-call | tf_op jit(solution)/shard_map/patch/pallas_call | solution.py:308
  51.4 13.1 %all_to_all.10.p_ref = bf16[16,24,128]{2,1,0:T(8,128)(2,1)S(1)} all-to-all(bf16[16,24,128]{2,1,0:T(8,128)(2,1)S(1)} %patch.1), channel_id=1, replica_groups=mesh['tm'=16,'lat'=32] {'tm'}, dimensions={0} | all-to-all | bytes 196608 | tf_op jit(solution)/shard_map/all_to_all | solution.py:361
  64.5 0.8 %unpack.1 = f32[336,128]{1,0:T(8,128)} custom-call(bf16[16,24,128]{2,1,0:T(8,128)(2,1)S(1)} %all_to_all.10.p_ref), custom_call_target="tpu_custom_call" | custom-call | tf_op jit(solution)/shard_map/unpack/pallas_call | solution.py:340
Async XLA Ops:
  0.0 0.9 %copy-start.2 = (f32[1,84,4,128]{3,2,1,0:T(4,128)S(1)}, f32[1,84,4,128]{3,2,1,0:T(4,128)}, u32[]{:S(2)}) copy-start(f32[1,84,4,128]{3,2,1,0:T(4,128)} %param.7) | copy-start | bytes 516100
  0.9 0.7 %copy-start.7 = (s32[17]{0:T(128)S(1)}, s32[17]{0:T(128)}, u32[]{:S(2)}) copy-start(s32[17]{0:T(128)} %levels_hbm.3) | copy-start | bytes 208
  3.2 21.2 %all-to-all-start = ((bf16[16,48,128]{2,1,0:T(8,128)(2,1)}), bf16[16,48,128]{2,1,0:T(8,128)(2,1)S(1)}, u32[]{:S(2)}, u32[]{:S(2)}) async-start(bf16[16,48,128]{2,1,0:T(8,128)(2,1)} %pack.1), calls=%async_computation | async-start | bytes 393216 | tf_op jit(solution)/shard_map/all_to_all | solution.py:355
  14.2 1.7 %copy-start = (bf16[2,256,2304]{2,1,0:T(8,128)(2,1)S(1)}, bf16[2,256,2304]{2,1,0:T(8,128)(2,1)}, u32[]{:S(2)}) copy-start(bf16[2,256,2304]{2,1,0:T(8,128)(2,1)} %conv_hbm.1) | copy-start | bytes 7077892
  15.9 1.0 %copy-start.1 = (bf16[256,1024]{1,0:T(8,128)(2,1)S(1)}, bf16[256,1024]{1,0:T(8,128)(2,1)}, u32[]{:S(2)}) copy-start(bf16[256,1024]{1,0:T(8,128)(2,1)} %cond_hbm.1) | copy-start | bytes 1572868
  16.9 0.8 %copy-start.3 = (bf16[256,84]{0,1:T(8,128)(2,1)S(1)}, bf16[256,84]{0,1:T(8,128)(2,1)}, u32[]{:S(2)}) copy-start(bf16[256,84]{0,1:T(8,128)(2,1)} %param.9) | copy-start | bytes 129028
  17.7 0.8 %copy-start.4 = (bf16[84,256]{1,0:T(8,128)(2,1)S(1)}, bf16[84,256]{1,0:T(8,128)(2,1)}, u32[]{:S(2)}) copy-start(bf16[84,256]{1,0:T(8,128)(2,1)} %out_w_hbm.1) | copy-start | bytes 129028
  18.5 0.7 %copy-start.8 = (s32[17]{0:T(128)S(1)}, s32[17]{0:T(128)}, u32[]{:S(2)}) copy-start(s32[17]{0:T(128)} %levels_hbm.3) | copy-start | bytes 208
  19.1 0.7 %copy-start.9 = (f32[256]{0:T(256)S(1)}, f32[256]{0:T(256)}, u32[]{:S(2)}) copy-start(f32[256]{0:T(256)} %param.10) | copy-start | bytes 3076
  20.9 0.6 copy-start.5
  24.4 9.8 %collective-permute-start.1 = (bf16[16,48,128]{2,1,0:T(8,128)(2,1)S(1)}, bf16[16,48,128]{2,1,0:T(8,128)(2,1)S(1)}, u32[]{:S(2)}, u32[]{:S(2)}) collective-permute-start(bf16[16,48,128]{2,1,0:T(8,128)(2,1)S(1)} %all-to-all-done.own_ref), channel_id=1, source_target_pairs={{1,0},{2,1},{3,2},{4,3},{5,4},{6,5},{7,6},{8,7},{9,8},{10,9},{11,1... | collective-permute-start | bytes 589832 | tf_op jit(solution)/shard_map/ppermute | solution.py:359
  29.8 10.4 %collective-permute-start = (bf16[16,48,128]{2,1,0:T(8,128)(2,1)S(1)}, bf16[16,48,128]{2,1,0:T(8,128)(2,1)S(1)}, u32[]{:S(2)}, u32[]{:S(2)}) collective-permute-start(bf16[16,48,128]{2,1,0:T(8,128)(2,1)S(1)} %all-to-all-done.own_ref), channel_id=1, source_target_pairs={{0,1},{1,2},{2,3},{3,4},{4,5},{5,6},{6,7},{7,8},{8,9},{9,10},{10,1... | collective-permute-start | bytes 589832 | tf_op jit(solution)/shard_map/ppermute | solution.py:358
  40.2 0.8 %copy-start.6 = (f32[4,16,128]{2,1,0:T(8,128)S(1)}, f32[4,16,128]{2,1,0:T(8,128)}, u32[]{:S(2)}) copy-start(f32[4,16,128]{2,1,0:T(8,128)} %copy-done.5) | copy-start | bytes 98308

commit v3 on v2

--- a/solution.py
+++ b/solution.py
@@ -90,11 +90,11 @@
             pltpu.SemaphoreType.DMA((2,)),
         ],
         name="pack",
-        compiler_params=pltpu.CompilerParams(vmem_limit_bytes=12 << 20),
+        compiler_params=pltpu.CompilerParams(vmem_limit_bytes=60 * 1024 * 1024),
     )(levels, x)
 
 
-def tables_kernel(levels_hbm, in_w_hbm, bias_hbm, cond_hbm, out_w_hbm, conv_hbm, film_ref, coef_ref, in_pack_ref, in_t_ref, out_t_ref, bias_ref, conv_ref, swap_ref, before_ref, gather_ref, levels_ref, in_w_ref, cond_ref, out_w_ref, sems):
+def tables_kernel(levels_hbm, in_w_hbm, bias_hbm, cond_hbm, out_w_hbm, conv_hbm, film_ref, in_pack_ref, in_t_ref, out_t_ref, bias_ref, conv_ref, swap_ref, before_ref, gather_ref, levels_ref, in_w_ref, cond_ref, out_w_ref, sems):
     sources = (levels_hbm, in_w_hbm, cond_hbm, out_w_hbm, bias_hbm, conv_hbm)
     targets = (levels_ref, in_w_ref, cond_ref, out_w_ref, bias_ref, conv_ref)
     copies = [pltpu.make_async_copy(a, b, sems.at[i]) for i, (a, b) in enumerate(zip(sources, targets))]
@@ -116,10 +116,10 @@
     variance = now * now + 0.25
     root = jnp.sqrt(variance)
     ratio = (following - now) / now
-    coef_ref[0] = 1.0 / root
-    coef_ref[1] = root
-    coef_ref[2] = (1.0 - 0.25 / variance) * ratio
-    coef_ref[3] = 0.5 * now / root * ratio
+    film_ref[4, :, :128] = 1.0 / root
+    film_ref[4, :, 128:] = root
+    film_ref[5, :, :128] = (1.0 - 0.25 / variance) * ratio
+    film_ref[5, :, 128:] = 0.5 * now / root * ratio
     j = iota((SLOTS, 128), 1).astype(F32)
     frequency = jnp.exp(j * (jnp.log(F32(100.0)) / 128.0))
     phases = jnp.log(now) / 4.0 * frequency
@@ -147,8 +147,7 @@
     return pl.pallas_call(
         tables_kernel,
         out_shape=[
-            jax.ShapeDtypeStruct((4, SLOTS, HID), F32),
-            jax.ShapeDtypeStruct((4, SLOTS, 128), F32),
+            jax.ShapeDtypeStruct((6, SLOTS, HID), F32),
             jax.ShapeDtypeStruct((ROWS, 256, HID), BF16),
             jax.ShapeDtypeStruct((128, HID), BF16),
             jax.ShapeDtypeStruct((HID, 128), BF16),
@@ -159,7 +158,7 @@
             jax.ShapeDtypeStruct((128, 256), BF16),
         ],
         in_specs=[pl.BlockSpec(memory_space=pltpu.HBM)] * 6,
-        out_specs=[pl.BlockSpec(memory_space=VMEM)] * 10,
+        out_specs=[pl.BlockSpec(memory_space=VMEM)] * 9,
         scratch_shapes=[
             pltpu.SMEM((SLOTS + 1,), jnp.int32),
             VMEM((C, HID), BF16),
@@ -168,7 +167,7 @@
             pltpu.SemaphoreType.DMA((6,)),
         ],
         name="tables",
-        compiler_params=pltpu.CompilerParams(vmem_limit_bytes=12 << 20),
+        compiler_params=pltpu.CompilerParams(vmem_limit_bytes=61400 << 10),
     )(levels, in_weight_t, in_bias, cond_weight, out_weight, conv_weight)
 
 
@@ -197,7 +196,7 @@
     return jnp.concatenate([high, low], axis=0)
 
 
-def main_kernel(low_ref, own_ref, high_ref, film_ref, coef_ref, in_pack_ref, in_t_ref, out_t_ref, bias_ref, conv_ref, swap_ref, before_ref, gather_ref, o_ref, h0, h1, g0, g1, x1, s2):
+def main_kernel(low_ref, own_ref, high_ref, film_ref, in_pack_ref, in_t_ref, out_t_ref, bias_ref, conv_ref, swap_ref, before_ref, gather_ref, o_ref, h0, h1, g0, g1, x1, s2):
     place = lax.axis_index("lat")
     count = lax.axis_size("lat")
     inside_low = jnp.where(place > 0, 1.0, 0.0).astype(F32)
@@ -239,7 +238,7 @@
                 if row != 2:
                     tail = pltpu.roll(tail, (64 - 32 * row) % 128, 1)
                 value = jnp.where(lane < 64, head, jnp.where(lane < C, tail, 0.0))
-                x1[i - 2] = (value.reshape(12, SLOTS, 128) * coef_ref[1][None]).reshape(192, 128)
+                x1[i - 2] = (value.reshape(12, SLOTS, 128) * film_ref[4, :, 128:][None]).reshape(192, 128)
 
     for top in (0, 5):
         response = convolve(h0, top, 5, 224, conv_ref[0])
@@ -255,7 +254,7 @@
         network = jnp.dot(hidden.astype(BF16), out_t_ref[...], preferred_element_type=F32)
         x = x1[top : top + 4].reshape(48, SLOTS, 128)
         anchor = jnp.where(first, x, 0.0)
-        drift = coef_ref[2][None] * x - coef_ref[3][None] * network.reshape(48, SLOTS, 128) + anchor
+        drift = film_ref[5, :, :128][None] * x - film_ref[5, :, 128:][None] * network.reshape(48, SLOTS, 128) + anchor
         drift = drift.reshape(768, 128)
         earlier = []
         for pair in range(3):
@@ -269,7 +268,7 @@
             here = state[12 * at : 12 * at + 12]
             if 2 <= i < 6:
                 s2[i - 2] = here[2:10].reshape(128, 128)
-            scaled.append((here * (coef_ref[0] * gate_of(i - 2))[None]).reshape(192, 128).astype(BF16))
+            scaled.append((here * (film_ref[4, :, :128] * gate_of(i - 2))[None]).reshape(192, 128).astype(BF16))
         hidden = jnp.dot(jnp.concatenate(scaled, axis=0), in_t_ref[...], preferred_element_type=F32)
         for at in range(4):
             g0[top + at] = (hidden[192 * at : 192 * at + 192] + bias * gate_of(top + at - 2)).astype(BF16)
@@ -287,7 +286,7 @@
     network = jnp.dot(hidden.astype(BF16), out_t_ref[...], preferred_element_type=F32)
     state = s2[...].reshape(32, SLOTS, 128)
     anchor = jnp.where(first, state, 0.0)
-    drift = coef_ref[2][None] * state - coef_ref[3][None] * network.reshape(32, SLOTS, 128) + anchor
+    drift = film_ref[5, :, :128][None] * state - film_ref[5, :, 128:][None] * network.reshape(32, SLOTS, 128) + anchor
     drift = drift.reshape(512, 128)
     done = []
     for pair in range(2):
@@ -308,7 +307,7 @@
     return pl.pallas_call(
         main_kernel,
         out_shape=jax.ShapeDtypeStruct((SLOTS, BACK, 128), BF16),
-        in_specs=[pl.BlockSpec(memory_space=VMEM)] * 13,
+        in_specs=[pl.BlockSpec(memory_space=VMEM)] * 12,
         out_specs=pl.BlockSpec(memory_space=VMEM),
         scratch_shapes=[
             VMEM((12, 256, HID), BF16),

time: 65.8 us -> 71.2 us (1.082)
  waiting for transfers between devices: 11.4 us -> 15 us
  Pallas kernels: 13.9 us -> 16.8 us
  blocking collectives: 13.1 us -> 11.8 us
    all_to_all x1, waiting for transfers between devices: 2.9 us -> 6.54 us  [on_device(): own = lax.all_to_all(pieces, 'tm', 0, 0)]
    pallas_call x1, Pallas kernels: 1.06 us -> 3.66 us  [tables(): pl.pallas_call(tables_kernel, out_shape=[jax.ShapeDtypeStruct((6, SLOTS,...]
    all_to_all x1, blocking collectives: 13.1 us -> 11.8 us  [on_device(): back = lax.all_to_all(done, 'tm', 0, 0)]
    unnamed x20 -> x18, local copies, waits for them, and re-layouts: 8.55 us -> 8.53 us
  transfers between devices with their start and end apart: 3 -> 3, of which waited for: 3 -> 3; matrix products, arithmetic and copies ran while one was open for 0% -> 0% of each run, Pallas kernels for 2% -> 5%
where the time goes in v3:
time: 71.2 us; the launch traced here: 70.5 us
  starting transfers between devices  18.3 us (26%)
  Pallas kernels  16.8 us (24%)
  waiting for transfers between devices  15 us (21%)
  blocking collectives  11.8 us (17%)
  local copies, waits for them, and re-layouts  8.53 us (12%)
    all_to_all x1, blocking collectives, on_device(): back = lax.all_to_all(done, 'tm', 0, 0)  11.8 us
    all_to_all x1, starting transfers between devices, on_device(): own = lax.all_to_all(pieces, 'tm', 0, 0)  11 us
    pallas_call x1, Pallas kernels, main(): pl.pallas_call(main_kernel, out_shape=jax.ShapeDtypeStruct((SLOTS, BACK,...  10.5 us
    unnamed x18, local copies, waits for them, and re-layouts  8.53 us
    all_to_all x1, waiting for transfers between devices, on_device(): own = lax.all_to_all(pieces, 'tm', 0, 0)  6.54 us
    ppermute x1, waiting for transfers between devices, on_device(): low = lax.ppermute(own, 'lat', forward)  5.95 us
    ppermute x1, starting transfers between devices, on_device(): high = lax.ppermute(own, 'lat', backward)  5.36 us
    pallas_call x1, Pallas kernels, tables(): pl.pallas_call(tables_kernel, out_shape=[jax.ShapeDtypeStruct((6, SLOTS,...  3.66 us
  transfers between devices with their start and end apart: 3, of which 3 were waited for; matrix products, arithmetic and copies ran while one was open for 0% of the time, Pallas kernels for 5%

profile of v3, /device:TPU:7, one launch (start us, length us, event | category | flops | bytes accessed | tf_op | source)
XLA Modules:
  0.0 70.5 jit_solution(2662513086433986894)
XLA Ops:
  0.0 2.0 %pack.1 = bf16[16,48,128]{2,1,0:T(8,128)(2,1)} custom-call(s32[17]{0:T(128)} %levels_hbm.3, f32[336,128]{1,0:T(8,128)} %bitcast.4), custom_call_target="tpu_custom_call" | custom-call | tf_op jit(solution)/shard_map/pack/pallas_call | solution.py:82
  2.0 11.0 %all-to-all-start = ((bf16[16,48,128]{2,1,0:T(8,128)(2,1)}), bf16[16,48,128]{2,1,0:T(8,128)(2,1)S(1)}, u32[]{:S(2)}, u32[]{:S(2)}) async-start(bf16[16,48,128]{2,1,0:T(8,128)(2,1)} %pack.1), calls=%async_computation | async-start | bytes 393216 | tf_op jit(solution)/shard_map/all_to_all | solution.py:354
  13.0 3.7 %tables.1 = (f32[6,16,256]{2,1,0:T(8,128)}, bf16[4,256,256]{2,1,0:T(8,128)(2,1)}, bf16[128,256]{1,0:T(8,128)(2,1)}, bf16[256,128]{1,0:T(8,128)(2,1)}, f32[1,256]...) custom-call(s32[17]{0:T(128)} %levels_hbm.3, ...), custom_call_target="tpu_custom_call" | custom-call | tf_op jit(solution)/shard_map/tables/pallas_call | solution.py:147
  16.6 6.5 %all-to-all-done.own_ref = bf16[16,48,128]{2,1,0:T(8,128)(2,1)S(1)} async-done(((bf16[16,48,128]{2,1,0:T(8,128)(2,1)}), bf16[16,48,128]{2,1,0:T(8,128)(2,1)S(1)}, u32[]{:S(2)}, u32[]{:S(2)}) %all-to-all-start) | async-done | bytes 196640 | tf_op jit(solution)/shard_map/all_to_all | solution.py:354
  23.2 5.4 %collective-permute-start.1 = (bf16[16,48,128]{2,1,0:T(8,128)(2,1)S(1)}, bf16[16,48,128]{2,1,0:T(8,128)(2,1)S(1)}, u32[]{:S(2)}, u32[]{:S(2)}) collective-permute-start(bf16[16,48,128]{2,1,0:T(8,128)(2,1)S(1)} %all-to-all-done.own_ref), channel_id=1, source_target_pairs={{1,0},{2,1},{3,2},{4,3},{5,4},{6,5},{7,6},{8,7},{9,8},{10,9},{11,1... | collective-permute-start | bytes 589832 | tf_op jit(solution)/shard_map/ppermute | solution.py:358
  28.5 1.9 %collective-permute-start = (bf16[16,48,128]{2,1,0:T(8,128)(2,1)S(1)}, bf16[16,48,128]{2,1,0:T(8,128)(2,1)S(1)}, u32[]{:S(2)}, u32[]{:S(2)}) collective-permute-start(bf16[16,48,128]{2,1,0:T(8,128)(2,1)S(1)} %all-to-all-done.own_ref), channel_id=1, source_target_pairs={{0,1},{1,2},{2,3},{3,4},{4,5},{5,6},{6,7},{7,8},{8,9},{9,10},{10,1... | collective-permute-start | bytes 589832 | tf_op jit(solution)/shard_map/ppermute | solution.py:357
  30.5 2.5 %collective-permute-done.1.high_ref = bf16[16,48,128]{2,1,0:T(8,128)(2,1)S(1)} collective-permute-done((bf16[16,48,128]{2,1,0:T(8,128)(2,1)S(1)}, bf16[16,48,128]{2,1,0:T(8,128)(2,1)S(1)}, u32[]{:S(2)}, u32[]{:S(2)}) %collective-permute-start.1) | collective-permute-done | bytes 196640 | tf_op jit(solution)/shard_map/ppermute | solution.py:358
  33.0 5.9 %collective-permute-done.low_ref = bf16[16,48,128]{2,1,0:T(8,128)(2,1)S(1)} collective-permute-done((bf16[16,48,128]{2,1,0:T(8,128)(2,1)S(1)}, bf16[16,48,128]{2,1,0:T(8,128)(2,1)S(1)}, u32[]{:S(2)}, u32[]{:S(2)}) %collective-permute-start) | collective-permute-done | bytes 196640 | tf_op jit(solution)/shard_map/ppermute | solution.py:357
  39.0 0.0 copy-start
  39.0 1.7 %copy-done = bf16[2,256,2304]{2,1,0:T(8,128)(2,1)S(1)} copy-done((bf16[2,256,2304]{2,1,0:T(8,128)(2,1)S(1)}, bf16[2,256,2304]{2,1,0:T(8,128)(2,1)}, u32[]{:S(2)}) %copy-start) | copy-done | bytes 2359320
  40.6 0.0 copy-start.1
  40.6 1.0 %copy-done.1 = bf16[4,256,256]{2,1,0:T(8,128)(2,1)S(1)} copy-done((bf16[4,256,256]{2,1,0:T(8,128)(2,1)S(1)}, bf16[4,256,256]{2,1,0:T(8,128)(2,1)}, u32[]{:S(2)}) %copy-start.1) | copy-done | bytes 524312
  41.7 0.0 copy-start.2
  41.7 0.9 %copy-done.2 = bf16[256,256]{1,0:T(8,128)(2,1)S(1)} copy-done((bf16[256,256]{1,0:T(8,128)(2,1)S(1)}, bf16[256,256]{1,0:T(8,128)(2,1)}, u32[]{:S(2)}) %copy-start.2) | copy-done | bytes 131096
  42.6 0.0 copy-start.3
  42.6 0.9 %copy-done.3 = f32[6,16,256]{2,1,0:T(8,128)S(1)} copy-done((f32[6,16,256]{2,1,0:T(8,128)S(1)}, f32[6,16,256]{2,1,0:T(8,128)}, u32[]{:S(2)}) %copy-start.3) | copy-done | bytes 98328
  43.5 0.0 copy-start.4
  43.5 0.8 %copy-done.4 = bf16[128,256]{1,0:T(8,128)(2,1)S(1)} copy-done((bf16[128,256]{1,0:T(8,128)(2,1)S(1)}, bf16[128,256]{1,0:T(8,128)(2,1)}, u32[]{:S(2)}) %copy-start.4) | copy-done | bytes 65560
  44.3 0.0 copy-start.5
  44.3 0.8 %copy-done.5 = bf16[256,128]{1,0:T(8,128)(2,1)S(1)} copy-done((bf16[256,128]{1,0:T(8,128)(2,1)S(1)}, bf16[256,128]{1,0:T(8,128)(2,1)}, u32[]{:S(2)}) %copy-start.5) | copy-done | bytes 65560
  45.1 0.0 copy-start.6
  45.1 0.8 %copy-done.6 = bf16[128,256]{1,0:T(8,128)(2,1)S(1)} copy-done((bf16[128,256]{1,0:T(8,128)(2,1)S(1)}, bf16[128,256]{1,0:T(8,128)(2,1)}, u32[]{:S(2)}) %copy-start.6) | copy-done | bytes 65560
  46.0 0.0 copy-start.7
  46.0 0.8 %copy-done.7 = bf16[128,256]{1,0:T(8,128)(2,1)S(1)} copy-done((bf16[128,256]{1,0:T(8,128)(2,1)S(1)}, bf16[128,256]{1,0:T(8,128)(2,1)}, u32[]{:S(2)}) %copy-start.7) | copy-done | bytes 65560
  46.8 0.0 copy-start.8
  46.8 0.7 copy-done.8
  47.5 10.5 %patch.1 = bf16[16,24,128]{2,1,0:T(8,128)(2,1)S(1)} custom-call(bf16[16,48,128]{2,1,0:T(8,128)(2,1)S(1)} %collective-permute-done.low_ref, bf16[16,48,128]{2,1,0:T(8,128)(2,1)S(1)} %all-to-all-done.own_ref, bf16[16,48,128]{2,1,0:T(8,128)(2,1)S(1)} %collective-permute-done.1.high_ref, f32[6,16,256]{2,1,0:T(8,128)S(1)} %copy-done.3, ...), custom_call_target="tpu_custom_call" | custom-call | tf_op jit(solution)/shard_map/patch/pallas_call | solution.py:307
  57.9 11.8 %all_to_all.10.p_ref = bf16[16,24,128]{2,1,0:T(8,128)(2,1)S(1)} all-to-all(bf16[16,24,128]{2,1,0:T(8,128)(2,1)S(1)} %patch.1), channel_id=1, replica_groups=mesh['tm'=16,'lat'=32] {'tm'}, dimensions={0} | all-to-all | bytes 196608 | tf_op jit(solution)/shard_map/all_to_all | solution.py:360
  69.8 0.8 %unpack.1 = f32[336,128]{1,0:T(8,128)} custom-call(bf16[16,24,128]{2,1,0:T(8,128)(2,1)S(1)} %all_to_all.10.p_ref), custom_call_target="tpu_custom_call" | custom-call | tf_op jit(solution)/shard_map/unpack/pallas_call | solution.py:339
Async XLA Ops:
  2.0 21.2 %all-to-all-start = ((bf16[16,48,128]{2,1,0:T(8,128)(2,1)}), bf16[16,48,128]{2,1,0:T(8,128)(2,1)S(1)}, u32[]{:S(2)}, u32[]{:S(2)}) async-start(bf16[16,48,128]{2,1,0:T(8,128)(2,1)} %pack.1), calls=%async_computation | async-start | bytes 393216 | tf_op jit(solution)/shard_map/all_to_all | solution.py:354
  23.2 9.8 %collective-permute-start.1 = (bf16[16,48,128]{2,1,0:T(8,128)(2,1)S(1)}, bf16[16,48,128]{2,1,0:T(8,128)(2,1)S(1)}, u32[]{:S(2)}, u32[]{:S(2)}) collective-permute-start(bf16[16,48,128]{2,1,0:T(8,128)(2,1)S(1)} %all-to-all-done.own_ref), channel_id=1, source_target_pairs={{1,0},{2,1},{3,2},{4,3},{5,4},{6,5},{7,6},{8,7},{9,8},{10,9},{11,1... | collective-permute-start | bytes 589832 | tf_op jit(solution)/shard_map/ppermute | solution.py:358
  28.5 10.4 %collective-permute-start = (bf16[16,48,128]{2,1,0:T(8,128)(2,1)S(1)}, bf16[16,48,128]{2,1,0:T(8,128)(2,1)S(1)}, u32[]{:S(2)}, u32[]{:S(2)}) collective-permute-start(bf16[16,48,128]{2,1,0:T(8,128)(2,1)S(1)} %all-to-all-done.own_ref), channel_id=1, source_target_pairs={{0,1},{1,2},{2,3},{3,4},{4,5},{5,6},{6,7},{7,8},{8,9},{9,10},{10,1... | collective-permute-start | bytes 589832 | tf_op jit(solution)/shard_map/ppermute | solution.py:357
  39.0 1.7 %copy-start = (bf16[2,256,2304]{2,1,0:T(8,128)(2,1)S(1)}, bf16[2,256,2304]{2,1,0:T(8,128)(2,1)}, u32[]{:S(2)}) copy-start(bf16[2,256,2304]{2,1,0:T(8,128)(2,1)} %get-tuple-element.39.conv_ref) | copy-start | bytes 7077892
  40.6 1.0 %copy-start.1 = (bf16[4,256,256]{2,1,0:T(8,128)(2,1)S(1)}, bf16[4,256,256]{2,1,0:T(8,128)(2,1)}, u32[]{:S(2)}) copy-start(bf16[4,256,256]{2,1,0:T(8,128)(2,1)} %get-tuple-element.35.in_pack_ref) | copy-start | bytes 1572868
  41.7 0.9 %copy-start.2 = (bf16[256,256]{1,0:T(8,128)(2,1)S(1)}, bf16[256,256]{1,0:T(8,128)(2,1)}, u32[]{:S(2)}) copy-start(bf16[256,256]{1,0:T(8,128)(2,1)} %get-tuple-element.40.swap_ref) | copy-start | bytes 393220
  42.6 0.9 %copy-start.3 = (f32[6,16,256]{2,1,0:T(8,128)S(1)}, f32[6,16,256]{2,1,0:T(8,128)}, u32[]{:S(2)}) copy-start(f32[6,16,256]{2,1,0:T(8,128)} %get-tuple-element.34.film_ref) | copy-start | bytes 294916
  43.5 0.8 %copy-start.4 = (bf16[128,256]{1,0:T(8,128)(2,1)S(1)}, bf16[128,256]{1,0:T(8,128)(2,1)}, u32[]{:S(2)}) copy-start(bf16[128,256]{1,0:T(8,128)(2,1)} %get-tuple-element.36.in_t_ref) | copy-start | bytes 196612
  44.3 0.8 %copy-start.5 = (bf16[256,128]{1,0:T(8,128)(2,1)S(1)}, bf16[256,128]{1,0:T(8,128)(2,1)}, u32[]{:S(2)}) copy-start(bf16[256,128]{1,0:T(8,128)(2,1)} %get-tuple-element.37.out_t_ref) | copy-start | bytes 196612
  45.1 0.8 %copy-start.6 = (bf16[128,256]{1,0:T(8,128)(2,1)S(1)}, bf16[128,256]{1,0:T(8,128)(2,1)}, u32[]{:S(2)}) copy-start(bf16[128,256]{1,0:T(8,128)(2,1)} %get-tuple-element.41.before_ref) | copy-start | bytes 196612
  46.0 0.8 %copy-start.7 = (bf16[128,256]{1,0:T(8,128)(2,1)S(1)}, bf16[128,256]{1,0:T(8,128)(2,1)}, u32[]{:S(2)}) copy-start(bf16[128,256]{1,0:T(8,128)(2,1)} %get-tuple-element.42.gather_ref) | copy-start | bytes 196612
  46.8 0.7 copy-start.8

commit v4 on v3

--- a/solution.py
+++ b/solution.py
@@ -90,8 +90,8 @@
             pltpu.SemaphoreType.DMA((2,)),
         ],
         name="pack",
-        compiler_params=pltpu.CompilerParams(vmem_limit_bytes=60 * 1024 * 1024),
-    )(levels, x)
+        compiler_params=pltpu.CompilerParams(vmem_limit_bytes=12000 << 10),
+    )(*[pltpu.with_memory_space_constraint(v, pltpu.HBM) for v in (levels, x)])
 
 
 def tables_kernel(levels_hbm, in_w_hbm, bias_hbm, cond_hbm, out_w_hbm, conv_hbm, film_ref, in_pack_ref, in_t_ref, out_t_ref, bias_ref, conv_ref, swap_ref, before_ref, gather_ref, levels_ref, in_w_ref, cond_ref, out_w_ref, sems):
@@ -167,8 +167,8 @@
             pltpu.SemaphoreType.DMA((6,)),
         ],
         name="tables",
-        compiler_params=pltpu.CompilerParams(vmem_limit_bytes=61400 << 10),
-    )(levels, in_weight_t, in_bias, cond_weight, out_weight, conv_weight)
+        compiler_params=pltpu.CompilerParams(vmem_limit_bytes=12000 << 10),
+    )(*[pltpu.with_memory_space_constraint(v, pltpu.HBM) for v in (levels, in_weight_t, in_bias, cond_weight, out_weight, conv_weight)])
 
 
 def split(value):

time: 71.2 us -> 63.1 us (0.89)
  local copies, waits for them, and re-layouts: 8.53 us -> 1.46 us
  Pallas kernels: 16.8 us -> 15.1 us
  waiting for transfers between devices: 15 us -> 16.1 us
    unnamed x18 -> x4, local copies, waits for them, and re-layouts: 8.53 us -> 1.46 us
    pallas_call x1, Pallas kernels: 3.66 us -> 1.95 us  [tables(): pl.pallas_call(tables_kernel, out_shape=[jax.ShapeDtypeStruct((6, SLOTS,...]
    all_to_all x1, waiting for transfers between devices: 6.54 us -> 7.62 us  [on_device(): own = lax.all_to_all(pieces, 'tm', 0, 0)]
  transfers between devices with their start and end apart: 3 -> 3, of which waited for: 3 -> 3; matrix products, arithmetic and copies ran while one was open for 0% -> 0% of each run, Pallas kernels for 5% -> 3%
where the time goes in v4:
time: 63.1 us; the launch traced here: 62.8 us
  starting transfers between devices  18.3 us (29%)
  waiting for transfers between devices  16.1 us (26%)
  Pallas kernels  15.1 us (24%)
  blocking collectives  11.8 us (19%)
  local copies, waits for them, and re-layouts  1.46 us (2%)
    all_to_all x1, blocking collectives, on_device(): back = lax.all_to_all(done, 'tm', 0, 0)  11.8 us
    all_to_all x1, starting transfers between devices, on_device(): own = lax.all_to_all(pieces, 'tm', 0, 0)  11 us
    pallas_call x1, Pallas kernels, main(): pl.pallas_call(main_kernel, out_shape=jax.ShapeDtypeStruct((SLOTS, BACK,...  10.4 us
    all_to_all x1, waiting for transfers between devices, on_device(): own = lax.all_to_all(pieces, 'tm', 0, 0)  7.62 us
    ppermute x1, waiting for transfers between devices, on_device(): low = lax.ppermute(own, 'lat', forward)  5.95 us
    ppermute x1, starting transfers between devices, on_device(): high = lax.ppermute(own, 'lat', backward)  5.36 us
    ppermute x1, waiting for transfers between devices, on_device(): high = lax.ppermute(own, 'lat', backward)  2.53 us
    pallas_call x1, Pallas kernels, tables(): pl.pallas_call(tables_kernel, out_shape=[jax.ShapeDtypeStruct((6, SLOTS,...  1.95 us
  transfers between devices with their start and end apart: 3, of which 3 were waited for; matrix products, arithmetic and copies ran while one was open for 0% of the time, Pallas kernels for 3%

profile of v4, /device:TPU:7, one launch (start us, length us, event | category | flops | bytes accessed | tf_op | source)
XLA Modules:
  0.0 62.8 jit_solution(5643561686402047824)
XLA Ops:
  0.0 1.9 %pack.1 = bf16[16,48,128]{2,1,0:T(8,128)(2,1)} custom-call(s32[17]{0:T(128)} %levels_hbm.3, f32[336,128]{1,0:T(8,128)} %bitcast.4), custom_call_target="tpu_custom_call" | custom-call | tf_op jit(solution)/shard_map/pack/pallas_call | solution.py:82
  2.0 11.0 %all-to-all-start = ((bf16[16,48,128]{2,1,0:T(8,128)(2,1)}), bf16[16,48,128]{2,1,0:T(8,128)(2,1)S(1)}, u32[]{:S(2)}, u32[]{:S(2)}) async-start(bf16[16,48,128]{2,1,0:T(8,128)(2,1)} %pack.1), calls=%async_computation | async-start | bytes 393216 | tf_op jit(solution)/shard_map/all_to_all | solution.py:354
  13.0 1.9 %tables.1 = (f32[6,16,256]{2,1,0:T(8,128)S(1)}, bf16[4,256,256]{2,1,0:T(8,128)(2,1)S(1)}, bf16[128,256]{1,0:T(8,128)(2,1)S(1)}, bf16[256,128]{1,0:T(8,128)(2,1)S...) custom-call(s32[17]{0:T(128)} %levels_hbm.3, ...), custom_call_target="tpu_custom_call" | custom-call | tf_op jit(solution)/shard_map/tables/pallas_call | solution.py:147
  14.9 0.0 copy-start
  14.9 0.6 copy-done
  15.6 7.6 %all-to-all-done.own_ref = bf16[16,48,128]{2,1,0:T(8,128)(2,1)S(1)} async-done(((bf16[16,48,128]{2,1,0:T(8,128)(2,1)}), bf16[16,48,128]{2,1,0:T(8,128)(2,1)S(1)}, u32[]{:S(2)}, u32[]{:S(2)}) %all-to-all-start) | async-done | bytes 196640 | tf_op jit(solution)/shard_map/all_to_all | solution.py:354
  23.2 5.4 %collective-permute-start.1 = (bf16[16,48,128]{2,1,0:T(8,128)(2,1)S(1)}, bf16[16,48,128]{2,1,0:T(8,128)(2,1)S(1)}, u32[]{:S(2)}, u32[]{:S(2)}) collective-permute-start(bf16[16,48,128]{2,1,0:T(8,128)(2,1)S(1)} %all-to-all-done.own_ref), channel_id=1, source_target_pairs={{1,0},{2,1},{3,2},{4,3},{5,4},{6,5},{7,6},{8,7},{9,8},{10,9},{11,1... | collective-permute-start | bytes 589832 | tf_op jit(solution)/shard_map/ppermute | solution.py:358
  28.5 1.9 %collective-permute-start = (bf16[16,48,128]{2,1,0:T(8,128)(2,1)S(1)}, bf16[16,48,128]{2,1,0:T(8,128)(2,1)S(1)}, u32[]{:S(2)}, u32[]{:S(2)}) collective-permute-start(bf16[16,48,128]{2,1,0:T(8,128)(2,1)S(1)} %all-to-all-done.own_ref), channel_id=1, source_target_pairs={{0,1},{1,2},{2,3},{3,4},{4,5},{5,6},{6,7},{7,8},{8,9},{9,10},{10,1... | collective-permute-start | bytes 589832 | tf_op jit(solution)/shard_map/ppermute | solution.py:357
  30.5 2.5 %collective-permute-done.1.high_ref = bf16[16,48,128]{2,1,0:T(8,128)(2,1)S(1)} collective-permute-done((bf16[16,48,128]{2,1,0:T(8,128)(2,1)S(1)}, bf16[16,48,128]{2,1,0:T(8,128)(2,1)S(1)}, u32[]{:S(2)}, u32[]{:S(2)}) %collective-permute-start.1) | collective-permute-done | bytes 196640 | tf_op jit(solution)/shard_map/ppermute | solution.py:358
  33.0 5.9 %collective-permute-done.low_ref = bf16[16,48,128]{2,1,0:T(8,128)(2,1)S(1)} collective-permute-done((bf16[16,48,128]{2,1,0:T(8,128)(2,1)S(1)}, bf16[16,48,128]{2,1,0:T(8,128)(2,1)S(1)}, u32[]{:S(2)}, u32[]{:S(2)}) %collective-permute-start) | collective-permute-done | bytes 196640 | tf_op jit(solution)/shard_map/ppermute | solution.py:357
  38.9 0.0 copy-start.1
  38.9 0.8 %copy-done.1 = bf16[128,256]{1,0:T(8,128)(2,1)S(1)} copy-done((bf16[128,256]{1,0:T(8,128)(2,1)S(1)}, bf16[128,256]{1,0:T(8,128)(2,1)}, u32[]{:S(2)}) %copy-start.1) | copy-done | bytes 65560
  39.8 10.4 %patch.1 = bf16[16,24,128]{2,1,0:T(8,128)(2,1)S(1)} custom-call(bf16[16,48,128]{2,1,0:T(8,128)(2,1)S(1)} %collective-permute-done.low_ref, bf16[16,48,128]{2,1,0:T(8,128)(2,1)S(1)} %all-to-all-done.own_ref, bf16[16,48,128]{2,1,0:T(8,128)(2,1)S(1)} %collective-permute-done.1.high_ref, f32[6,16,256]{2,1,0:T(8,128)S(1)} %get-tuple-element.34.film_ref, ...), custom_call_target="tpu_custom_call" | custom-call | tf_op jit(solution)/shard_map/patch/pallas_call | solution.py:307
  50.2 11.8 %all_to_all.10.p_ref = bf16[16,24,128]{2,1,0:T(8,128)(2,1)S(1)} all-to-all(bf16[16,24,128]{2,1,0:T(8,128)(2,1)S(1)} %patch.1), channel_id=1, replica_groups=mesh['tm'=16,'lat'=32] {'tm'}, dimensions={0} | all-to-all | bytes 196608 | tf_op jit(solution)/shard_map/all_to_all | solution.py:360
  62.0 0.8 %unpack.1 = f32[336,128]{1,0:T(8,128)} custom-call(bf16[16,24,128]{2,1,0:T(8,128)(2,1)S(1)} %all_to_all.10.p_ref), custom_call_target="tpu_custom_call" | custom-call | tf_op jit(solution)/shard_map/unpack/pallas_call | solution.py:339
Async XLA Ops:
  2.0 21.2 %all-to-all-start = ((bf16[16,48,128]{2,1,0:T(8,128)(2,1)}), bf16[16,48,128]{2,1,0:T(8,128)(2,1)S(1)}, u32[]{:S(2)}, u32[]{:S(2)}) async-start(bf16[16,48,128]{2,1,0:T(8,128)(2,1)} %pack.1), calls=%async_computation | async-start | bytes 393216 | tf_op jit(solution)/shard_map/all_to_all | solution.py:354
  14.9 0.6 %copy-start = (bf16[128,256]{1,0:T(8,128)(2,1)}, bf16[128,256]{1,0:T(8,128)(2,1)S(1)}, u32[]{:S(2)}) copy-start(bf16[128,256]{1,0:T(8,128)(2,1)S(1)} %get-tuple-element.42.gather_ref) | copy-start | bytes 196612
  23.2 9.8 %collective-permute-start.1 = (bf16[16,48,128]{2,1,0:T(8,128)(2,1)S(1)}, bf16[16,48,128]{2,1,0:T(8,128)(2,1)S(1)}, u32[]{:S(2)}, u32[]{:S(2)}) collective-permute-start(bf16[16,48,128]{2,1,0:T(8,128)(2,1)S(1)} %all-to-all-done.own_ref), channel_id=1, source_target_pairs={{1,0},{2,1},{3,2},{4,3},{5,4},{6,5},{7,6},{8,7},{9,8},{10,9},{11,1... | collective-permute-start | bytes 589832 | tf_op jit(solution)/shard_map/ppermute | solution.py:358
  28.5 10.4 %collective-permute-start = (bf16[16,48,128]{2,1,0:T(8,128)(2,1)S(1)}, bf16[16,48,128]{2,1,0:T(8,128)(2,1)S(1)}, u32[]{:S(2)}, u32[]{:S(2)}) collective-permute-start(bf16[16,48,128]{2,1,0:T(8,128)(2,1)S(1)} %all-to-all-done.own_ref), channel_id=1, source_target_pairs={{0,1},{1,2},{2,3},{3,4},{4,5},{5,6},{6,7},{7,8},{8,9},{9,10},{10,1... | collective-permute-start | bytes 589832 | tf_op jit(solution)/shard_map/ppermute | solution.py:357
  38.9 0.8 %copy-start.1 = (bf16[128,256]{1,0:T(8,128)(2,1)S(1)}, bf16[128,256]{1,0:T(8,128)(2,1)}, u32[]{:S(2)}) copy-start(bf16[128,256]{1,0:T(8,128)(2,1)} %copy-done) | copy-start | bytes 196612

commit v5 on v4

--- a/solution.py
+++ b/solution.py
@@ -94,17 +94,17 @@
     )(*[pltpu.with_memory_space_constraint(v, pltpu.HBM) for v in (levels, x)])
 
 
-def tables_kernel(levels_hbm, in_w_hbm, bias_hbm, cond_hbm, out_w_hbm, conv_hbm, film_ref, in_pack_ref, in_t_ref, out_t_ref, bias_ref, conv_ref, swap_ref, before_ref, gather_ref, levels_ref, in_w_ref, cond_ref, out_w_ref, sems):
+def tables_kernel(levels_hbm, in_w_hbm, bias_hbm, cond_hbm, out_w_hbm, conv_hbm, film_ref, in_pack_ref, in_t_ref, out_t_ref, bias_ref, conv_ref, picks_ref, levels_ref, in_w_ref, cond_ref, out_w_ref, sems):
     sources = (levels_hbm, in_w_hbm, cond_hbm, out_w_hbm, bias_hbm, conv_hbm)
     targets = (levels_ref, in_w_ref, cond_ref, out_w_ref, bias_ref, conv_ref)
     copies = [pltpu.make_async_copy(a, b, sems.at[i]) for i, (a, b) in enumerate(zip(sources, targets))]
     for copy in copies:
         copy.start()
     to, frm = iota((256, 256), 0), iota((256, 256), 1)
-    swap_ref[...] = one_hot(((to >> 4) == (frm & 15)) & ((to & 15) == (frm >> 4)))
+    picks_ref[:256] = one_hot(((to >> 4) == (frm & 15)) & ((to & 15) == (frm >> 4)))
     to, frm = iota((128, 256), 0), iota((128, 256), 1) & 127
-    before_ref[...] = one_hot(((to >> 4) == (frm >> 4)) & ((frm & 15) < (to & 15)))
-    gather_ref[...] = one_hot(((to & 7) == (frm >> 4)) & ((frm & 15) <= (to >> 3)))
+    picks_ref[256:384] = one_hot(((to >> 4) == (frm >> 4)) & ((frm & 15) < (to & 15)))
+    picks_ref[384:] = one_hot(((to & 7) == (frm >> 4)) & ((frm & 15) <= (to >> 3)))
     copies[0].wait()
     place = iota((SLOTS, 128), 0)
     now = jnp.zeros((SLOTS, 128), jnp.int32)
@@ -153,12 +153,10 @@
             jax.ShapeDtypeStruct((HID, 128), BF16),
             jax.ShapeDtypeStruct((1, HID), F32),
             jax.ShapeDtypeStruct((2, HID, 9 * HID), BF16),
-            jax.ShapeDtypeStruct((256, 256), BF16),
-            jax.ShapeDtypeStruct((128, 256), BF16),
-            jax.ShapeDtypeStruct((128, 256), BF16),
+            jax.ShapeDtypeStruct((512, 256), BF16),
         ],
         in_specs=[pl.BlockSpec(memory_space=pltpu.HBM)] * 6,
-        out_specs=[pl.BlockSpec(memory_space=VMEM)] * 9,
+        out_specs=[pl.BlockSpec(memory_space=VMEM)] * 7,
         scratch_shapes=[
             pltpu.SMEM((SLOTS + 1,), jnp.int32),
             VMEM((C, HID), BF16),
@@ -196,7 +194,7 @@
     return jnp.concatenate([high, low], axis=0)
 
 
-def main_kernel(low_ref, own_ref, high_ref, film_ref, in_pack_ref, in_t_ref, out_t_ref, bias_ref, conv_ref, swap_ref, before_ref, gather_ref, o_ref, h0, h1, g0, g1, x1, s2):
+def main_kernel(near_ref, own_ref, far_ref, film_ref, in_pack_ref, in_t_ref, out_t_ref, bias_ref, conv_ref, picks_ref, o_ref, h0, h1, g0, g1, x1, s2):
     place = lax.axis_index("lat")
     count = lax.axis_size("lat")
     inside_low = jnp.where(place > 0, 1.0, 0.0).astype(F32)
@@ -209,11 +207,13 @@
     def gate_of(row):
         return inside_low if row < 0 else inside_high if row >= ROWS else F32(1.0)
 
+    odd = (place & 1) == 1
+    near, far = near_ref[...], far_ref[...]
     blocks = [
-        [ref[:, 16 * group : 16 * group + 16, :].reshape(256, 128) for group in range(3)]
-        for ref in (low_ref, own_ref, high_ref)
+        [value[:, 16 * group : 16 * group + 16, :].reshape(256, 128) for group in range(3)]
+        for value in (jnp.where(odd, near, far), own_ref[...], jnp.where(odd, far, near))
     ]
-    swap = swap_ref[...]
+    swap = picks_ref[:256]
 
     def swapped(left, right):
         both = jnp.dot(swap, jnp.concatenate([left, right], axis=1), preferred_element_type=F32)
@@ -259,7 +259,7 @@
         earlier = []
         for pair in range(3):
             rhs = [halves(drift[256 * pair + 128 * k : 256 * pair + 128 * k + 128]) for k in range(2)]
-            both = jnp.dot(before_ref[...], jnp.concatenate(rhs, axis=1), preferred_element_type=F32)
+            both = jnp.dot(picks_ref[256:384], jnp.concatenate(rhs, axis=1), preferred_element_type=F32)
             earlier += [both[:, :128], both[:, 128:]]
         state = jnp.concatenate(earlier, axis=0).reshape(48, SLOTS, 128) + anchor
         scaled = []
@@ -291,7 +291,7 @@
     done = []
     for pair in range(2):
         rhs = [halves(drift[256 * pair + 128 * k : 256 * pair + 128 * k + 128]) for k in range(2)]
-        both = jnp.dot(gather_ref[...], jnp.concatenate(rhs, axis=1), preferred_element_type=F32)
+        both = jnp.dot(picks_ref[384:], jnp.concatenate(rhs, axis=1), preferred_element_type=F32)
         done += [both[:, :128], both[:, 128:]]
     tail = pltpu.roll(done[0], 64, 1)
     for row in range(1, ROWS):
@@ -303,11 +303,11 @@
     o_ref[:, 2 * COLS :, :] = tail.reshape(SLOTS, COLS, 128).astype(BF16)
 
 
-def main(low, own, high, prepared):
+def main(near, own, far, prepared):
     return pl.pallas_call(
         main_kernel,
         out_shape=jax.ShapeDtypeStruct((SLOTS, BACK, 128), BF16),
-        in_specs=[pl.BlockSpec(memory_space=VMEM)] * 12,
+        in_specs=[pl.BlockSpec(memory_space=VMEM)] * 10,
         out_specs=pl.BlockSpec(memory_space=VMEM),
         scratch_shapes=[
             VMEM((12, 256, HID), BF16),
@@ -319,7 +319,7 @@
         ],
         name="patch",
         compiler_params=pltpu.CompilerParams(vmem_limit_bytes=32 << 20),
-    )(low, own, high, *prepared)
+    )(near, own, far, *prepared)
 
 
 def unpack_kernel(p_ref, o_ref):
@@ -348,15 +348,15 @@
 
 def on_device(trajectory, step_levels, in_weight, in_bias, conv_weight, cond_weight, out_weight):
     count = lax.axis_size("lat")
-    forward = [(i, i + 1) for i in range(count - 1)]
-    backward = [(b, a) for a, b in forward]
+    near_pairs = [(i, i ^ 1) for i in range(count)]
+    far_pairs = [pair for i in range(1, count - 1, 2) for pair in ((i, i + 1), (i + 1, i))]
     pieces = pack(step_levels, trajectory.reshape(C * ROWS, 128))
     own = lax.all_to_all(pieces, "tm", 0, 0)
     prepared = tables(step_levels, in_weight.T, in_bias[None, :], cond_weight, out_weight, conv_weight)
     own, prepared = lax.optimization_barrier((own, prepared))
-    low = lax.ppermute(own, "lat", forward)
-    high = lax.ppermute(own, "lat", backward)
-    done = main(low, own, high, prepared)
+    near = lax.ppermute(own, "lat", near_pairs)
+    far = lax.ppermute(own, "lat", far_pairs)
+    done = main(near, own, far, prepared)
     back = lax.all_to_all(done, "tm", 0, 0)
     return unpack(back).reshape(1, C, ROWS, 128)
 

time: 63.1 us -> 61 us (0.967)
  waiting for transfers between devices: 16.1 us -> 14 us
    ppermute x2, waiting for transfers between devices: 8.47 us -> 6.37 us  [the longest x1 3.38 us: on_device(): far = lax.ppermute(own, 'lat', far_pairs)]
where the time goes in v5:
time: 61 us; the launch traced here: 60.7 us
  starting transfers between devices  18.3 us (30%)
  Pallas kernels  15.1 us (25%)
  waiting for transfers between devices  14 us (23%)
  blocking collectives  11.8 us (19%)
  local copies, waits for them, and re-layouts  1.46 us (2%)
    all_to_all x1, blocking collectives, on_device(): back = lax.all_to_all(done, 'tm', 0, 0)  11.8 us
    all_to_all x1, starting transfers between devices, on_device(): own = lax.all_to_all(pieces, 'tm', 0, 0)  11 us
    pallas_call x1, Pallas kernels, main(): pl.pallas_call(main_kernel, out_shape=jax.ShapeDtypeStruct((SLOTS, BACK,...  10.4 us
    all_to_all x1, waiting for transfers between devices, on_device(): own = lax.all_to_all(pieces, 'tm', 0, 0)  7.62 us
    ppermute x1, starting transfers between devices, on_device(): far = lax.ppermute(own, 'lat', far_pairs)  5.36 us
    ppermute x1, waiting for transfers between devices, on_device(): far = lax.ppermute(own, 'lat', far_pairs)  3.38 us
    ppermute x1, waiting for transfers between devices, on_device(): near = lax.ppermute(own, 'lat', near_pairs)  2.99 us
    pallas_call x1, Pallas kernels, tables(): pl.pallas_call(tables_kernel, out_shape=[jax.ShapeDtypeStruct((6, SLOTS,...  1.95 us
  transfers between devices with their start and end apart: 3, of which 3 were waited for; matrix products, arithmetic and copies ran while one was open for 0% of the time, Pallas kernels for 3%

profile of v5, /device:TPU:7, one launch (start us, length us, event | category | flops | bytes accessed | tf_op | source)
XLA Modules:
  0.0 60.7 jit_solution(8619263081162977889)
XLA Ops:
  0.0 1.9 %pack.1 = bf16[16,48,128]{2,1,0:T(8,128)(2,1)} custom-call(s32[17]{0:T(128)} %levels_hbm.3, f32[336,128]{1,0:T(8,128)} %bitcast.4), custom_call_target="tpu_custom_call" | custom-call | tf_op jit(solution)/shard_map/pack/pallas_call | solution.py:82
  2.0 11.0 %all-to-all-start = ((bf16[16,48,128]{2,1,0:T(8,128)(2,1)}), bf16[16,48,128]{2,1,0:T(8,128)(2,1)S(1)}, u32[]{:S(2)}, u32[]{:S(2)}) async-start(bf16[16,48,128]{2,1,0:T(8,128)(2,1)} %pack.1), calls=%async_computation | async-start | bytes 393216 | tf_op jit(solution)/shard_map/all_to_all | solution.py:354
  13.0 1.9 %tables.1 = (f32[6,16,256]{2,1,0:T(8,128)S(1)}, bf16[4,256,256]{2,1,0:T(8,128)(2,1)S(1)}, bf16[128,256]{1,0:T(8,128)(2,1)S(1)}, bf16[256,128]{1,0:T(8,128)(2,1)S...) custom-call(s32[17]{0:T(128)} %levels_hbm.3, bf16[84,256]{1,0:T(8,128)(2,1)} %bitcast.5, ...), custom_call_target="tpu_custom_call" | custom-call | tf_op jit(solution)/shard_map/tables/pallas_call | solution.py:147
  14.9 0.0 copy-start
  14.9 0.6 %copy-done = bf16[256,128]{1,0:T(8,128)(2,1)} copy-done((bf16[256,128]{1,0:T(8,128)(2,1)}, bf16[256,128]{1,0:T(8,128)(2,1)S(1)}, u32[]{:S(2)}) %copy-start) | copy-done | bytes 65560
  15.6 7.6 %all-to-all-done.own_ref = bf16[16,48,128]{2,1,0:T(8,128)(2,1)S(1)} async-done(((bf16[16,48,128]{2,1,0:T(8,128)(2,1)}), bf16[16,48,128]{2,1,0:T(8,128)(2,1)S(1)}, u32[]{:S(2)}, u32[]{:S(2)}) %all-to-all-start) | async-done | bytes 196640 | tf_op jit(solution)/shard_map/all_to_all | solution.py:354
  23.2 5.4 %collective-permute-start.1 = (bf16[16,48,128]{2,1,0:T(8,128)(2,1)S(1)}, bf16[16,48,128]{2,1,0:T(8,128)(2,1)S(1)}, u32[]{:S(2)}, u32[]{:S(2)}) collective-permute-start(bf16[16,48,128]{2,1,0:T(8,128)(2,1)S(1)} %all-to-all-done.own_ref), channel_id=1, source_target_pairs={{1,2},{2,1},{3,4},{4,3},{5,6},{6,5},{7,8},{8,7},{9,10},{10,9},{11,... | collective-permute-start | bytes 589832 | tf_op jit(solution)/shard_map/ppermute | solution.py:358
  28.5 1.9 %collective-permute-start = (bf16[16,48,128]{2,1,0:T(8,128)(2,1)S(1)}, bf16[16,48,128]{2,1,0:T(8,128)(2,1)S(1)}, u32[]{:S(2)}, u32[]{:S(2)}) collective-permute-start(bf16[16,48,128]{2,1,0:T(8,128)(2,1)S(1)} %all-to-all-done.own_ref), channel_id=1, source_target_pairs={{0,1},{1,0},{2,3},{3,2},{4,5},{5,4},{6,7},{7,6},{8,9},{9,8},{10,11... | collective-permute-start | bytes 589832 | tf_op jit(solution)/shard_map/ppermute | solution.py:357
  30.5 3.4 %collective-permute-done.1.far_ref = bf16[16,48,128]{2,1,0:T(8,128)(2,1)S(1)} collective-permute-done((bf16[16,48,128]{2,1,0:T(8,128)(2,1)S(1)}, bf16[16,48,128]{2,1,0:T(8,128)(2,1)S(1)}, u32[]{:S(2)}, u32[]{:S(2)}) %collective-permute-start.1) | collective-permute-done | bytes 196640 | tf_op jit(solution)/shard_map/ppermute | solution.py:358
  33.8 3.0 %collective-permute-done.near_ref = bf16[16,48,128]{2,1,0:T(8,128)(2,1)S(1)} collective-permute-done((bf16[16,48,128]{2,1,0:T(8,128)(2,1)S(1)}, bf16[16,48,128]{2,1,0:T(8,128)(2,1)S(1)}, u32[]{:S(2)}, u32[]{:S(2)}) %collective-permute-start) | collective-permute-done | bytes 196640 | tf_op jit(solution)/shard_map/ppermute | solution.py:357
  36.8 0.0 copy-start.1
  36.8 0.8 %copy-done.1 = bf16[256,128]{1,0:T(8,128)(2,1)S(1)} copy-done((bf16[256,128]{1,0:T(8,128)(2,1)S(1)}, bf16[256,128]{1,0:T(8,128)(2,1)}, u32[]{:S(2)}) %copy-start.1) | copy-done | bytes 65560
  37.7 10.4 %patch.1 = bf16[16,24,128]{2,1,0:T(8,128)(2,1)S(1)} custom-call(bf16[16,48,128]{2,1,0:T(8,128)(2,1)S(1)} %collective-permute-done.near_ref, bf16[16,48,128]{2,1,0:T(8,128)(2,1)S(1)} %all-to-all-done.own_ref, bf16[16,48,128]{2,1,0:T(8,128)(2,1)S(1)} %collective-permute-done.1.far_ref, f32[6,16,256]{2,1,0:T(8,128)S(1)} %get-tuple-element.28.film_ref, ...), custom_call_target="tpu_custom_call" | custom-call | tf_op jit(solution)/shard_map/patch/pallas_call | solution.py:307
  48.1 11.8 %all_to_all.10.p_ref = bf16[16,24,128]{2,1,0:T(8,128)(2,1)S(1)} all-to-all(bf16[16,24,128]{2,1,0:T(8,128)(2,1)S(1)} %patch.1), channel_id=1, replica_groups=mesh['tm'=16,'lat'=32] {'tm'}, dimensions={0} | all-to-all | bytes 196608 | tf_op jit(solution)/shard_map/all_to_all | solution.py:360
  59.9 0.8 %unpack.1 = f32[336,128]{1,0:T(8,128)} custom-call(bf16[16,24,128]{2,1,0:T(8,128)(2,1)S(1)} %all_to_all.10.p_ref), custom_call_target="tpu_custom_call" | custom-call | tf_op jit(solution)/shard_map/unpack/pallas_call | solution.py:339
Async XLA Ops:
  2.0 21.2 %all-to-all-start = ((bf16[16,48,128]{2,1,0:T(8,128)(2,1)}), bf16[16,48,128]{2,1,0:T(8,128)(2,1)S(1)}, u32[]{:S(2)}, u32[]{:S(2)}) async-start(bf16[16,48,128]{2,1,0:T(8,128)(2,1)} %pack.1), calls=%async_computation | async-start | bytes 393216 | tf_op jit(solution)/shard_map/all_to_all | solution.py:354
  14.9 0.6 %copy-start = (bf16[256,128]{1,0:T(8,128)(2,1)}, bf16[256,128]{1,0:T(8,128)(2,1)S(1)}, u32[]{:S(2)}) copy-start(bf16[256,128]{1,0:T(8,128)(2,1)S(1)} %get-tuple-element.31.out_t_ref) | copy-start | bytes 196612
  23.2 10.7 %collective-permute-start.1 = (bf16[16,48,128]{2,1,0:T(8,128)(2,1)S(1)}, bf16[16,48,128]{2,1,0:T(8,128)(2,1)S(1)}, u32[]{:S(2)}, u32[]{:S(2)}) collective-permute-start(bf16[16,48,128]{2,1,0:T(8,128)(2,1)S(1)} %all-to-all-done.own_ref), channel_id=1, source_target_pairs={{1,2},{2,1},{3,4},{4,3},{5,6},{6,5},{7,8},{8,7},{9,10},{10,9},{11,... | collective-permute-start | bytes 589832 | tf_op jit(solution)/shard_map/ppermute | solution.py:358
  28.5 8.3 %collective-permute-start = (bf16[16,48,128]{2,1,0:T(8,128)(2,1)S(1)}, bf16[16,48,128]{2,1,0:T(8,128)(2,1)S(1)}, u32[]{:S(2)}, u32[]{:S(2)}) collective-permute-start(bf16[16,48,128]{2,1,0:T(8,128)(2,1)S(1)} %all-to-all-done.own_ref), channel_id=1, source_target_pairs={{0,1},{1,0},{2,3},{3,2},{4,5},{5,4},{6,7},{7,6},{8,9},{9,8},{10,11... | collective-permute-start | bytes 589832 | tf_op jit(solution)/shard_map/ppermute | solution.py:357
  36.8 0.8 %copy-start.1 = (bf16[256,128]{1,0:T(8,128)(2,1)S(1)}, bf16[256,128]{1,0:T(8,128)(2,1)}, u32[]{:S(2)}) copy-start(bf16[256,128]{1,0:T(8,128)(2,1)} %copy-done) | copy-start | bytes 196612

commit v6 on v5

v6 whole, which is shorter than its diff:
```python
import functools

import jax
import jax.numpy as jnp
from jax import lax
from jax.experimental import pallas as pl
from jax.experimental.pallas import tpu as pltpu
from jax.sharding import PartitionSpec as P

LEVELS = 64
C = 84
HID = 256
SLOTS = 16
ROWS = 4
COLS = 8
PIECE = 48
BACK = 24
SWAP, BEFORE, UPTO, IN_T, OUT_T = slice(0, 256), slice(256, 384), slice(384, 512), slice(512, 640), slice(640, 768)
IN_PACK = 768

SIGMA_TOP = 1.0
SIGMA_LOW = 0.02
RHO = 7.0
ROOT_TOP = SIGMA_TOP ** (1.0 / RHO)
ROOT_LOW = SIGMA_LOW ** (1.0 / RHO)

F32 = jnp.float32
BF16 = jnp.bfloat16
VMEM = pltpu.VMEM
NT = (((1,), (1,)), ((), ()))
TN = (((0,), (0,)), ((), ()))


def iota(shape, dim):
    return lax.broadcasted_iota(jnp.int32, shape, dim)


def one_hot(mask):
    return jnp.where(mask, 1.0, 0.0).astype(BF16)


def sigma_of(level):
    root = ROOT_TOP + level.astype(F32) / (LEVELS - 1) * (ROOT_LOW - ROOT_TOP)
    square = root * root
    return square * square * square * root


def lane_of(channel, row):
    head = channel + jnp.where(row >= 2, 64, 0)
    tail = 128 + 32 * row + (channel - 64)
    return jnp.where(channel < 64, head, tail)


def pack_kernel(levels_hbm, x_hbm, o_ref, levels_ref, x_ref, sems):
    get_levels = pltpu.make_async_copy(levels_hbm, levels_ref, sems.at[0])
    get_x = pltpu.make_async_copy(x_hbm, x_ref, sems.at[1])
    get_levels.start()
    get_x.start()
    slot = lax.axis_index("tm")
    shape = (C * ROWS, 3 * 128)
    index, lane = iota(shape, 0), iota(shape, 1)
    channel, row = index >> 2, index & 3
    target = lane_of(channel, row)
    target = jnp.where(target < 128, target + 128 * (row & 1), target + 128)
    places = one_hot(lane == target)
    get_levels.wait()
    sigma = sigma_of(jnp.full((1, 128), levels_ref[slot], jnp.int32))
    scale = jnp.sqrt(sigma * sigma + 0.25)
    get_x.wait()
    scaled = pltpu.roll(x_ref[...] / scale, 4, 1).astype(BF16)
    packed = lax.dot_general(scaled, places, TN, preferred_element_type=F32)
    for window in range(SLOTS):
        start = COLS * window
        if window < SLOTS - 1:
            part = packed[start : start + 2 * COLS]
        else:
            part = jnp.concatenate([packed[start:], packed[:COLS]], axis=0)
        part = part.astype(BF16)
        for group in range(3):
            o_ref[window, 16 * group : 16 * group + 16, :] = part[:, 128 * group : 128 * group + 128]


def pack(levels, x):
    return pl.pallas_call(
        pack_kernel,
        out_shape=jax.ShapeDtypeStruct((SLOTS, PIECE, 128), BF16),
        in_specs=[pl.BlockSpec(memory_space=pltpu.HBM)] * 2,
        out_specs=pl.BlockSpec(memory_space=VMEM),
        scratch_shapes=[
            pltpu.SMEM((SLOTS + 1,), jnp.int32),
            VMEM((C * ROWS, 128), F32),
            pltpu.SemaphoreType.DMA((2,)),
        ],
        name="pack",
        compiler_params=pltpu.CompilerParams(vmem_limit_bytes=12000 << 10),
    )(*[pltpu.with_memory_space_constraint(v, pltpu.HBM) for v in (levels, x)])


def tables_kernel(levels_hbm, in_w_hbm, bias_hbm, cond_hbm, out_w_hbm, conv_hbm, film_ref, picks_ref, filter_ref, levels_ref, in_w_ref, bias_ref, cond_ref, out_w_ref, conv_ref, sems):
    sources = (levels_hbm, in_w_hbm, cond_hbm, out_w_hbm, bias_hbm, conv_hbm)
    targets = (levels_ref, in_w_ref, cond_ref, out_w_ref, bias_ref, conv_ref)
    copies = [pltpu.make_async_copy(a, b, sems.at[i]) for i, (a, b) in enumerate(zip(sources, targets))]
    for copy in copies:
        copy.start()
    to, frm = iota((256, 256), 0), iota((256, 256), 1)
    picks_ref[SWAP] = one_hot(((to >> 4) == (frm & 15)) & ((to & 15) == (frm >> 4)))
    to, frm = iota((128, 256), 0), iota((128, 256), 1) & 127
    picks_ref[BEFORE] = one_hot(((to >> 4) == (frm >> 4)) & ((frm & 15) < (to & 15)))
    cell = frm >> 4
    column = ((cell & 3) << 1) + (cell >> 2)
    picks_ref[UPTO] = one_hot(((to & 7) == column) & ((frm & 15) <= (to >> 3)))
    copies[0].wait()
    place = iota((SLOTS, 128), 0)
    now = jnp.zeros((SLOTS, 128), jnp.int32)
    following = now
    for k in range(SLOTS):
        now = jnp.where(place == k, levels_ref[k], now)
        following = jnp.where(place == k, levels_ref[k + 1], following)
    now, following = sigma_of(now), sigma_of(following)
    variance = now * now + 0.25
    root = jnp.sqrt(variance)
    ratio = (following - now) / now
    film_ref[4, :, :128] = 1.0 / root
    film_ref[4, :, 128:] = root
    film_ref[5, :, :128] = (1.0 - 0.25 / variance) * ratio
    film_ref[5, :, 128:] = 0.5 * now / root * ratio
    j = iota((SLOTS, 128), 1).astype(F32)
    frequency = jnp.exp(j * (jnp.log(F32(100.0)) / 128.0))
    phases = jnp.log(now) / 4.0 * frequency
    embedding = jnp.concatenate([jnp.cos(phases), jnp.sin(phases)], axis=1).astype(BF16)
    for copy in copies[1:5]:
        copy.wait()
    film_ref[6] = jnp.broadcast_to(bias_ref[...], (SLOTS, HID))
    conditions = jnp.dot(embedding, cond_ref[...], preferred_element_type=F32)
    film_ref[0] = 0.5 * (1.0 + conditions[:, 0:256])
    film_ref[1] = 0.5 * conditions[:, 256:512]
    film_ref[2] = 0.5 * (1.0 + conditions[:, 512:768])
    film_ref[3] = 0.5 * conditions[:, 768:1024]
    channel, lane = iota((C, 256), 0), iota((C, 256), 1)
    for row in range(ROWS):
        pick = one_hot(lane == lane_of(channel, row))
        packed = lax.dot_general(pick, in_w_ref[...], TN, preferred_element_type=F32)
        picks_ref[IN_PACK + 256 * row : IN_PACK + 256 * row + 256] = packed.astype(BF16)
    eye = one_hot(iota((C, 128), 0) == iota((C, 128), 1))
    picks_ref[IN_T] = lax.dot_general(eye, in_w_ref[...], TN, preferred_element_type=F32).astype(BF16)
    picks_ref[OUT_T] = lax.dot_general(eye, out_w_ref[...], TN, preferred_element_type=F32).astype(BF16)
    copies[5].wait()
    for layer in range(2):
        for a in range(3):
            west, mid, east = [conv_ref[layer, :, HID * (3 * a + b) : HID * (3 * a + b) + HID] for b in range(3)]
            lanes = slice(HID * a, HID * a + HID)
            outer = 0.5 * (west.astype(F32) + east.astype(F32))
            inner = 0.5 * mid.astype(F32)
            filter_ref[layer, 0, :, lanes] = west
            filter_ref[layer, 1, :, lanes] = (outer + inner).astype(BF16)
            filter_ref[layer, 2, :, lanes] = (outer - inner).astype(BF16)
            filter_ref[layer, 3, :, lanes] = east


def tables(levels, in_weight_t, in_bias, cond_weight, out_weight, conv_weight):
    return pl.pallas_call(
        tables_kernel,
        out_shape=[
            jax.ShapeDtypeStruct((7, SLOTS, HID), F32),
            jax.ShapeDtypeStruct((IN_PACK + 1024, 256), BF16),
            jax.ShapeDtypeStruct((2, 4, HID, 3 * HID), BF16),
        ],
        in_specs=[pl.BlockSpec(memory_space=pltpu.HBM)] * 6,
        out_specs=[pl.BlockSpec(memory_space=VMEM)] * 3,
        scratch_shapes=[
            pltpu.SMEM((SLOTS + 1,), jnp.int32),
            VMEM((C, HID), BF16),
            VMEM((1, HID), F32),
            VMEM((256, 1024), BF16),
            VMEM((C, HID), BF16),
            VMEM((2, HID, 9 * HID), BF16),
            pltpu.SemaphoreType.DMA((6,)),
        ],
        name="tables",
        compiler_params=pltpu.CompilerParams(vmem_limit_bytes=24 << 20),
    )(*[pltpu.with_memory_space_constraint(v, pltpu.HBM) for v in (levels, in_weight_t, in_bias, cond_weight, out_weight, conv_weight)])


def split(value):
    high = value.astype(BF16)
    return high, (value - high.astype(F32)).astype(BF16)


def convolve(ref, top, rows, pairs, filters):
    parts = []
    for kind in range(4):
        views = [ref[kind, top + a : top + a + rows].reshape(rows * pairs * SLOTS, HID) for a in range(3)]
        lhs = jnp.concatenate(views, axis=1)
        parts.append(lax.dot_general(lhs, filters[kind], NT, preferred_element_type=F32))
    shape = (rows, pairs, SLOTS, HID)
    even = parts[0] + (parts[1] + parts[2])
    odd = (parts[1] - parts[2]) - parts[3]
    return even.reshape(shape), odd.reshape(shape)


def transform(ref, row, even, odd):
    size = (even.shape[0] - 1) * SLOTS
    values = (even[:-1] - even[1:], odd[:-1] + even[1:], even[1:] - odd[:-1], odd[:-1] - odd[1:])
    for kind, value in enumerate(values):
        ref[kind, row] = value.reshape(size, HID).astype(BF16)


def film(response, scale, shift):
    half = response * scale + shift
    return half * jnp.tanh(half) + half


def halves(value):
    high, low = split(value)
    return jnp.concatenate([high, low], axis=0)


def columns(value, count):
    pairs = value.reshape(count // 2, 2, SLOTS, value.shape[1])
    return pairs[:, 0], pairs[:, 1]


def scan(picks, drift):
    sums = []
    for start in range(0, drift.shape[0], 256):
        rhs = [halves(drift[start + at : start + at + 128]) for at in (0, 128)]
        both = jnp.dot(picks, jnp.concatenate(rhs, axis=1), preferred_element_type=F32)
        sums += [both[:, :128], both[:, 128:]]
    return sums


def main_kernel(near_ref, own_ref, far_ref, film_ref, picks_ref, filter_ref, o_ref, h0, h1, g0, g1, h1_even, h1_odd, g1_even, g1_odd, x_even, x_odd, s_even, s_odd):
    place = lax.axis_index("lat")
    count = lax.axis_size("lat")
    inside_low = jnp.where(place > 0, 1.0, 0.0).astype(F32)
    inside_high = jnp.where(place < count - 1, 1.0, 0.0).astype(F32)
    gates = (inside_low, F32(1.0), inside_high)
    bias = film_ref[6]
    inverse, root = film_ref[4, :, :128], film_ref[4, :, 128:]
    keep, gain = film_ref[5, :, :128], film_ref[5, :, 128:]
    lane = iota((1, 128), 1)
    first = iota((1, 1, SLOTS, 128), 2) == 0

    def gate_of(row):
        return inside_low if row < 0 else inside_high if row >= ROWS else F32(1.0)

    swap_odd = (place & 1) == 1
    near, far = near_ref[...], far_ref[...]
    blocks = [
        [value[:, 16 * group : 16 * group + 16, :].reshape(256, 128) for group in range(3)]
        for value in (jnp.where(swap_odd, near, far), own_ref[...], jnp.where(swap_odd, far, near))
    ]
    swap = picks_ref[SWAP]

    def swapped(left, right):
        both = jnp.dot(swap, jnp.concatenate([left, right], axis=1), preferred_element_type=F32)
        return both[:, :128], both[:, 128:]

    heads = [swapped(block[0], block[1]) for block in blocks]
    tails = [*swapped(blocks[0][2], blocks[1][2])]
    tails.append(jnp.dot(swap, blocks[2][2], preferred_element_type=F32))

    for row in range(ROWS):
        lhs = jnp.concatenate(
            [jnp.concatenate([heads[at][row & 1], tails[at]], axis=1).astype(BF16) for at in range(3)], axis=0
        )
        weight = picks_ref[IN_PACK + 256 * row : IN_PACK + 256 * row + 256]
        hidden = jnp.dot(lhs, weight, preferred_element_type=F32)
        for at in range(3):
            i = 4 * at + row
            even, odd = columns(hidden[256 * at : 256 * at + 256], 16)
            shift = (bias * gates[at])[None]
            transform(h0, i, even + shift, odd + shift)
            if 2 <= i < 10:
                head, tail = heads[at][row & 1][32:224], tails[at][32:224]
                if row >= 2:
                    head = pltpu.roll(head, 64, 1)
                if row != 2:
                    tail = pltpu.roll(tail, (64 - 32 * row) % 128, 1)
                value = jnp.where(lane < 64, head, jnp.where(lane < C, tail, 0.0))
                even, odd = columns(value, 12)
                x_even[i - 2], x_odd[i - 2] = even * root[None], odd * root[None]

    for top in range(0, 10, 5):
        even, odd = convolve(h0, top, 5, 7, filter_ref.at[0])
        for at in range(5):
            i = top + at
            scale, shift = film_ref[0] * gate_of(i - 3), film_ref[1] * gate_of(i - 3)
            here_even, here_odd = film(even[at], scale[None], shift[None]), film(odd[at], scale[None], shift[None])
            transform(h1, i, here_even, here_odd)
            if 1 <= i < 9:
                h1_even[i - 1] = here_odd[:-1].astype(BF16)
                h1_odd[i - 1] = here_even[1:].astype(BF16)

    def network(even, odd):
        hidden = jnp.concatenate([even.reshape(-1, HID), odd.reshape(-1, HID)], axis=0).astype(BF16)
        return lax.dot_general(hidden, picks_ref[OUT_T], NT, preferred_element_type=F32)

    film_two = film_ref[2][None, None], film_ref[3][None, None]

    for top in range(0, 8, 4):
        even, odd = convolve(h1, top, 4, 6, filter_ref.at[1])
        even = h1_even[top : top + 4].astype(F32) + film(even, *film_two)
        odd = h1_odd[top : top + 4].astype(F32) + film(odd, *film_two)
        x = jnp.concatenate([x_even[top : top + 4], x_odd[top : top + 4]], axis=0)
        anchor = jnp.where(first, x, 0.0)
        drift = keep * x - gain * network(even, odd).reshape(8, 6, SLOTS, 128) + anchor
        state = jnp.concatenate(scan(picks_ref[BEFORE], drift.reshape(768, 128)), axis=0)
        state = state.reshape(8, 6, SLOTS, 128) + anchor
        scaled = []
        for parity in range(2):
            for at in range(4):
                i = top + at
                here = state[4 * parity + at]
                if 2 <= i < 6:
                    if parity == 0:
                        s_even[i - 2] = here[1:5]
                    else:
                        s_odd[i - 2] = here[1:5]
                scaled.append((here * (inverse * gate_of(i - 2))[None]).reshape(96, 128).astype(BF16))
        hidden = jnp.dot(jnp.concatenate(scaled, axis=0), picks_ref[IN_T], preferred_element_type=F32)
        hidden = hidden.reshape(8, 6, SLOTS, HID)
        for at in range(4):
            shift = (bias * gate_of(top + at - 2))[None]
            transform(g0, top + at, hidden[at] + shift, hidden[4 + at] + shift)

    for top in range(0, 6, 3):
        even, odd = convolve(g0, top, 3, 5, filter_ref.at[0])
        for at in range(3):
            i = top + at
            scale, shift = film_ref[0] * gate_of(i - 1), film_ref[1] * gate_of(i - 1)
            here_even, here_odd = film(even[at], scale[None], shift[None]), film(odd[at], scale[None], shift[None])
            transform(g1, i, here_even, here_odd)
            if 1 <= i < 5:
                g1_even[i - 1] = here_odd[:-1].astype(BF16)
                g1_odd[i - 1] = here_even[1:].astype(BF16)

    even, odd = convolve(g1, 0, 4, 4, filter_ref.at[1])
    even = g1_even[...].astype(F32) + film(even, *film_two)
    odd = g1_odd[...].astype(F32) + film(odd, *film_two)
    state = jnp.concatenate([s_even[...], s_odd[...]], axis=0)
    drift = keep * state - gain * network(even, odd).reshape(8, 4, SLOTS, 128) + jnp.where(first, state, 0.0)
    drift = drift.reshape(2, 4, 64, 128)
    done = scan(picks_ref[UPTO], jnp.concatenate([drift[0], drift[1]], axis=1).reshape(512, 128))
    tail = pltpu.roll(done[0], 64, 1)
    for row in range(1, ROWS):
        here = done[row] if row == 2 else pltpu.roll(done[row], (32 * row - 64) % 128, 1)
        tail = jnp.where(lane < 32 * row, tail, here)
    for half in range(2):
        head = jnp.where(lane < 64, done[half], pltpu.roll(done[half + 2], 64, 1))
        o_ref[:, COLS * half : COLS * half + COLS, :] = head.reshape(SLOTS, COLS, 128).astype(BF16)
    o_ref[:, 2 * COLS :, :] = tail.reshape(SLOTS, COLS, 128).astype(BF16)


def main(near, own, far, prepared):
    return pl.pallas_call(
        main_kernel,
        out_shape=jax.ShapeDtypeStruct((SLOTS, BACK, 128), BF16),
        in_specs=[pl.BlockSpec(memory_space=VMEM)] * 6,
        out_specs=pl.BlockSpec(memory_space=VMEM),
        scratch_shapes=[
            VMEM((4, 12, 112, HID), BF16),
            VMEM((4, 10, 96, HID), BF16),
            VMEM((4, 8, 80, HID), BF16),
            VMEM((4, 6, 64, HID), BF16),
            *[VMEM((8, 6, SLOTS, HID), BF16)] * 2,
            *[VMEM((ROWS, 4, SLOTS, HID), BF16)] * 2,
            *[VMEM((8, 6, SLOTS, 128), F32)] * 2,
            *[VMEM((ROWS, 4, SLOTS, 128), F32)] * 2,
        ],
        name="patch",
        compiler_params=pltpu.CompilerParams(vmem_limit_bytes=32 << 20),
    )(near, own, far, *prepared)


def unpack_kernel(p_ref, o_ref):
    pieces = p_ref[...].astype(F32)

    def turned(group):
        return pieces[:, COLS * group : COLS * group + COLS, :].reshape(128, 128).T

    heads, tail = [turned(0), turned(1)], turned(2)
    for row in range(ROWS):
        start = 64 if row >= 2 else 0
        o_ref[pl.ds(row, 64, stride=ROWS), :] = heads[row & 1][start : start + 64]
        o_ref[pl.ds(64 * ROWS + row, C - 64, stride=ROWS), :] = tail[32 * row : 32 * row + C - 64]


def unpack(pieces):
    return pl.pallas_call(
        unpack_kernel,
        out_shape=jax.ShapeDtypeStruct((C * ROWS, 128), F32),
        in_specs=[pl.BlockSpec(memory_space=VMEM)],
        out_specs=pl.BlockSpec(memory_space=VMEM),
        name="unpack",
        compiler_params=pltpu.CompilerParams(vmem_limit_bytes=8 << 20),
    )(pieces)


def on_device(trajectory, step_levels, in_weight, in_bias, conv_weight, cond_weight, out_weight):
    count = lax.axis_size("lat")
    near_pairs = [(i, i ^ 1) for i in range(count)]
    far_pairs = [pair for i in range(1, count - 1, 2) for pair in ((i, i + 1), (i + 1, i))]
    pieces = pack(step_levels, trajectory.reshape(C * ROWS, 128))
    own = lax.all_to_all(pieces, "tm", 0, 0)
    prepared = tables(step_levels, in_weight.T, in_bias[None, :], cond_weight, out_weight, conv_weight)
    own, prepared = lax.optimization_barrier((own, prepared))
    near = lax.ppermute(own, "lat", near_pairs)
    far = lax.ppermute(own, "lat", far_pairs)
    done = main(near, own, far, prepared)
    back = lax.all_to_all(done, "tm", 0, 0)
    return unpack(back).reshape(1, C, ROWS, 128)


def solution(mesh):
    in_specs = (P("tm", None, "lat", None), P(), P(), P(), P(), P(), P())
    out_specs = P("tm", None, "lat", None)
    return jax.shard_map(on_device, mesh=mesh, in_specs=in_specs, out_specs=out_specs, check_vma=False)
```

time: 61 us -> 57.9 us (0.949)
  Pallas kernels: 15.1 us -> 12.2 us
  waiting for transfers between devices: 14 us -> 13.1 us
  local copies, waits for them, and re-layouts: 1.46 us -> 2.12 us
    pallas_call x1, Pallas kernels: 10.4 us -> 6.99 us  [main(): pl.pallas_call(main_kernel, out_shape=jax.ShapeDtypeStruct((SLOTS, BACK,...]
    all_to_all x1, waiting for transfers between devices: 7.62 us -> 6.75 us  [on_device(): own = lax.all_to_all(pieces, 'tm', 0, 0)]
    unnamed x4, local copies, waits for them, and re-layouts: 1.46 us -> 2.12 us
  transfers between devices with their start and end apart: 3 -> 3, of which waited for: 3 -> 3; matrix products, arithmetic and copies ran while one was open for 0% -> 0% of each run, Pallas kernels for 3% -> 4%
where the time goes in v6:
time: 57.9 us; the launch traced here: 57.6 us
  starting transfers between devices  18.3 us (32%)
  waiting for transfers between devices  13.1 us (23%)
  Pallas kernels  12.2 us (21%)
  blocking collectives  11.8 us (20%)
  local copies, waits for them, and re-layouts  2.12 us (4%)
    all_to_all x1, blocking collectives, on_device(): back = lax.all_to_all(done, 'tm', 0, 0)  11.8 us
    all_to_all x1, starting transfers between devices, on_device(): own = lax.all_to_all(pieces, 'tm', 0, 0)  11 us
    pallas_call x1, Pallas kernels, main(): pl.pallas_call(main_kernel, out_shape=jax.ShapeDtypeStruct((SLOTS, BACK,...  6.99 us
    all_to_all x1, waiting for transfers between devices, on_device(): own = lax.all_to_all(pieces, 'tm', 0, 0)  6.75 us
    ppermute x1, starting transfers between devices, on_device(): far = lax.ppermute(own, 'lat', far_pairs)  5.36 us
    ppermute x1, waiting for transfers between devices, on_device(): far = lax.ppermute(own, 'lat', far_pairs)  3.38 us
    ppermute x1, waiting for transfers between devices, on_device(): near = lax.ppermute(own, 'lat', near_pairs)  2.99 us
    pallas_call x1, Pallas kernels, tables(): pl.pallas_call(tables_kernel, out_shape=[jax.ShapeDtypeStruct((7, SLOTS,...  2.49 us
  transfers between devices with their start and end apart: 3, of which 3 were waited for; matrix products, arithmetic and copies ran while one was open for 0% of the time, Pallas kernels for 4%

profile of v6, /device:TPU:7, one launch (start us, length us, event | category | flops | bytes accessed | tf_op | source)
XLA Modules:
  0.0 57.6 jit_solution(10607637172038432520)
XLA Ops:
  0.0 2.0 %pack.1 = bf16[16,48,128]{2,1,0:T(8,128)(2,1)} custom-call(s32[17]{0:T(128)} %levels_hbm.3, f32[336,128]{1,0:T(8,128)} %bitcast.4), custom_call_target="tpu_custom_call" | custom-call | tf_op jit(solution)/shard_map/pack/pallas_call | solution.py:84
  2.0 11.0 %all-to-all-start = ((bf16[16,48,128]{2,1,0:T(8,128)(2,1)}), bf16[16,48,128]{2,1,0:T(8,128)(2,1)S(1)}, u32[]{:S(2)}, u32[]{:S(2)}) async-start(bf16[16,48,128]{2,1,0:T(8,128)(2,1)} %pack.1), calls=%async_computation | async-start | bytes 393216 | tf_op jit(solution)/shard_map/all_to_all | solution.py:405
  13.0 2.5 %tables.1 = (f32[7,16,256]{2,1,0:T(8,128)S(1)}, bf16[1792,256]{1,0:T(8,128)(2,1)S(1)}, bf16[2,4,256,768]{3,2,1,0:T(8,128)(2,1)S(1)}) custom-call(s32[17]{0:T(128)} %levels_hbm.3, bf16[84,256]{1,0:T(8,128)(2,1)} %bitcast.5, f32[1,256]{1,0:T(1,128)} %bitcast.6, bf16[256,1024]{1,0:T(8,128)(2,1)} %cond_hbm.1, bf16[84,256]{1,0:T(8,128)(2,1)} %out_w_hbm.1, ...), custom_call_target="tpu_custom_call" | custom-call | tf_op jit(solution)/shard_map/tables/pallas_call | solution.py:161
  15.5 0.0 copy-start
  15.5 0.9 %copy-done = bf16[1792,256]{1,0:T(8,128)(2,1)} copy-done((bf16[1792,256]{1,0:T(8,128)(2,1)}, bf16[1792,256]{1,0:T(8,128)(2,1)S(1)}, u32[]{:S(2)}) %copy-start) | copy-done | bytes 917528
  16.4 6.8 %all-to-all-done.own_ref = bf16[16,48,128]{2,1,0:T(8,128)(2,1)S(1)} async-done(((bf16[16,48,128]{2,1,0:T(8,128)(2,1)}), bf16[16,48,128]{2,1,0:T(8,128)(2,1)S(1)}, u32[]{:S(2)}, u32[]{:S(2)}) %all-to-all-start) | async-done | bytes 196640 | tf_op jit(solution)/shard_map/all_to_all | solution.py:405
  23.2 5.4 %collective-permute-start.1 = (bf16[16,48,128]{2,1,0:T(8,128)(2,1)S(1)}, bf16[16,48,128]{2,1,0:T(8,128)(2,1)S(1)}, u32[]{:S(2)}, u32[]{:S(2)}) collective-permute-start(bf16[16,48,128]{2,1,0:T(8,128)(2,1)S(1)} %all-to-all-done.own_ref), channel_id=1, source_target_pairs={{1,2},{2,1},{3,4},{4,3},{5,6},{6,5},{7,8},{8,7},{9,10},{10,9},{11,... | collective-permute-start | bytes 589832 | tf_op jit(solution)/shard_map/ppermute | solution.py:409
  28.5 1.9 %collective-permute-start = (bf16[16,48,128]{2,1,0:T(8,128)(2,1)S(1)}, bf16[16,48,128]{2,1,0:T(8,128)(2,1)S(1)}, u32[]{:S(2)}, u32[]{:S(2)}) collective-permute-start(bf16[16,48,128]{2,1,0:T(8,128)(2,1)S(1)} %all-to-all-done.own_ref), channel_id=1, source_target_pairs={{0,1},{1,0},{2,3},{3,2},{4,5},{5,4},{6,7},{7,6},{8,9},{9,8},{10,11... | collective-permute-start | bytes 589832 | tf_op jit(solution)/shard_map/ppermute | solution.py:408
  30.5 3.4 %collective-permute-done.1.far_ref = bf16[16,48,128]{2,1,0:T(8,128)(2,1)S(1)} collective-permute-done((bf16[16,48,128]{2,1,0:T(8,128)(2,1)S(1)}, bf16[16,48,128]{2,1,0:T(8,128)(2,1)S(1)}, u32[]{:S(2)}, u32[]{:S(2)}) %collective-permute-start.1) | collective-permute-done | bytes 196640 | tf_op jit(solution)/shard_map/ppermute | solution.py:409
  33.8 3.0 %collective-permute-done.near_ref = bf16[16,48,128]{2,1,0:T(8,128)(2,1)S(1)} collective-permute-done((bf16[16,48,128]{2,1,0:T(8,128)(2,1)S(1)}, bf16[16,48,128]{2,1,0:T(8,128)(2,1)S(1)}, u32[]{:S(2)}, u32[]{:S(2)}) %collective-permute-start) | collective-permute-done | bytes 196640 | tf_op jit(solution)/shard_map/ppermute | solution.py:408
  36.8 0.0 copy-start.1
  36.8 1.2 %copy-done.1 = bf16[1792,256]{1,0:T(8,128)(2,1)S(1)} copy-done((bf16[1792,256]{1,0:T(8,128)(2,1)S(1)}, bf16[1792,256]{1,0:T(8,128)(2,1)}, u32[]{:S(2)}) %copy-start.1) | copy-done | bytes 917528
  38.0 7.0 %patch.1 = bf16[16,24,128]{2,1,0:T(8,128)(2,1)S(1)} custom-call(bf16[16,48,128]{2,1,0:T(8,128)(2,1)S(1)} %collective-permute-done.near_ref, bf16[16,48,128]{2,1,0:T(8,128)(2,1)S(1)} %all-to-all-done.own_ref, bf16[16,48,128]{2,1,0:T(8,128)(2,1)S(1)} %collective-permute-done.1.far_ref, f32[7,16,256]{2,1,0:T(8,128)S(1)} %get-tuple-element.16.film_ref, ...), custom_call_target="tpu_custom_call" | custom-call | tf_op jit(solution)/shard_map/patch/pallas_call | solution.py:356
  45.0 11.8 %all_to_all.10.p_ref = bf16[16,24,128]{2,1,0:T(8,128)(2,1)S(1)} all-to-all(bf16[16,24,128]{2,1,0:T(8,128)(2,1)S(1)} %patch.1), channel_id=1, replica_groups=mesh['tm'=16,'lat'=32] {'tm'}, dimensions={0} | all-to-all | bytes 196608 | tf_op jit(solution)/shard_map/all_to_all | solution.py:411
  56.8 0.8 %unpack.1 = f32[336,128]{1,0:T(8,128)} custom-call(bf16[16,24,128]{2,1,0:T(8,128)(2,1)S(1)} %all_to_all.10.p_ref), custom_call_target="tpu_custom_call" | custom-call | tf_op jit(solution)/shard_map/unpack/pallas_call | solution.py:390
Async XLA Ops:
  2.0 21.2 %all-to-all-start = ((bf16[16,48,128]{2,1,0:T(8,128)(2,1)}), bf16[16,48,128]{2,1,0:T(8,128)(2,1)S(1)}, u32[]{:S(2)}, u32[]{:S(2)}) async-start(bf16[16,48,128]{2,1,0:T(8,128)(2,1)} %pack.1), calls=%async_computation | async-start | bytes 393216 | tf_op jit(solution)/shard_map/all_to_all | solution.py:405
  15.5 1.0 %copy-start = (bf16[1792,256]{1,0:T(8,128)(2,1)}, bf16[1792,256]{1,0:T(8,128)(2,1)S(1)}, u32[]{:S(2)}) copy-start(bf16[1792,256]{1,0:T(8,128)(2,1)S(1)} %get-tuple-element.17.picks_ref) | copy-start | bytes 2752516
  23.2 10.7 %collective-permute-start.1 = (bf16[16,48,128]{2,1,0:T(8,128)(2,1)S(1)}, bf16[16,48,128]{2,1,0:T(8,128)(2,1)S(1)}, u32[]{:S(2)}, u32[]{:S(2)}) collective-permute-start(bf16[16,48,128]{2,1,0:T(8,128)(2,1)S(1)} %all-to-all-done.own_ref), channel_id=1, source_target_pairs={{1,2},{2,1},{3,4},{4,3},{5,6},{6,5},{7,8},{8,7},{9,10},{10,9},{11,... | collective-permute-start | bytes 589832 | tf_op jit(solution)/shard_map/ppermute | solution.py:409
  28.5 8.3 %collective-permute-start = (bf16[16,48,128]{2,1,0:T(8,128)(2,1)S(1)}, bf16[16,48,128]{2,1,0:T(8,128)(2,1)S(1)}, u32[]{:S(2)}, u32[]{:S(2)}) collective-permute-start(bf16[16,48,128]{2,1,0:T(8,128)(2,1)S(1)} %all-to-all-done.own_ref), channel_id=1, source_target_pairs={{0,1},{1,0},{2,3},{3,2},{4,5},{5,4},{6,7},{7,6},{8,9},{9,8},{10,11... | collective-permute-start | bytes 589832 | tf_op jit(solution)/shard_map/ppermute | solution.py:408
  36.8 1.2 %copy-start.1 = (bf16[1792,256]{1,0:T(8,128)(2,1)S(1)}, bf16[1792,256]{1,0:T(8,128)(2,1)}, u32[]{:S(2)}) copy-start(bf16[1792,256]{1,0:T(8,128)(2,1)} %copy-done) | copy-start | bytes 2752516

commit v7 on v6

--- a/solution.py
+++ b/solution.py
@@ -17,6 +17,7 @@
 BACK = 24
 SWAP, BEFORE, UPTO, IN_T, OUT_T = slice(0, 256), slice(256, 384), slice(384, 512), slice(512, 640), slice(640, 768)
 IN_PACK = 768
+LIMIT = 32 << 20
 
 SIGMA_TOP = 1.0
 SIGMA_LOW = 0.02
@@ -92,7 +93,7 @@
             pltpu.SemaphoreType.DMA((2,)),
         ],
         name="pack",
-        compiler_params=pltpu.CompilerParams(vmem_limit_bytes=12000 << 10),
+        compiler_params=pltpu.CompilerParams(vmem_limit_bytes=LIMIT),
     )(*[pltpu.with_memory_space_constraint(v, pltpu.HBM) for v in (levels, x)])
 
 
@@ -177,7 +178,7 @@
             pltpu.SemaphoreType.DMA((6,)),
         ],
         name="tables",
-        compiler_params=pltpu.CompilerParams(vmem_limit_bytes=24 << 20),
+        compiler_params=pltpu.CompilerParams(vmem_limit_bytes=LIMIT),
     )(*[pltpu.with_memory_space_constraint(v, pltpu.HBM) for v in (levels, in_weight_t, in_bias, cond_weight, out_weight, conv_weight)])
 
 
@@ -186,13 +187,13 @@
     return high, (value - high.astype(F32)).astype(BF16)
 
 
-def convolve(ref, top, rows, pairs, filters):
+def convolve(view, rows, filters):
     parts = []
     for kind in range(4):
-        views = [ref[kind, top + a : top + a + rows].reshape(rows * pairs * SLOTS, HID) for a in range(3)]
+        views = [jnp.concatenate([view(kind, i + a) for i in rows], axis=0) for a in range(3)]
         lhs = jnp.concatenate(views, axis=1)
         parts.append(lax.dot_general(lhs, filters[kind], NT, preferred_element_type=F32))
-    shape = (rows, pairs, SLOTS, HID)
+    shape = (len(rows), parts[0].shape[0] // (len(rows) * SLOTS), SLOTS, HID)
     even = parts[0] + (parts[1] + parts[2])
     odd = (parts[1] - parts[2]) - parts[3]
     return even.reshape(shape), odd.reshape(shape)
@@ -229,14 +230,76 @@
     return sums
 
 
-def main_kernel(near_ref, own_ref, far_ref, film_ref, picks_ref, filter_ref, o_ref, h0, h1, g0, g1, h1_even, h1_odd, g1_even, g1_odd, x_even, x_odd, s_even, s_odd):
+def ordered(values, picks_ref):
+    blocks = [
+        [value[:, 16 * group : 16 * group + 16, :].reshape(256, 128) for group in range(3)] for value in values
+    ]
+    swap = picks_ref[SWAP]
+    heads = []
+    for block in blocks:
+        both = jnp.dot(swap, jnp.concatenate(block[:2], axis=1), preferred_element_type=F32)
+        heads.append((both[:, :128], both[:, 128:]))
+    tails = jnp.dot(swap, jnp.concatenate([block[2] for block in blocks], axis=1), preferred_element_type=F32)
+    return heads, [tails[:, 128 * at : 128 * at + 128] for at in range(len(blocks))]
+
+
+def project(heads, tails, row, picks_ref):
+    lhs = [jnp.concatenate([head[row & 1], tail], axis=1).astype(BF16) for head, tail in zip(heads, tails)]
+    weight = picks_ref[IN_PACK + 256 * row : IN_PACK + 256 * row + 256]
+    hidden = jnp.dot(jnp.concatenate(lhs, axis=0), weight, preferred_element_type=F32)
+    return [columns(hidden[256 * at : 256 * at + 256], 16) for at in range(len(heads))]
+
+
+def state_of(head, tail, row, film_ref):
+    head, tail = head[row & 1][32:224], tail[32:224]
+    if row >= 2:
+        head = pltpu.roll(head, 64, 1)
+    if row != 2:
+        tail = pltpu.roll(tail, (64 - 32 * row) % 128, 1)
+    lane = iota((1, 128), 1)
+    even, odd = columns(jnp.where(lane < 64, head, jnp.where(lane < C, tail, 0.0)), 12)
+    root = film_ref[4, :, 128:][None]
+    return even * root, odd * root
+
+
+def inner_kernel(own_ref, film_ref, picks_ref, filter_ref, h0, h1, keep_ref, x_ref):
+    heads, tails = ordered([own_ref[...]], picks_ref)
+    shift = film_ref[6][None]
+    for row in range(ROWS):
+        even, odd = project(heads, tails, row, picks_ref)[0]
+        transform(h0, row, even + shift, odd + shift)
+        x_ref[0, row], x_ref[1, row] = state_of(heads[0], tails[0], row, film_ref)
+    even, odd = convolve(lambda kind, i: h0[kind, i], (0, 1), filter_ref.at[0])
+    even, odd = film(even, film_ref[0], film_ref[1]), film(odd, film_ref[0], film_ref[1])
+    for at in range(2):
+        transform(h1, at, even[at], odd[at])
+        keep_ref[0, at], keep_ref[1, at] = odd[at, :-1].astype(BF16), even[at, 1:].astype(BF16)
+
+
+def inner(own, prepared):
+    return pl.pallas_call(
+        inner_kernel,
+        out_shape=[
+            jax.ShapeDtypeStruct((4, ROWS, 112, HID), BF16),
+            jax.ShapeDtypeStruct((4, 2, 96, HID), BF16),
+            jax.ShapeDtypeStruct((2, 2, 6, SLOTS, HID), BF16),
+            jax.ShapeDtypeStruct((2, ROWS, 6, SLOTS, 128), F32),
+        ],
+        in_specs=[pl.BlockSpec(memory_space=VMEM)] * 4,
+        out_specs=[pl.BlockSpec(memory_space=VMEM)] * 4,
+        name="inner",
+        compiler_params=pltpu.CompilerParams(vmem_limit_bytes=LIMIT),
+    )(own, *prepared)
+
+
+def main_kernel(near_ref, far_ref, film_ref, picks_ref, filter_ref, h0_own, h1_own, keep_own, x_own, o_ref, h0, h1, g0, g1, h1_even, h1_odd, g1_even, g1_odd, x_even, x_odd, s_even, s_odd):
     place = lax.axis_index("lat")
     count = lax.axis_size("lat")
     inside_low = jnp.where(place > 0, 1.0, 0.0).astype(F32)
     inside_high = jnp.where(place < count - 1, 1.0, 0.0).astype(F32)
-    gates = (inside_low, F32(1.0), inside_high)
+    gates = (inside_low, inside_high)
     bias = film_ref[6]
-    inverse, root = film_ref[4, :, :128], film_ref[4, :, 128:]
+    inverse = film_ref[4, :, :128]
     keep, gain = film_ref[5, :, :128], film_ref[5, :, 128:]
     lane = iota((1, 128), 1)
     first = iota((1, 1, SLOTS, 128), 2) == 0
@@ -246,51 +309,31 @@
 
     swap_odd = (place & 1) == 1
     near, far = near_ref[...], far_ref[...]
-    blocks = [
-        [value[:, 16 * group : 16 * group + 16, :].reshape(256, 128) for group in range(3)]
-        for value in (jnp.where(swap_odd, near, far), own_ref[...], jnp.where(swap_odd, far, near))
-    ]
-    swap = picks_ref[SWAP]
-
-    def swapped(left, right):
-        both = jnp.dot(swap, jnp.concatenate([left, right], axis=1), preferred_element_type=F32)
-        return both[:, :128], both[:, 128:]
-
-    heads = [swapped(block[0], block[1]) for block in blocks]
-    tails = [*swapped(blocks[0][2], blocks[1][2])]
-    tails.append(jnp.dot(swap, blocks[2][2], preferred_element_type=F32))
-
+    heads, tails = ordered([jnp.where(swap_odd, near, far), jnp.where(swap_odd, far, near)], picks_ref)
     for row in range(ROWS):
-        lhs = jnp.concatenate(
-            [jnp.concatenate([heads[at][row & 1], tails[at]], axis=1).astype(BF16) for at in range(3)], axis=0
-        )
-        weight = picks_ref[IN_PACK + 256 * row : IN_PACK + 256 * row + 256]
-        hidden = jnp.dot(lhs, weight, preferred_element_type=F32)
-        for at in range(3):
-            i = 4 * at + row
-            even, odd = columns(hidden[256 * at : 256 * at + 256], 16)
+        for at, (even, odd) in enumerate(project(heads, tails, row, picks_ref)):
             shift = (bias * gates[at])[None]
-            transform(h0, i, even + shift, odd + shift)
-            if 2 <= i < 10:
-                head, tail = heads[at][row & 1][32:224], tails[at][32:224]
-                if row >= 2:
-                    head = pltpu.roll(head, 64, 1)
-                if row != 2:
-                    tail = pltpu.roll(tail, (64 - 32 * row) % 128, 1)
-                value = jnp.where(lane < 64, head, jnp.where(lane < C, tail, 0.0))
-                even, odd = columns(value, 12)
-                x_even[i - 2], x_odd[i - 2] = even * root[None], odd * root[None]
-
-    for top in range(0, 10, 5):
-        even, odd = convolve(h0, top, 5, 7, filter_ref.at[0])
-        for at in range(5):
-            i = top + at
+            transform(h0, 4 * at + row, even + shift, odd + shift)
+        at = 1 if row < 2 else 0
+        i = 2 + row if row < 2 else row - 2
+        x_even[i], x_odd[i] = state_of(heads[at], tails[at], row, film_ref)
+
+    def view_zero(kind, i):
+        return h0_own[kind, i - 4] if 4 <= i < 8 else h0[kind, i if i < 4 else i - 4]
+
+    def view_one(kind, i):
+        return h1_own[kind, i - 4] if 4 <= i < 6 else h1[kind, i if i < 4 else i - 2]
+
+    for rows in (range(0, 4), range(6, 10)):
+        even, odd = convolve(view_zero, rows, filter_ref.at[0])
+        for at, i in enumerate(rows):
+            to = i if i < 4 else i - 2
             scale, shift = film_ref[0] * gate_of(i - 3), film_ref[1] * gate_of(i - 3)
             here_even, here_odd = film(even[at], scale[None], shift[None]), film(odd[at], scale[None], shift[None])
-            transform(h1, i, here_even, here_odd)
+            transform(h1, to, here_even, here_odd)
             if 1 <= i < 9:
-                h1_even[i - 1] = here_odd[:-1].astype(BF16)
-                h1_odd[i - 1] = here_even[1:].astype(BF16)
+                h1_even[to - 1] = here_odd[:-1].astype(BF16)
+                h1_odd[to - 1] = here_even[1:].astype(BF16)
 
     def network(even, odd):
         hidden = jnp.concatenate([even.reshape(-1, HID), odd.reshape(-1, HID)], axis=0).astype(BF16)
@@ -299,10 +342,18 @@
     film_two = film_ref[2][None, None], film_ref[3][None, None]
 
     for top in range(0, 8, 4):
-        even, odd = convolve(h1, top, 4, 6, filter_ref.at[1])
-        even = h1_even[top : top + 4].astype(F32) + film(even, *film_two)
-        odd = h1_odd[top : top + 4].astype(F32) + film(odd, *film_two)
-        x = jnp.concatenate([x_even[top : top + 4], x_odd[top : top + 4]], axis=0)
+        even, odd = convolve(view_one, range(top, top + 4), filter_ref.at[1])
+        lower = top == 0
+
+        def around(own, other):
+            return jnp.concatenate([other, own] if lower else [own, other], axis=0).astype(F32)
+
+        side = slice(0, 3) if lower else slice(3, 6)
+        mine = slice(0, 1) if lower else slice(1, 2)
+        even = around(keep_own[0, mine], h1_even[side]) + film(even, *film_two)
+        odd = around(keep_own[1, mine], h1_odd[side]) + film(odd, *film_two)
+        side, mine = (slice(0, 2), slice(0, 2)) if lower else (slice(2, 4), slice(2, 4))
+        x = jnp.concatenate([around(x_own[0, mine], x_even[side]), around(x_own[1, mine], x_odd[side])], axis=0)
         anchor = jnp.where(first, x, 0.0)
         drift = keep * x - gain * network(even, odd).reshape(8, 6, SLOTS, 128) + anchor
         state = jnp.concatenate(scan(picks_ref[BEFORE], drift.reshape(768, 128)), axis=0)
@@ -325,7 +376,7 @@
             transform(g0, top + at, hidden[at] + shift, hidden[4 + at] + shift)
 
     for top in range(0, 6, 3):
-        even, odd = convolve(g0, top, 3, 5, filter_ref.at[0])
+        even, odd = convolve(lambda kind, i: g0[kind, i], range(top, top + 3), filter_ref.at[0])
         for at in range(3):
             i = top + at
             scale, shift = film_ref[0] * gate_of(i - 1), film_ref[1] * gate_of(i - 1)
@@ -335,7 +386,7 @@
                 g1_even[i - 1] = here_odd[:-1].astype(BF16)
                 g1_odd[i - 1] = here_even[1:].astype(BF16)
 
-    even, odd = convolve(g1, 0, 4, 4, filter_ref.at[1])
+    even, odd = convolve(lambda kind, i: g1[kind, i], range(4), filter_ref.at[1])
     even = g1_even[...].astype(F32) + film(even, *film_two)
     odd = g1_odd[...].astype(F32) + film(odd, *film_two)
     state = jnp.concatenate([s_even[...], s_odd[...]], axis=0)
@@ -352,25 +403,25 @@
     o_ref[:, 2 * COLS :, :] = tail.reshape(SLOTS, COLS, 128).astype(BF16)
 
 
-def main(near, own, far, prepared):
+def main(near, far, prepared, middle):
     return pl.pallas_call(
         main_kernel,
         out_shape=jax.ShapeDtypeStruct((SLOTS, BACK, 128), BF16),
-        in_specs=[pl.BlockSpec(memory_space=VMEM)] * 6,
+        in_specs=[pl.BlockSpec(memory_space=VMEM)] * 9,
         out_specs=pl.BlockSpec(memory_space=VMEM),
         scratch_shapes=[
-            VMEM((4, 12, 112, HID), BF16),
-            VMEM((4, 10, 96, HID), BF16),
+            VMEM((4, 8, 112, HID), BF16),
+            VMEM((4, 8, 96, HID), BF16),
             VMEM((4, 8, 80, HID), BF16),
             VMEM((4, 6, 64, HID), BF16),
-            *[VMEM((8, 6, SLOTS, HID), BF16)] * 2,
+            *[VMEM((6, 6, SLOTS, HID), BF16)] * 2,
             *[VMEM((ROWS, 4, SLOTS, HID), BF16)] * 2,
-            *[VMEM((8, 6, SLOTS, 128), F32)] * 2,
+            *[VMEM((4, 6, SLOTS, 128), F32)] * 2,
             *[VMEM((ROWS, 4, SLOTS, 128), F32)] * 2,
         ],
         name="patch",
-        compiler_params=pltpu.CompilerParams(vmem_limit_bytes=32 << 20),
-    )(near, own, far, *prepared)
+        compiler_params=pltpu.CompilerParams(vmem_limit_bytes=LIMIT),
+    )(near, far, *prepared, *middle)
 
 
 def unpack_kernel(p_ref, o_ref):
@@ -393,7 +444,7 @@
         in_specs=[pl.BlockSpec(memory_space=VMEM)],
         out_specs=pl.BlockSpec(memory_space=VMEM),
         name="unpack",
-        compiler_params=pltpu.CompilerParams(vmem_limit_bytes=8 << 20),
+        compiler_params=pltpu.CompilerParams(vmem_limit_bytes=LIMIT),
     )(pieces)
 
 
@@ -407,7 +458,7 @@
     own, prepared = lax.optimization_barrier((own, prepared))
     near = lax.ppermute(own, "lat", near_pairs)
     far = lax.ppermute(own, "lat", far_pairs)
-    done = main(near, own, far, prepared)
+    done = main(near, far, prepared, inner(own, prepared))
     back = lax.all_to_all(done, "tm", 0, 0)
     return unpack(back).reshape(1, C, ROWS, 128)
 

time: 57.9 us -> 56.2 us (0.971)
  waiting for transfers between devices: 13.1 us -> 10.9 us
    ppermute x1, waiting for transfers between devices: 3.38 us -> 1.19 us  [on_device(): far = lax.ppermute(own, 'lat', far_pairs)]
    pallas_call x0 -> x1, Pallas kernels: none -> 1.01 us  [inner(): pl.pallas_call(inner_kernel, out_shape=[jax.ShapeDtypeStruct((4, ROWS, 11...]
  transfers between devices with their start and end apart: 3 -> 3, of which waited for: 3 -> 3; matrix products, arithmetic and copies ran while one was open for 0% -> 0% of each run, Pallas kernels for 4% -> 6%
where the time goes in v7:
time: 56.2 us; the launch traced here: 55.9 us
  starting transfers between devices  18.3 us (33%)
  Pallas kernels  12.7 us (23%)
  blocking collectives  11.8 us (21%)
  waiting for transfers between devices  10.9 us (19%)
  local copies, waits for them, and re-layouts  2.11 us (4%)
    all_to_all x1, blocking collectives, on_device(): back = lax.all_to_all(done, 'tm', 0, 0)  11.8 us
    all_to_all x1, starting transfers between devices, on_device(): own = lax.all_to_all(pieces, 'tm', 0, 0)  11 us
    all_to_all x1, waiting for transfers between devices, on_device(): own = lax.all_to_all(pieces, 'tm', 0, 0)  6.76 us
    pallas_call x1, Pallas kernels, main(): pl.pallas_call(main_kernel, out_shape=jax.ShapeDtypeStruct((SLOTS, BACK,...  6.46 us
    ppermute x1, starting transfers between devices, on_device(): far = lax.ppermute(own, 'lat', far_pairs)  5.36 us
    ppermute x1, waiting for transfers between devices, on_device(): near = lax.ppermute(own, 'lat', near_pairs)  2.99 us
    pallas_call x1, Pallas kernels, tables(): pl.pallas_call(tables_kernel, out_shape=[jax.ShapeDtypeStruct((7, SLOTS,...  2.49 us
    unnamed x4, local copies, waits for them, and re-layouts  2.11 us
  transfers between devices with their start and end apart: 3, of which 3 were waited for; matrix products, arithmetic and copies ran while one was open for 0% of the time, Pallas kernels for 6%

profile of v7, /device:TPU:7, one launch (start us, length us, event | category | flops | bytes accessed | tf_op | source)
XLA Modules:
  0.0 55.9 jit_solution(14663554714839944091)
XLA Ops:
  0.0 2.0 %pack.1 = bf16[16,48,128]{2,1,0:T(8,128)(2,1)} custom-call(s32[17]{0:T(128)} %levels_hbm.3, f32[336,128]{1,0:T(8,128)} %bitcast.4), custom_call_target="tpu_custom_call" | custom-call | tf_op jit(solution)/shard_map/pack/pallas_call | solution.py:85
  2.0 11.0 %all-to-all-start = ((bf16[16,48,128]{2,1,0:T(8,128)(2,1)}), bf16[16,48,128]{2,1,0:T(8,128)(2,1)S(1)}, u32[]{:S(2)}, u32[]{:S(2)}) async-start(bf16[16,48,128]{2,1,0:T(8,128)(2,1)} %pack.1), calls=%async_computation | async-start | bytes 393216 | tf_op jit(solution)/shard_map/all_to_all | solution.py:456
  13.0 2.5 %tables.1 = (f32[7,16,256]{2,1,0:T(8,128)S(1)}, bf16[1792,256]{1,0:T(8,128)(2,1)S(1)}, bf16[2,4,256,768]{3,2,1,0:T(8,128)(2,1)S(1)}) custom-call(s32[17]{0:T(128)} %levels_hbm.3, bf16[84,256]{1,0:T(8,128)(2,1)} %bitcast.5, f32[1,256]{1,0:T(1,128)} %bitcast.6, bf16[256,1024]{1,0:T(8,128)(2,1)} %cond_hbm.1, bf16[84,256]{1,0:T(8,128)(2,1)} %out_w_hbm.1, ...), custom_call_target="tpu_custom_call" | custom-call | tf_op jit(solution)/shard_map/tables/pallas_call | solution.py:162
  15.5 0.0 copy-start
  15.5 0.9 %copy-done = bf16[1792,256]{1,0:T(8,128)(2,1)} copy-done((bf16[1792,256]{1,0:T(8,128)(2,1)}, bf16[1792,256]{1,0:T(8,128)(2,1)S(1)}, u32[]{:S(2)}) %copy-start) | copy-done | bytes 917528
  16.4 6.8 %all-to-all-done.own_ref = bf16[16,48,128]{2,1,0:T(8,128)(2,1)S(1)} async-done(((bf16[16,48,128]{2,1,0:T(8,128)(2,1)}), bf16[16,48,128]{2,1,0:T(8,128)(2,1)S(1)}, u32[]{:S(2)}, u32[]{:S(2)}) %all-to-all-start) | async-done | bytes 196640 | tf_op jit(solution)/shard_map/all_to_all | solution.py:456
  23.2 5.4 %collective-permute-start.1 = (bf16[16,48,128]{2,1,0:T(8,128)(2,1)S(1)}, bf16[16,48,128]{2,1,0:T(8,128)(2,1)S(1)}, u32[]{:S(2)}, u32[]{:S(2)}) collective-permute-start(bf16[16,48,128]{2,1,0:T(8,128)(2,1)S(1)} %all-to-all-done.own_ref), channel_id=1, source_target_pairs={{1,2},{2,1},{3,4},{4,3},{5,6},{6,5},{7,8},{8,7},{9,10},{10,9},{11,... | collective-permute-start | bytes 589832 | tf_op jit(solution)/shard_map/ppermute | solution.py:460
  28.5 1.9 %collective-permute-start = (bf16[16,48,128]{2,1,0:T(8,128)(2,1)S(1)}, bf16[16,48,128]{2,1,0:T(8,128)(2,1)S(1)}, u32[]{:S(2)}, u32[]{:S(2)}) collective-permute-start(bf16[16,48,128]{2,1,0:T(8,128)(2,1)S(1)} %all-to-all-done.own_ref), channel_id=1, source_target_pairs={{0,1},{1,0},{2,3},{3,2},{4,5},{5,4},{6,7},{7,6},{8,9},{9,8},{10,11... | collective-permute-start | bytes 589832 | tf_op jit(solution)/shard_map/ppermute | solution.py:459
  30.5 0.0 copy-start.1
  30.5 1.2 %copy-done.1 = bf16[1792,256]{1,0:T(8,128)(2,1)S(1)} copy-done((bf16[1792,256]{1,0:T(8,128)(2,1)S(1)}, bf16[1792,256]{1,0:T(8,128)(2,1)}, u32[]{:S(2)}) %copy-start.1) | copy-done | bytes 917528
  31.7 1.0 %inner.1 = (bf16[4,4,112,256]{3,2,1,0:T(8,128)(2,1)S(1)}, bf16[4,2,96,256]{3,2,1,0:T(8,128)(2,1)S(1)}, bf16[2,2,6,16,256]{4,3,2,1,0:T(8,128)(2,1)S(1)}, f32[2,4,6,16,128]{4,3,2,1,0:T(8,128)S(1)}) custom-call(bf16[16,48,128]{2,1,0:T(8,128)(2,1)S(1)} %all-to-all-done.own_ref, f32[7,16,256]{2,1,0:T(8,128)S(1)} %get-tuple-element.20.film_ref, ...), custom_call_target="tpu_custom_call" | custom-call | tf_op jit(solution)/shard_map/inner/pallas_call | solution.py:280
  32.7 1.2 %collective-permute-done.1.far_ref = bf16[16,48,128]{2,1,0:T(8,128)(2,1)S(1)} collective-permute-done((bf16[16,48,128]{2,1,0:T(8,128)(2,1)S(1)}, bf16[16,48,128]{2,1,0:T(8,128)(2,1)S(1)}, u32[]{:S(2)}, u32[]{:S(2)}) %collective-permute-start.1) | collective-permute-done | bytes 196640 | tf_op jit(solution)/shard_map/ppermute | solution.py:460
  33.9 3.0 %collective-permute-done.near_ref = bf16[16,48,128]{2,1,0:T(8,128)(2,1)S(1)} collective-permute-done((bf16[16,48,128]{2,1,0:T(8,128)(2,1)S(1)}, bf16[16,48,128]{2,1,0:T(8,128)(2,1)S(1)}, u32[]{:S(2)}, u32[]{:S(2)}) %collective-permute-start) | collective-permute-done | bytes 196640 | tf_op jit(solution)/shard_map/ppermute | solution.py:459
  36.8 6.5 %patch.1 = bf16[16,24,128]{2,1,0:T(8,128)(2,1)S(1)} custom-call(bf16[16,48,128]{2,1,0:T(8,128)(2,1)S(1)} %collective-permute-done.near_ref, bf16[16,48,128]{2,1,0:T(8,128)(2,1)S(1)} %collective-permute-done.1.far_ref, f32[7,16,256]{2,1,0:T(8,128)S(1)} %get-tuple-element.20.film_ref, bf16[1792,256]{1,0:T(8,128)(2,1)S(1)} %copy-done.1, ...), custom_call_target="tpu_custom_call" | custom-call | tf_op jit(solution)/shard_map/patch/pallas_call | solution.py:407
  43.3 11.8 %all_to_all.10.p_ref = bf16[16,24,128]{2,1,0:T(8,128)(2,1)S(1)} all-to-all(bf16[16,24,128]{2,1,0:T(8,128)(2,1)S(1)} %patch.1), channel_id=1, replica_groups=mesh['tm'=16,'lat'=32] {'tm'}, dimensions={0} | all-to-all | bytes 196608 | tf_op jit(solution)/shard_map/all_to_all | solution.py:462
  55.1 0.8 %unpack.1 = f32[336,128]{1,0:T(8,128)} custom-call(bf16[16,24,128]{2,1,0:T(8,128)(2,1)S(1)} %all_to_all.10.p_ref), custom_call_target="tpu_custom_call" | custom-call | tf_op jit(solution)/shard_map/unpack/pallas_call | solution.py:441
Async XLA Ops:
  2.0 21.2 %all-to-all-start = ((bf16[16,48,128]{2,1,0:T(8,128)(2,1)}), bf16[16,48,128]{2,1,0:T(8,128)(2,1)S(1)}, u32[]{:S(2)}, u32[]{:S(2)}) async-start(bf16[16,48,128]{2,1,0:T(8,128)(2,1)} %pack.1), calls=%async_computation | async-start | bytes 393216 | tf_op jit(solution)/shard_map/all_to_all | solution.py:456
  15.5 0.9 %copy-start = (bf16[1792,256]{1,0:T(8,128)(2,1)}, bf16[1792,256]{1,0:T(8,128)(2,1)S(1)}, u32[]{:S(2)}) copy-start(bf16[1792,256]{1,0:T(8,128)(2,1)S(1)} %get-tuple-element.21.picks_ref) | copy-start | bytes 2752516
  23.2 10.7 %collective-permute-start.1 = (bf16[16,48,128]{2,1,0:T(8,128)(2,1)S(1)}, bf16[16,48,128]{2,1,0:T(8,128)(2,1)S(1)}, u32[]{:S(2)}, u32[]{:S(2)}) collective-permute-start(bf16[16,48,128]{2,1,0:T(8,128)(2,1)S(1)} %all-to-all-done.own_ref), channel_id=1, source_target_pairs={{1,2},{2,1},{3,4},{4,3},{5,6},{6,5},{7,8},{8,7},{9,10},{10,9},{11,... | collective-permute-start | bytes 589832 | tf_op jit(solution)/shard_map/ppermute | solution.py:460
  28.5 8.3 %collective-permute-start = (bf16[16,48,128]{2,1,0:T(8,128)(2,1)S(1)}, bf16[16,48,128]{2,1,0:T(8,128)(2,1)S(1)}, u32[]{:S(2)}, u32[]{:S(2)}) collective-permute-start(bf16[16,48,128]{2,1,0:T(8,128)(2,1)S(1)} %all-to-all-done.own_ref), channel_id=1, source_target_pairs={{0,1},{1,0},{2,3},{3,2},{4,5},{5,4},{6,7},{7,6},{8,9},{9,8},{10,11... | collective-permute-start | bytes 589832 | tf_op jit(solution)/shard_map/ppermute | solution.py:459
  30.5 1.2 %copy-start.1 = (bf16[1792,256]{1,0:T(8,128)(2,1)S(1)}, bf16[1792,256]{1,0:T(8,128)(2,1)}, u32[]{:S(2)}) copy-start(bf16[1792,256]{1,0:T(8,128)(2,1)} %copy-done) | copy-start | bytes 2752516

commit v8 on v7

--- a/solution.py
+++ b/solution.py
@@ -17,6 +17,10 @@
 BACK = 24
 SWAP, BEFORE, UPTO, IN_T, OUT_T = slice(0, 256), slice(256, 384), slice(384, 512), slice(512, 640), slice(640, 768)
 IN_PACK = 768
+CONV_ONE = (((0, 1, 2, 3), (0, 1, 2), (0, 1)), ((8, 9), (7, 8, 9), (6, 7, 8, 9)))
+CONV_TWO = (((0, 1, 2, 3), (0, 1, 2), (0, 1)), ((6, 7), (5, 6, 7), (4, 5, 6, 7)))
+OWN_ONE = ((4, 5, 6, 7), (3, 4, 5, 6), (2, 3, 4, 5))
+OWN_TWO = ((4, 5), (3, 4), (2, 3))
 LIMIT = 32 << 20
 
 SIGMA_TOP = 1.0
@@ -199,6 +203,26 @@
     return even.reshape(shape), odd.reshape(shape)
 
 
+def partial_responses(view, rows_of, filters):
+    sums = []
+    for kind in range(4):
+        total = {}
+        for a, rows in enumerate(rows_of):
+            lhs = jnp.concatenate([view(kind, i + a) for i in rows], axis=0)
+            weight = filters[kind, :, HID * a : HID * a + HID]
+            out = lax.dot_general(lhs, weight, NT, preferred_element_type=F32)
+            size = out.shape[0] // len(rows)
+            for at, i in enumerate(rows):
+                piece = out[size * at : size * at + size]
+                total[i] = total[i] + piece if i in total else piece
+        sums.append(total)
+    result = {}
+    for i in sums[0]:
+        parts = [total[i].reshape(-1, SLOTS, HID) for total in sums]
+        result[i] = parts[0] + (parts[1] + parts[2]), (parts[1] - parts[2]) - parts[3]
+    return result
+
+
 def transform(ref, row, even, odd):
     size = (even.shape[0] - 1) * SLOTS
     values = (even[:-1] - even[1:], odd[:-1] + even[1:], even[1:] - odd[:-1], odd[:-1] - odd[1:])
@@ -262,37 +286,44 @@
     return even * root, odd * root
 
 
-def inner_kernel(own_ref, film_ref, picks_ref, filter_ref, h0, h1, keep_ref, x_ref):
+def inner_kernel(own_ref, film_ref, picks_ref, filter_ref, h1, keep_ref, x_ref, part_one, part_two, h0):
     heads, tails = ordered([own_ref[...]], picks_ref)
     shift = film_ref[6][None]
     for row in range(ROWS):
         even, odd = project(heads, tails, row, picks_ref)[0]
         transform(h0, row, even + shift, odd + shift)
         x_ref[0, row], x_ref[1, row] = state_of(heads[0], tails[0], row, film_ref)
-    even, odd = convolve(lambda kind, i: h0[kind, i], (0, 1), filter_ref.at[0])
-    even, odd = film(even, film_ref[0], film_ref[1]), film(odd, film_ref[0], film_ref[1])
+    found = partial_responses(lambda kind, i: h0[kind, i - 4], OWN_ONE, filter_ref.at[0])
+    for at, i in enumerate((2, 3, 6, 7)):
+        part_one[0, at], part_one[1, at] = found[i]
     for at in range(2):
-        transform(h1, at, even[at], odd[at])
-        keep_ref[0, at], keep_ref[1, at] = odd[at, :-1].astype(BF16), even[at, 1:].astype(BF16)
+        even, odd = [film(value, film_ref[0][None], film_ref[1][None]) for value in found[4 + at]]
+        transform(h1, at, even, odd)
+        keep_ref[0, at], keep_ref[1, at] = odd[:-1].astype(BF16), even[1:].astype(BF16)
+    found = partial_responses(lambda kind, i: h1[kind, i - 4], OWN_TWO, filter_ref.at[1])
+    for at in range(4):
+        part_two[0, at], part_two[1, at] = found[2 + at]
 
 
 def inner(own, prepared):
     return pl.pallas_call(
         inner_kernel,
         out_shape=[
-            jax.ShapeDtypeStruct((4, ROWS, 112, HID), BF16),
             jax.ShapeDtypeStruct((4, 2, 96, HID), BF16),
             jax.ShapeDtypeStruct((2, 2, 6, SLOTS, HID), BF16),
             jax.ShapeDtypeStruct((2, ROWS, 6, SLOTS, 128), F32),
+            jax.ShapeDtypeStruct((2, 4, 7, SLOTS, HID), F32),
+            jax.ShapeDtypeStruct((2, 4, 6, SLOTS, HID), F32),
         ],
         in_specs=[pl.BlockSpec(memory_space=VMEM)] * 4,
-        out_specs=[pl.BlockSpec(memory_space=VMEM)] * 4,
+        out_specs=[pl.BlockSpec(memory_space=VMEM)] * 5,
+        scratch_shapes=[VMEM((4, ROWS, 112, HID), BF16)],
         name="inner",
         compiler_params=pltpu.CompilerParams(vmem_limit_bytes=LIMIT),
     )(own, *prepared)
 
 
-def main_kernel(near_ref, far_ref, film_ref, picks_ref, filter_ref, h0_own, h1_own, keep_own, x_own, o_ref, h0, h1, g0, g1, h1_even, h1_odd, g1_even, g1_odd, x_even, x_odd, s_even, s_odd):
+def main_kernel(near_ref, far_ref, film_ref, picks_ref, filter_ref, h1_own, keep_own, x_own, part_one, part_two, o_ref, h0, h1, g0, g1, h1_even, h1_odd, g1_even, g1_odd, x_even, x_odd, s_even, s_odd):
     place = lax.axis_index("lat")
     count = lax.axis_size("lat")
     inside_low = jnp.where(place > 0, 1.0, 0.0).astype(F32)
@@ -319,17 +350,24 @@
         x_even[i], x_odd[i] = state_of(heads[at], tails[at], row, film_ref)
 
     def view_zero(kind, i):
-        return h0_own[kind, i - 4] if 4 <= i < 8 else h0[kind, i if i < 4 else i - 4]
+        return h0[kind, i if i < 4 else i - 4]
 
     def view_one(kind, i):
-        return h1_own[kind, i - 4] if 4 <= i < 6 else h1[kind, i if i < 4 else i - 2]
-
-    for rows in (range(0, 4), range(6, 10)):
-        even, odd = convolve(view_zero, rows, filter_ref.at[0])
-        for at, i in enumerate(rows):
+        return h1[kind, i if i < 4 else i - 2]
+
+    def with_own(found, i, rows, part):
+        if i not in rows:
+            return found[i]
+        at = rows.index(i)
+        return found[i][0] + part[0, at], found[i][1] + part[1, at]
+
+    for rows_of in CONV_ONE:
+        found = partial_responses(view_zero, rows_of, filter_ref.at[0])
+        for i in sorted(found):
             to = i if i < 4 else i - 2
-            scale, shift = film_ref[0] * gate_of(i - 3), film_ref[1] * gate_of(i - 3)
-            here_even, here_odd = film(even[at], scale[None], shift[None]), film(odd[at], scale[None], shift[None])
+            even, odd = with_own(found, i, (2, 3, 6, 7), part_one)
+            scale, shift = (film_ref[0] * gate_of(i - 3))[None], (film_ref[1] * gate_of(i - 3))[None]
+            here_even, here_odd = film(even, scale, shift), film(odd, scale, shift)
             transform(h1, to, here_even, here_odd)
             if 1 <= i < 9:
                 h1_even[to - 1] = here_odd[:-1].astype(BF16)
@@ -341,28 +379,35 @@
 
     film_two = film_ref[2][None, None], film_ref[3][None, None]
 
-    for top in range(0, 8, 4):
-        even, odd = convolve(view_one, range(top, top + 4), filter_ref.at[1])
-        lower = top == 0
-
-        def around(own, other):
-            return jnp.concatenate([other, own] if lower else [own, other], axis=0).astype(F32)
-
-        side = slice(0, 3) if lower else slice(3, 6)
-        mine = slice(0, 1) if lower else slice(1, 2)
-        even = around(keep_own[0, mine], h1_even[side]) + film(even, *film_two)
-        odd = around(keep_own[1, mine], h1_odd[side]) + film(odd, *film_two)
-        side, mine = (slice(0, 2), slice(0, 2)) if lower else (slice(2, 4), slice(2, 4))
-        x = jnp.concatenate([around(x_own[0, mine], x_even[side]), around(x_own[1, mine], x_odd[side])], axis=0)
+    def stacked(pick, rows):
+        return jnp.concatenate([pick(r)[None] for r in rows], axis=0)
+
+    def kept(parity, r):
+        if 3 <= r < 5:
+            return keep_own[parity, r - 3].astype(F32)
+        return (h1_even, h1_odd)[parity][r if r < 3 else r - 2].astype(F32)
+
+    def x_of(parity, r):
+        return x_own[parity, r - 2] if 2 <= r < 6 else (x_even, x_odd)[parity][r if r < 2 else r - 4]
+
+    for rows_of in CONV_TWO:
+        found = partial_responses(view_one, rows_of, filter_ref.at[1])
+        rows = sorted(found)
+        n = len(rows)
+        sums = [with_own(found, r, (2, 3, 4, 5), part_two) for r in rows]
+        even, odd = [jnp.concatenate([pair[parity][None] for pair in sums], axis=0) for parity in range(2)]
+        even = stacked(lambda r: kept(0, r), rows) + film(even, *film_two)
+        odd = stacked(lambda r: kept(1, r), rows) + film(odd, *film_two)
+        x = jnp.concatenate([stacked(lambda r: x_of(0, r), rows), stacked(lambda r: x_of(1, r), rows)], axis=0)
         anchor = jnp.where(first, x, 0.0)
-        drift = keep * x - gain * network(even, odd).reshape(8, 6, SLOTS, 128) + anchor
-        state = jnp.concatenate(scan(picks_ref[BEFORE], drift.reshape(768, 128)), axis=0)
-        state = state.reshape(8, 6, SLOTS, 128) + anchor
+        drift = keep * x - gain * network(even, odd).reshape(2 * n, 6, SLOTS, 128) + anchor
+        drift = drift.reshape(n * 192, 128)
+        state = jnp.concatenate(scan(picks_ref[BEFORE], drift), axis=0)
+        state = state.reshape(2 * n, 6, SLOTS, 128) + anchor
         scaled = []
         for parity in range(2):
-            for at in range(4):
-                i = top + at
-                here = state[4 * parity + at]
+            for at, i in enumerate(rows):
+                here = state[n * parity + at]
                 if 2 <= i < 6:
                     if parity == 0:
                         s_even[i - 2] = here[1:5]
@@ -370,10 +415,10 @@
                         s_odd[i - 2] = here[1:5]
                 scaled.append((here * (inverse * gate_of(i - 2))[None]).reshape(96, 128).astype(BF16))
         hidden = jnp.dot(jnp.concatenate(scaled, axis=0), picks_ref[IN_T], preferred_element_type=F32)
-        hidden = hidden.reshape(8, 6, SLOTS, HID)
-        for at in range(4):
-            shift = (bias * gate_of(top + at - 2))[None]
-            transform(g0, top + at, hidden[at] + shift, hidden[4 + at] + shift)
+        hidden = hidden.reshape(2 * n, 6, SLOTS, HID)
+        for at, i in enumerate(rows):
+            shift = (bias * gate_of(i - 2))[None]
+            transform(g0, i, hidden[at] + shift, hidden[n + at] + shift)
 
     for top in range(0, 6, 3):
         even, odd = convolve(lambda kind, i: g0[kind, i], range(top, top + 3), filter_ref.at[0])
@@ -407,7 +452,7 @@
     return pl.pallas_call(
         main_kernel,
         out_shape=jax.ShapeDtypeStruct((SLOTS, BACK, 128), BF16),
-        in_specs=[pl.BlockSpec(memory_space=VMEM)] * 9,
+        in_specs=[pl.BlockSpec(memory_space=VMEM)] * 10,
         out_specs=pl.BlockSpec(memory_space=VMEM),
         scratch_shapes=[
             VMEM((4, 8, 112, HID), BF16),

time: 56.2 us -> 55.7 us (level)
  waiting for transfers between devices: 10.9 us -> 10.1 us
    ppermute x1, waiting for transfers between devices: 1.19 us -> 0.38 us  [on_device(): far = lax.ppermute(own, 'lat', far_pairs)]
    pallas_call x1, Pallas kernels: 1.01 us -> 1.82 us  [inner(): pl.pallas_call(inner_kernel, out_shape=[jax.ShapeDtypeStruct((4, 2, 96, H...]
  transfers between devices with their start and end apart: 3 -> 3, of which waited for: 3 -> 3; matrix products, arithmetic and copies ran while one was open for 0% -> 0% of each run, Pallas kernels for 6% -> 8%
where the time goes in v8:
time: 55.7 us; the launch traced here: 55.4 us
  starting transfers between devices  18.3 us (33%)
  Pallas kernels  13 us (23%)
  blocking collectives  11.8 us (21%)
  waiting for transfers between devices  10.1 us (18%)
  local copies, waits for them, and re-layouts  2.11 us (4%)
    all_to_all x1, blocking collectives, on_device(): back = lax.all_to_all(done, 'tm', 0, 0)  11.8 us
    all_to_all x1, starting transfers between devices, on_device(): own = lax.all_to_all(pieces, 'tm', 0, 0)  11 us
    all_to_all x1, waiting for transfers between devices, on_device(): own = lax.all_to_all(pieces, 'tm', 0, 0)  6.76 us
    pallas_call x1, Pallas kernels, main(): pl.pallas_call(main_kernel, out_shape=jax.ShapeDtypeStruct((SLOTS, BACK,...  5.98 us
    ppermute x1, starting transfers between devices, on_device(): far = lax.ppermute(own, 'lat', far_pairs)  5.36 us
    ppermute x1, waiting for transfers between devices, on_device(): near = lax.ppermute(own, 'lat', near_pairs)  2.99 us
    pallas_call x1, Pallas kernels, tables(): pl.pallas_call(tables_kernel, out_shape=[jax.ShapeDtypeStruct((7, SLOTS,...  2.49 us
    unnamed x4, local copies, waits for them, and re-layouts  2.11 us
  transfers between devices with their start and end apart: 3, of which 3 were waited for; matrix products, arithmetic and copies ran while one was open for 0% of the time, Pallas kernels for 8%

profile of v8, /device:TPU:7, one launch (start us, length us, event | category | flops | bytes accessed | tf_op | source)
XLA Modules:
  0.0 55.4 jit_solution(10961244191335064075)
XLA Ops:
  0.0 2.0 %pack.1 = bf16[16,48,128]{2,1,0:T(8,128)(2,1)} custom-call(s32[17]{0:T(128)} %levels_hbm.3, f32[336,128]{1,0:T(8,128)} %bitcast.4), custom_call_target="tpu_custom_call" | custom-call | tf_op jit(solution)/shard_map/pack/pallas_call | solution.py:89
  2.0 11.0 %all-to-all-start = ((bf16[16,48,128]{2,1,0:T(8,128)(2,1)}), bf16[16,48,128]{2,1,0:T(8,128)(2,1)S(1)}, u32[]{:S(2)}, u32[]{:S(2)}) async-start(bf16[16,48,128]{2,1,0:T(8,128)(2,1)} %pack.1), calls=%async_computation | async-start | bytes 393216 | tf_op jit(solution)/shard_map/all_to_all | solution.py:501
  13.0 2.5 %tables.1 = (f32[7,16,256]{2,1,0:T(8,128)S(1)}, bf16[1792,256]{1,0:T(8,128)(2,1)S(1)}, bf16[2,4,256,768]{3,2,1,0:T(8,128)(2,1)S(1)}) custom-call(s32[17]{0:T(128)} %levels_hbm.3, bf16[84,256]{1,0:T(8,128)(2,1)} %bitcast.5, f32[1,256]{1,0:T(1,128)} %bitcast.6, bf16[256,1024]{1,0:T(8,128)(2,1)} %cond_hbm.1, bf16[84,256]{1,0:T(8,128)(2,1)} %out_w_hbm.1, ...), custom_call_target="tpu_custom_call" | custom-call | tf_op jit(solution)/shard_map/tables/pallas_call | solution.py:166
  15.5 0.0 copy-start
  15.5 0.9 %copy-done = bf16[1792,256]{1,0:T(8,128)(2,1)} copy-done((bf16[1792,256]{1,0:T(8,128)(2,1)}, bf16[1792,256]{1,0:T(8,128)(2,1)S(1)}, u32[]{:S(2)}) %copy-start) | copy-done | bytes 917528
  16.4 6.8 %all-to-all-done.own_ref = bf16[16,48,128]{2,1,0:T(8,128)(2,1)S(1)} async-done(((bf16[16,48,128]{2,1,0:T(8,128)(2,1)}), bf16[16,48,128]{2,1,0:T(8,128)(2,1)S(1)}, u32[]{:S(2)}, u32[]{:S(2)}) %all-to-all-start) | async-done | bytes 196640 | tf_op jit(solution)/shard_map/all_to_all | solution.py:501
  23.2 5.4 %collective-permute-start.1 = (bf16[16,48,128]{2,1,0:T(8,128)(2,1)S(1)}, bf16[16,48,128]{2,1,0:T(8,128)(2,1)S(1)}, u32[]{:S(2)}, u32[]{:S(2)}) collective-permute-start(bf16[16,48,128]{2,1,0:T(8,128)(2,1)S(1)} %all-to-all-done.own_ref), channel_id=1, source_target_pairs={{1,2},{2,1},{3,4},{4,3},{5,6},{6,5},{7,8},{8,7},{9,10},{10,9},{11,... | collective-permute-start | bytes 589832 | tf_op jit(solution)/shard_map/ppermute | solution.py:505
  28.5 1.9 %collective-permute-start = (bf16[16,48,128]{2,1,0:T(8,128)(2,1)S(1)}, bf16[16,48,128]{2,1,0:T(8,128)(2,1)S(1)}, u32[]{:S(2)}, u32[]{:S(2)}) collective-permute-start(bf16[16,48,128]{2,1,0:T(8,128)(2,1)S(1)} %all-to-all-done.own_ref), channel_id=1, source_target_pairs={{0,1},{1,0},{2,3},{3,2},{4,5},{5,4},{6,7},{7,6},{8,9},{9,8},{10,11... | collective-permute-start | bytes 589832 | tf_op jit(solution)/shard_map/ppermute | solution.py:504
  30.5 0.0 copy-start.1
  30.5 1.2 %copy-done.1 = bf16[1792,256]{1,0:T(8,128)(2,1)S(1)} copy-done((bf16[1792,256]{1,0:T(8,128)(2,1)S(1)}, bf16[1792,256]{1,0:T(8,128)(2,1)}, u32[]{:S(2)}) %copy-start.1) | copy-done | bytes 917528
  31.7 1.8 %inner.1 = (bf16[4,2,96,256]{3,2,1,0:T(8,128)(2,1)S(1)}, bf16[2,2,6,16,256]{4,3,2,1,0:T(8,128)(2,1)S(1)}, f32[2,4,6,16,128]{4,3,2,1,0:T(8,128)S(1)}, f32[2,4,7,1...) custom-call(bf16[16,48,128]{2,1,0:T(8,128)(2,1)S(1)} %all-to-all-done.own_ref, ...), custom_call_target="tpu_custom_call" | custom-call | tf_op jit(solution)/shard_map/inner/pallas_call | solution.py:309
  33.5 0.4 collective-permute-done.1.far_ref
  33.9 3.0 %collective-permute-done.near_ref = bf16[16,48,128]{2,1,0:T(8,128)(2,1)S(1)} collective-permute-done((bf16[16,48,128]{2,1,0:T(8,128)(2,1)S(1)}, bf16[16,48,128]{2,1,0:T(8,128)(2,1)S(1)}, u32[]{:S(2)}, u32[]{:S(2)}) %collective-permute-start) | collective-permute-done | bytes 196640 | tf_op jit(solution)/shard_map/ppermute | solution.py:504
  36.8 6.0 %patch.1 = bf16[16,24,128]{2,1,0:T(8,128)(2,1)S(1)} custom-call(bf16[16,48,128]{2,1,0:T(8,128)(2,1)S(1)} %collective-permute-done.near_ref, bf16[16,48,128]{2,1,0:T(8,128)(2,1)S(1)} %collective-permute-done.1.far_ref, f32[7,16,256]{2,1,0:T(8,128)S(1)} %get-tuple-element.21.film_ref, bf16[1792,256]{1,0:T(8,128)(2,1)S(1)} %copy-done.1, ...), custom_call_target="tpu_custom_call" | custom-call | tf_op jit(solution)/shard_map/patch/pallas_call | solution.py:452
  42.8 11.8 %all_to_all.10.p_ref = bf16[16,24,128]{2,1,0:T(8,128)(2,1)S(1)} all-to-all(bf16[16,24,128]{2,1,0:T(8,128)(2,1)S(1)} %patch.1), channel_id=1, replica_groups=mesh['tm'=16,'lat'=32] {'tm'}, dimensions={0} | all-to-all | bytes 196608 | tf_op jit(solution)/shard_map/all_to_all | solution.py:507
  54.6 0.8 %unpack.1 = f32[336,128]{1,0:T(8,128)} custom-call(bf16[16,24,128]{2,1,0:T(8,128)(2,1)S(1)} %all_to_all.10.p_ref), custom_call_target="tpu_custom_call" | custom-call | tf_op jit(solution)/shard_map/unpack/pallas_call | solution.py:486
Async XLA Ops:
  2.0 21.2 %all-to-all-start = ((bf16[16,48,128]{2,1,0:T(8,128)(2,1)}), bf16[16,48,128]{2,1,0:T(8,128)(2,1)S(1)}, u32[]{:S(2)}, u32[]{:S(2)}) async-start(bf16[16,48,128]{2,1,0:T(8,128)(2,1)} %pack.1), calls=%async_computation | async-start | bytes 393216 | tf_op jit(solution)/shard_map/all_to_all | solution.py:501
  15.5 0.9 %copy-start = (bf16[1792,256]{1,0:T(8,128)(2,1)}, bf16[1792,256]{1,0:T(8,128)(2,1)S(1)}, u32[]{:S(2)}) copy-start(bf16[1792,256]{1,0:T(8,128)(2,1)S(1)} %get-tuple-element.22.picks_ref) | copy-start | bytes 2752516
  23.2 10.7 %collective-permute-start.1 = (bf16[16,48,128]{2,1,0:T(8,128)(2,1)S(1)}, bf16[16,48,128]{2,1,0:T(8,128)(2,1)S(1)}, u32[]{:S(2)}, u32[]{:S(2)}) collective-permute-start(bf16[16,48,128]{2,1,0:T(8,128)(2,1)S(1)} %all-to-all-done.own_ref), channel_id=1, source_target_pairs={{1,2},{2,1},{3,4},{4,3},{5,6},{6,5},{7,8},{8,7},{9,10},{10,9},{11,... | collective-permute-start | bytes 589832 | tf_op jit(solution)/shard_map/ppermute | solution.py:505
  28.5 8.3 %collective-permute-start = (bf16[16,48,128]{2,1,0:T(8,128)(2,1)S(1)}, bf16[16,48,128]{2,1,0:T(8,128)(2,1)S(1)}, u32[]{:S(2)}, u32[]{:S(2)}) collective-permute-start(bf16[16,48,128]{2,1,0:T(8,128)(2,1)S(1)} %all-to-all-done.own_ref), channel_id=1, source_target_pairs={{0,1},{1,0},{2,3},{3,2},{4,5},{5,4},{6,7},{7,6},{8,9},{9,8},{10,11... | collective-permute-start | bytes 589832 | tf_op jit(solution)/shard_map/ppermute | solution.py:504
  30.5 1.2 %copy-start.1 = (bf16[1792,256]{1,0:T(8,128)(2,1)S(1)}, bf16[1792,256]{1,0:T(8,128)(2,1)}, u32[]{:S(2)}) copy-start(bf16[1792,256]{1,0:T(8,128)(2,1)} %copy-done) | copy-start | bytes 2752516
